TPU v7x, 32 devices: a whole 2x2x4 slice. The times are simulated.
32 devices in a mesh: fsdp: 16 (over z, y, core), seq: 2 (over x).
Axes of the slice: x: 2, y: 2, z: 4, core: 2. Of those that a mesh axis runs over, the one named last changes fastest.
Arguments:
- tokens: bfloat16 [16, 1024, 1024], P('fsdp', 'seq'), may hold values from -6 to 6
- condition: bfloat16 [16, 1024], P('fsdp'), may hold values from -6 to 6
- w_ada: bfloat16 [1024, 6144], P('fsdp'), may hold values from -0.1875 to 0.1875
- b_ada: bfloat16 [6144], P('fsdp'), may hold values from -3 to 3
- w_qkv: bfloat16 [1024, 3072], P('fsdp'), may hold values from -0.1875 to 0.1875
- b_qv: bfloat16 [2048], P('fsdp'), may hold values from -1.1953125 to 1.1953125
- w_proj: bfloat16 [1024, 1024], P('fsdp'), may hold values from -0.1875 to 0.1875
- b_proj: bfloat16 [1024], P('fsdp'), may hold values from -1.1953125 to 1.1953125
- w_fc1: bfloat16 [1024, 4096], P('fsdp'), may hold values from -0.1875 to 0.1875
- b_fc1: bfloat16 [4096], P('fsdp'), may hold values from -1.1953125 to 1.1953125
- w_fc2: bfloat16 [4096, 1024], P('fsdp'), may hold values from -0.09375 to 0.09375
- b_fc2: bfloat16 [1024], P('fsdp'), may hold values from -1.1953125 to 1.1953125
- cotangent: bfloat16 [16, 1024, 1024], P('fsdp', 'seq'), may hold values from -6 to 6
Outputs:
- out_tokens: bfloat16 [16, 1024, 1024], P('fsdp', 'seq')
- grad_tokens: float32 [16, 1024, 1024], P('fsdp', 'seq')
- grad_condition: float32 [16, 1024], P('fsdp')
- grad_w_ada: float32 [1024, 6144], P('fsdp')
- grad_b_ada: float32 [6144], P('fsdp')
- grad_w_qkv: float32 [1024, 3072], P('fsdp')
- grad_b_qv: float32 [2048], P('fsdp')
- grad_w_proj: float32 [1024, 1024], P('fsdp')
- grad_b_proj: float32 [1024], P('fsdp')
- grad_w_fc1: float32 [1024, 4096], P('fsdp')
- grad_b_fc1: float32 [4096], P('fsdp')
- grad_w_fc2: float32 [4096, 1024], P('fsdp')
- grad_b_fc2: float32 [1024], P('fsdp')
All inputs are finite; a program needn't handle non-finite values.
Results may differ from a plain program's by a relative error of at most 0.018.
The roundings to bfloat16 on the way count: a program that leaves them out, or rounds other values in their place, can miss the bound.
Values may be sent and summed in bfloat16 or wider, within the bound.
A program may use at most 256 MiB of HBM per device.

v0:
```python
from functools import partial

import jax
import jax.numpy as jnp
from jax import lax
from jax.sharding import PartitionSpec as P

HD = 64


norm_eps = 1e-06
block_rows = 512


def layer_norm(values):
    center = values - jnp.mean(values, axis=-1, keepdims=True)
    rscale = lax.rsqrt(jnp.mean(center * center, axis=-1, keepdims=True) + norm_eps)
    return (center * rscale, rscale)


def norm_back(upstream, normed, rscale):
    mean_up = jnp.mean(upstream, axis=-1, keepdims=True)
    mean_cross = jnp.mean(upstream * normed, axis=-1, keepdims=True)
    return rscale * (upstream - mean_up - normed * mean_cross)


def attend_forward(queries, keys_all, values_all):
    seq_len = keys_all.shape[1]
    rows = min(block_rows, seq_len)
    score_scale = queries.shape[-1] ** (-0.5)
    outputs = []
    totals = []
    for offset in range(0, seq_len, rows):
        q_block = queries[:, offset : offset + rows]
        raw_scores = jnp.einsum(
            "bqhd,bkhd->bhqk", q_block, keys_all, preferred_element_type=jnp.float32
        )
        scores = raw_scores * score_scale
        row_max = jnp.max(scores, axis=-1, keepdims=True)
        shifted = jnp.exp(scores - row_max)
        row_total = jnp.sum(shifted, axis=-1, keepdims=True)
        attn_prob = (shifted / row_total).astype(jnp.bfloat16)
        block_out = jnp.einsum(
            "bhqk,bkhd->bqhd", attn_prob, values_all, preferred_element_type=jnp.float32
        )
        outputs.append(block_out.astype(jnp.bfloat16))
        totals.append(row_max + jnp.log(row_total))
    return (jnp.concatenate(outputs, axis=1), jnp.concatenate(totals, axis=2))


def attend_backward(queries, keys_all, values_all, log_total, d_out):
    seq_len = keys_all.shape[1]
    rows = min(block_rows, seq_len)
    score_scale = queries.shape[-1] ** (-0.5)
    grad_keys = jnp.zeros(keys_all.shape, jnp.float32)
    grad_values = jnp.zeros(values_all.shape, jnp.float32)
    grad_queries = []
    for offset in range(0, seq_len, rows):
        q_block = queries[:, offset : offset + rows]
        d_block = d_out[:, offset : offset + rows]
        raw_scores = jnp.einsum(
            "bqhd,bkhd->bhqk", q_block, keys_all, preferred_element_type=jnp.float32
        )
        attn_prob = jnp.exp(raw_scores * score_scale - log_total[:, :, offset : offset + rows])
        grad_values = grad_values + jnp.einsum(
            "bhqk,bqhd->bkhd",
            attn_prob.astype(jnp.bfloat16),
            d_block,
            preferred_element_type=jnp.float32,
        )
        d_prob = jnp.einsum(
            "bqhd,bkhd->bhqk", d_block, values_all, preferred_element_type=jnp.float32
        )
        center = jnp.sum(attn_prob * d_prob, axis=-1, keepdims=True)
        d_raw = (attn_prob * (d_prob - center) * score_scale).astype(jnp.bfloat16)
        grad_queries.append(
            jnp.einsum("bhqk,bkhd->bqhd", d_raw, keys_all, preferred_element_type=jnp.float32)
        )
        grad_keys = grad_keys + jnp.einsum(
            "bhqk,bqhd->bkhd", d_raw, q_block, preferred_element_type=jnp.float32
        )
    grad_q = jnp.concatenate(grad_queries, axis=1).astype(jnp.bfloat16)
    return (grad_q, grad_keys.astype(jnp.bfloat16), grad_values.astype(jnp.bfloat16))


def on_device(
    tokens,
    condition,
    w_ada,
    b_ada,
    w_qkv,
    b_qv,
    w_proj,
    b_proj,
    w_fc1,
    b_fc1,
    w_fc2,
    b_fc2,
    cotangent,
):
    latents, local_len, model_width = tokens.shape
    groups = lax.axis_size("seq")
    head_dim = HD
    group_width = model_width // groups
    per_group = group_width // head_dim
    ada_w, ada_b, qkv_w, qv_b, proj_w, proj_b, fc1_w, fc1_b, fc2_w, fc2_b = (
        lax.all_gather(w_ada, "fsdp", axis=0, tiled=True),
        lax.all_gather(b_ada, "fsdp", axis=0, tiled=True),
        lax.all_gather(w_qkv, "fsdp", axis=0, tiled=True),
        lax.all_gather(b_qv, "fsdp", axis=0, tiled=True),
        lax.all_gather(w_proj, "fsdp", axis=0, tiled=True),
        lax.all_gather(b_proj, "fsdp", axis=0, tiled=True),
        lax.all_gather(w_fc1, "fsdp", axis=0, tiled=True),
        lax.all_gather(b_fc1, "fsdp", axis=0, tiled=True),
        lax.all_gather(w_fc2, "fsdp", axis=0, tiled=True),
        lax.all_gather(b_fc2, "fsdp", axis=0, tiled=True),
    )
    tokens_f = tokens.astype(jnp.float32)
    lifted, silu_back = jax.vjp(jax.nn.silu, condition.astype(jnp.float32))
    lifted_b = lifted.astype(jnp.bfloat16)
    modulation = jnp.dot(lifted_b, ada_w, preferred_element_type=jnp.float32) + ada_b.astype(
        jnp.float32
    )
    shift_one, scale_one, gate_one, shift_two, scale_two, gate_two = jnp.split(
        modulation[:, None, :], 6, axis=-1
    )
    normed_one, rscale_one = layer_norm(tokens_f)
    hidden_one = (normed_one * (1.0 + scale_one) + shift_one).astype(jnp.bfloat16)
    qkv_bias = jnp.concatenate(
        [qv_b[:model_width], jnp.zeros((model_width,), jnp.bfloat16), qv_b[model_width:]]
    ).astype(jnp.float32)
    qkv_tok = (jnp.dot(hidden_one, qkv_w, preferred_element_type=jnp.float32) + qkv_bias).astype(
        jnp.bfloat16
    )
    spread = lax.all_to_all(
        qkv_tok.reshape(latents, local_len, 3, groups, group_width),
        "seq",
        split_axis=3,
        concat_axis=1,
        tiled=True,
    )
    seq_len = spread.shape[1]
    queries = spread[:, :, 0, 0].reshape(latents, seq_len, per_group, head_dim)
    keys_all = spread[:, :, 1, 0].reshape(latents, seq_len, per_group, head_dim)
    values_all = spread[:, :, 2, 0].reshape(latents, seq_len, per_group, head_dim)
    attn_out, log_total = attend_forward(queries, keys_all, values_all)
    returned = lax.all_to_all(
        attn_out.reshape(latents, seq_len, 1, group_width),
        "seq",
        split_axis=1,
        concat_axis=2,
        tiled=True,
    )
    attn_tok = returned.reshape(latents, local_len, model_width)
    branch = jnp.dot(attn_tok, proj_w, preferred_element_type=jnp.float32) + proj_b.astype(
        jnp.float32
    )
    middle = tokens_f + gate_one * branch
    normed_two, rscale_two = layer_norm(middle)
    hidden_two = (normed_two * (1.0 + scale_two) + shift_two).astype(jnp.bfloat16)
    pre_act = jnp.dot(hidden_two, fc1_w, preferred_element_type=jnp.float32) + fc1_b.astype(
        jnp.float32
    )
    act_f, gelu_back = jax.vjp(partial(jax.nn.gelu, approximate=True), pre_act)
    act_b = act_f.astype(jnp.bfloat16)
    mlp_out = jnp.dot(act_b, fc2_w, preferred_element_type=jnp.float32) + fc2_b.astype(jnp.float32)
    result = (middle + gate_two * mlp_out).astype(jnp.bfloat16)
    grad_out = cotangent.astype(jnp.float32)
    d_gate_two = jnp.sum(grad_out * mlp_out, axis=1)
    d_mlp = (grad_out * gate_two).astype(jnp.bfloat16)
    grad_fc2 = jnp.einsum("btf,btd->fd", act_b, d_mlp, preferred_element_type=jnp.float32)
    bias_fc2 = jnp.sum(d_mlp, axis=(0, 1), dtype=jnp.float32)
    d_act = jnp.einsum("btd,fd->btf", d_mlp, fc2_w, preferred_element_type=jnp.float32)
    d_pre = gelu_back(d_act)[0].astype(jnp.bfloat16)
    grad_fc1 = jnp.einsum("btd,btf->df", hidden_two, d_pre, preferred_element_type=jnp.float32)
    bias_fc1 = jnp.sum(d_pre, axis=(0, 1), dtype=jnp.float32)
    d_hidden_two = jnp.einsum("btf,df->btd", d_pre, fc1_w, preferred_element_type=jnp.float32)
    d_shift_two = jnp.sum(d_hidden_two, axis=1)
    d_scale_two = jnp.sum(d_hidden_two * normed_two, axis=1)
    d_middle = grad_out + norm_back(d_hidden_two * (1.0 + scale_two), normed_two, rscale_two)
    d_gate_one = jnp.sum(d_middle * branch, axis=1)
    d_branch = (d_middle * gate_one).astype(jnp.bfloat16)
    grad_proj = jnp.einsum("btk,btd->kd", attn_tok, d_branch, preferred_element_type=jnp.float32)
    bias_proj = jnp.sum(d_branch, axis=(0, 1), dtype=jnp.float32)
    d_attn = jnp.einsum("btd,kd->btk", d_branch, proj_w, preferred_element_type=jnp.float32).astype(
        jnp.bfloat16
    )
    d_heads = lax.all_to_all(
        d_attn.reshape(latents, local_len, groups, group_width),
        "seq",
        split_axis=2,
        concat_axis=1,
        tiled=True,
    )
    d_heads = d_heads.reshape(latents, seq_len, per_group, head_dim)
    grad_q, grad_k, grad_v = attend_backward(queries, keys_all, values_all, log_total, d_heads)
    d_spread = jnp.stack([grad_q, grad_k, grad_v], axis=2).reshape(
        latents, seq_len, 3, 1, group_width
    )
    d_qkv = lax.all_to_all(d_spread, "seq", split_axis=1, concat_axis=3, tiled=True).reshape(
        latents, local_len, 3 * model_width
    )
    grad_qkv = jnp.einsum("btd,bte->de", hidden_one, d_qkv, preferred_element_type=jnp.float32)
    column_sums = jnp.sum(d_qkv, axis=(0, 1), dtype=jnp.float32)
    bias_qv = jnp.concatenate([column_sums[:model_width], column_sums[2 * model_width :]])
    d_hidden_one = jnp.einsum("bte,de->btd", d_qkv, qkv_w, preferred_element_type=jnp.float32)
    d_shift_one = jnp.sum(d_hidden_one, axis=1)
    d_scale_one = jnp.sum(d_hidden_one * normed_one, axis=1)
    grad_input = d_middle + norm_back(d_hidden_one * (1.0 + scale_one), normed_one, rscale_one)
    d_partial = jnp.concatenate(
        [d_shift_one, d_scale_one, d_gate_one, d_shift_two, d_scale_two, d_gate_two], axis=-1
    )
    d_modulation = lax.psum(d_partial, "seq").astype(jnp.bfloat16)
    d_lifted = jnp.einsum("be,ce->bc", d_modulation, ada_w, preferred_element_type=jnp.float32)
    grad_condition = silu_back(d_lifted)[0]
    grad_ada = jnp.einsum("bc,be->ce", lifted_b, d_modulation, preferred_element_type=jnp.float32)
    bias_ada = jnp.sum(d_modulation, axis=0, dtype=jnp.float32)
    total_ada, total_bada = (
        lax.psum_scatter(
            grad_ada.astype(jnp.bfloat16), "fsdp", scatter_dimension=0, tiled=True
        ).astype(jnp.float32),
        lax.psum_scatter(
            bias_ada.astype(jnp.bfloat16), "fsdp", scatter_dimension=0, tiled=True
        ).astype(jnp.float32),
    )
    shard_qkv, shard_bqv, shard_proj, shard_bproj, shard_fc1, shard_bfc1, shard_fc2, shard_bfc2 = (
        lax.psum_scatter(grad_qkv, "fsdp", scatter_dimension=0, tiled=True),
        lax.psum_scatter(bias_qv, "fsdp", scatter_dimension=0, tiled=True),
        lax.psum_scatter(grad_proj, "fsdp", scatter_dimension=0, tiled=True),
        lax.psum_scatter(bias_proj, "fsdp", scatter_dimension=0, tiled=True),
        lax.psum_scatter(grad_fc1, "fsdp", scatter_dimension=0, tiled=True),
        lax.psum_scatter(bias_fc1, "fsdp", scatter_dimension=0, tiled=True),
        lax.psum_scatter(grad_fc2, "fsdp", scatter_dimension=0, tiled=True),
        lax.psum_scatter(bias_fc2, "fsdp", scatter_dimension=0, tiled=True),
    )
    total_qkv, total_bqv, total_proj, total_bproj, total_fc1, total_bfc1, total_fc2, total_bfc2 = (
        lax.psum(
            (
                shard_qkv,
                shard_bqv,
                shard_proj,
                shard_bproj,
                shard_fc1,
                shard_bfc1,
                shard_fc2,
                shard_bfc2,
            ),
            "seq",
        )
    )
    return (
        result,
        grad_input,
        grad_condition,
        total_ada,
        total_bada,
        total_qkv,
        total_bqv,
        total_proj,
        total_bproj,
        total_fc1,
        total_bfc1,
        total_fc2,
        total_bfc2,
    )


def solution(mesh):
    return jax.shard_map(
        on_device,
        mesh=mesh,
        in_specs=(
            P("fsdp", "seq", None),
            P("fsdp", None),
            P("fsdp", None),
            P("fsdp"),
            P("fsdp", None),
            P("fsdp"),
            P("fsdp", None),
            P("fsdp"),
            P("fsdp", None),
            P("fsdp"),
            P("fsdp", None),
            P("fsdp"),
            P("fsdp", "seq", None),
        ),
        out_specs=(
            P("fsdp", "seq", None),
            P("fsdp", "seq", None),
            P("fsdp", None),
            P("fsdp", None),
            P("fsdp"),
            P("fsdp", None),
            P("fsdp"),
            P("fsdp", None),
            P("fsdp"),
            P("fsdp", None),
            P("fsdp"),
            P("fsdp", None),
            P("fsdp"),
        ),
        check_vma=False,
    )
```

profile of v0, /device:TPU:0, one launch (start us, length us, event | category | flops | bytes accessed | tf_op | source)
XLA Modules:
  0.0 1429.1 jit_solution(12914743900525769951)
XLA Ops:
  12.0 23.8 %all-gather.1 = bf16[16,1,128]{2,1,0:T(2,128)(2,1)S(1)} all-gather(bf16[1,1,128]{2,1,0:T(2,128)(2,1)} %bitcast.251), channel_id=1, replica_groups=mesh['fsdp'=16,'seq'=2] {'fsdp'}, dimensions={0}, use_global_device_ids=true | all-gather | bytes 4352 | tf_op jit(solution)/shard_map/all_gather | solution.py:110
  36.5 18.1 %all-gather = bf16[16,1,384]{2,1,0:T(2,128)(2,1)S(1)} all-gather(bf16[1,1,384]{2,1,0:T(2,128)(2,1)S(1)} %reshape.506), channel_id=1, replica_groups=mesh['fsdp'=16,'seq'=2] {'fsdp'}, dimensions={0}, use_global_device_ids=true | all-gather | bytes 13056 | tf_op jit(solution)/shard_map/all_gather | solution.py:108
  56.7 56.9 %all-gather.9.cloned.1.call-done = bf16[1024,6144]{1,0:T(8,128)(2,1)} async-done(((bf16[64,6144]{1,0:T(8,128)(2,1)}), bf16[1024,6144]{1,0:T(8,128)(2,1)}) %all-gather.9.cloned.1.call-update) | async-done | bytes 12582928 | tf_op jit(solution)/shard_map/all_gather | solution.py:107
  120.0 55.6 %all-gather.11.cloned.1.call-done = bf16[1024,3072]{1,0:T(8,128)(2,1)} async-done(((bf16[64,3072]{1,0:T(8,128)(2,1)}), bf16[1024,3072]{1,0:T(8,128)(2,1)}) %all-gather.11.cloned.1.call-update) | async-done | bytes 6291472 | tf_op jit(solution)/shard_map/all_gather | solution.py:109
  191.0 39.7 %all_to_all.63 = bf16[1,512,3,2,512]{4,1,2,0,3:T(8,128)(2,1)S(1)} all-to-all(bf16[1,512,3,2,512]{4,1,2,0,3:T(8,128)(2,1)S(1)} %copy.46), channel_id=1, replica_groups=mesh['fsdp'=16,'seq'=2] {'seq'}, dimensions={3} | all-to-all | bytes 6291456 | tf_op jit(solution)/shard_map/all_to_all | solution.py:135
  293.8 30.7 %all-reduce.10 = (bf16[1024]{0:T(1024)(128)(2,1)S(1)}, bf16[1024]{0:T(1024)(128)(2,1)S(1)}) all-reduce(bf16[1024]{0:T(1024)(128)(2,1)S(1)} %dynamic-update-slice, bf16[1024]{0:T(1024)(128)(2,1)S(1)} %dynamic-update-slice.1), channel_id=1, replica_groups=mesh['fsdp'=16,'seq'=2] {'fsdp'}, use_global_device_ids=true, to_apply=%add | all-reduce | flops 2048 | bytes 8192
  324.5 17.6 %all-gather.2 = bf16[16,1,256]{2,1,0:T(2,128)(2,1)S(1)} all-gather(bf16[1,1,256]{2,1,0:T(2,128)(2,1)S(1)} %reshape.510), channel_id=1, replica_groups=mesh['fsdp'=16,'seq'=2] {'fsdp'}, dimensions={0}, use_global_device_ids=true | all-gather | bytes 8704 | tf_op jit(solution)/shard_map/all_gather | solution.py:114
  356.6 12.0 fusion.122
  368.6 13.9 convert_reduce_fusion
  393.1 10.4 convert_reduce_fusion.3
  463.1 37.1 %fusion.64 = bf16[8,64,512]{2,1,0:T(8,128)(2,1)} fusion(bf16[1024,8,64]{0,2,1:T(8,128)(2,1)S(1)} %bitcast.199, f32[8,512,1024]{2,1,0:T(8,128)} %fusion.90, f32[8,512]{1,0:T(8,128)S(1)} %log_add_fusion, f32[8,512,1024]{2,1,0:T(8,128)} %copy-done), kind=kOutput, calls=%fused_computation.90 | convolution fusion | flops 574886912 | bytes 35143680 | tf_op jit(solution)/shard_map/bhqk,bkhd->bqhd/dot_general | solution.py:77
  511.8 36.6 %fusion.67 = bf16[8,64,512]{2,1,0:T(8,128)(2,1)S(1)} fusion(bf16[1024,8,64]{0,2,1:T(8,128)(2,1)S(1)} %bitcast.200, f32[8,512,1024]{2,1,0:T(8,128)} %fusion.89, f32[8,512]{1,0:T(8,128)S(1)} %log_add_fusion.1, f32[8,512,1024]{2,1,0:T(8,128)} %get-tuple-element.67), kind=kOutput, calls=%fused_computation.91 | convolution fusion | flops 574886912 | bytes 35143680 | tf_op jit(solution)/shard_map/bhqk,bkhd->bqhd/dot_general | solution.py:77
  550.4 30.7 %fusion.11 = f32[8,64,1024]{2,1,0:T(8,128)} fusion(f32[8,512,1024]{2,1,0:T(8,128)} %fusion.89, f32[8,512,1024]{2,1,0:T(8,128)} %get-tuple-element.67, f32[8,512]{1,0:T(8,128)S(1)} %log_add_fusion.1, bf16[1,1024,8,64]{1,3,2,0:T(8,128)(2,1)S(1)} %bitcast.210), kind=kOutput, calls=%fused_computation.21 | convolution fusion | flops 574624768 | bytes 69763072 | tf_op jit(solution)/shard_map/bhqk,bqhd->bkhd/dot_general | solution.py:79
  581.1 31.5 %add_convert_fusion.2 = bf16[8,64,1024]{2,1,0:T(8,128)(2,1)} fusion(f32[8,64,1024]{2,1,0:T(8,128)} %fusion.11, f32[8,512,1024]{2,1,0:T(8,128)} %fusion.90, f32[8,512]{1,0:T(8,128)S(1)} %log_add_fusion, f32[8,512,1024]{2,1,0:T(8,128)} %copy-done, bf16[1,1024,8,64]{1,3,2,0:T(8,128)(2,1)} %bitcast.208), kind=kOutput, calls=%fused_computation.82 | convolution fusion | flops 575673344 | bytes 70811648 | tf_op jit(solution)/shard_map/bhqk,bqhd->bkhd/dot_general | solution.py:79
  627.1 50.3 %all_to_all.64 = bf16[1,1024,3,1,512]{4,2,3,0,1:T(4,128)(2,1)S(1)} all-to-all(bf16[1,1024,3,1,512]{4,2,3,0,1:T(4,128)(2,1)S(1)} %pad_maximum_fusion), channel_id=1, replica_groups=mesh['fsdp'=16,'seq'=2] {'seq'}, dimensions={1} | all-to-all | bytes 6291456 | tf_op jit(solution)/shard_map/all_to_all | solution.py:200
  681.1 10.5 fusion.117
  691.7 18.5 %fusion.79 = f32[4096,1024]{1,0:T(8,128)} fusion(bf16[1,512,1024]{2,1,0:T(8,128)(2,1)} %param.25, f32[1024]{0:T(1024)S(1)} %bitcast.243, f32[512,4096]{1,0:T(8,128)} %fusion.122, f32[4096]{0:T(1024)S(1)} %bitcast.236), kind=kOutput, calls=%fused_computation.102 | convolution fusion | flops 4317511680 | bytes 26234880 | tf_op jit(solution)/shard_map/btf,btd->fd/dot_general | solution.py:171
  710.8 15.0 %fusion.120 = f32[1024,4096]{1,0:T(8,128)} fusion(bf16[512,4096]{1,0:T(8,128)(2,1)} %copy-done.37, f32[1,512,1024]{2,1,0:T(8,128)} %copy-done.9, f32[1024]{0:T(1024)S(1)} %bitcast.240, f32[1024]{0:T(1024)S(1)} %bitcast.230, f32[512]{0:T(512)S(1)} %add_rsqrt_fusion, f32[512]{0:T(512)S(1)} %broadcast_multiply_fusion.4), kind=kOutput, calls=%fused_computation.165 | convolution fusion | flops 4297588736 | bytes 23080960 | tf_op jit(solution)/shard_map/btd,btf->df/dot_general | solution.py:175
  728.3 61.3 %all-reduce.7 = (f32[2048]{0:T(1024)S(1)}, f32[1024]{0:T(1024)S(1)}, f32[4096]{0:T(1024)S(1)}, f32[1024]{0:T(1024)S(1)}) all-reduce(f32[2048]{0:T(1024)S(1)} %pad_maximum_fusion.2, f32[1024]{0:T(1024)S(1)} %get-tuple-element.47, f32[4096]{0:T(1024)S(1)} %copy-done.21, ...), channel_id=5, replica_groups=mesh['fsdp'=16,'seq'=2] {'fsdp'}, use_global_device_ids=true, to_apply=%region_26.27.clone | all-reduce | flops 8192 | bytes 65536
  827.0 180.7 %reduce-scatter.14.cloned.1.call-done = f32[256,1024]{1,0:T(8,128)} async-done(((f32[4096,1024]{1,0:T(8,128)}), f32[256,1024]{1,0:T(8,128)}) %reduce-scatter.14.cloned.1.call-update) | async-done | bytes 1048592 | tf_op jit(solution)/shard_map/reduce_scatter | solution.py:233
  1007.7 180.6 %reduce-scatter.12.cloned.1.call-done = f32[64,4096]{1,0:T(8,128)} async-done(((f32[1024,4096]{1,0:T(8,128)}), f32[64,4096]{1,0:T(8,128)}) %reduce-scatter.12.cloned.1.call-update) | async-done | bytes 1048592 | tf_op jit(solution)/shard_map/reduce_scatter | solution.py:231
  1188.9 61.3 %all-reduce.2 = bf16[6144]{0:T(1024)(128)(2,1)S(1)} all-reduce(bf16[6144]{0:T(1024)(128)(2,1)S(1)} %convert_reduce_fusion.5), channel_id=3, replica_groups=mesh['fsdp'=16,'seq'=2] {'fsdp'}, use_global_device_ids=true, to_apply=%region_22.23.clone | all-reduce | flops 6144 | bytes 24576
  1259.5 67.0 %reduce-scatter.6.cloned.1.call-done = bf16[64,6144]{1,0:T(8,128)(2,1)} async-done(((bf16[1024,6144]{1,0:T(8,128)(2,1)}), bf16[64,6144]{1,0:T(8,128)(2,1)}) %reduce-scatter.6.cloned.1.call-update) | async-done | bytes 786448 | tf_op jit(solution)/shard_map/reduce_scatter | solution.py:219
  1328.8 85.2 %all-reduce.13.cloned.1.call-done = (f32[64,3072]{1,0:T(8,128)}, f32[64,1024]{1,0:T(8,128)}, f32[64,4096]{1,0:T(8,128)}, f32[256,1024]{1,0:T(8,128)}) async-done(((f32[64,3072]{1,0:T(8,128)}, f32[64,1024]{1,0:T(8,128)}, f32[64,4096]{1,0:T(8,128)}, f32[256,1024]{1,0:T(8,128)}), (f32[64,3072]{1,0:T(8,128)}, f32[64,1024]{1,0:T(8,128)}, f32[64,4096]{1,0:T(8,128)}, ...) | async-done | bytes 3145744 | tf_op jit(solution)/shard_map/psum | solution.py:237
  (211 shorter events, 266.5 us)
Async XLA Ops:
  7.2 106.4 %all-gather.9.cloned.1.call-start = ((), (), s32[]{:S(2)}) async-start(), calls=%async_computation.9 | async-start | bytes 13369344 | tf_op jit(solution)/shard_map/all_gather | solution.py:107
  7.9 167.6 %all-gather.11.cloned.1.call-start = ((), (), s32[]{:S(2)}) async-start(), calls=%async_computation.10 | async-start | bytes 6684672 | tf_op jit(solution)/shard_map/all_gather | solution.py:109
  8.7 341.7 %all-gather.13.cloned.1.call-start = ((), (), s32[]{:S(2)}) async-start(), calls=%async_computation.11 | async-start | bytes 2228224 | tf_op jit(solution)/shard_map/all_gather | solution.py:111
  9.4 347.2 %all-gather.15.cloned.1.call-start = ((), (), s32[]{:S(2)}) async-start(), calls=%async_computation.12 | async-start | bytes 8912896 | tf_op jit(solution)/shard_map/all_gather | solution.py:113
  10.0 358.7 %all-gather.17.cloned.1.call-start = ((), (), s32[]{:S(2)}) async-start(), calls=%async_computation.13 | async-start | bytes 8912896 | tf_op jit(solution)/shard_map/all_gather | solution.py:115
  54.7 120.8 %copy-start.16 = (f32[512]{0:T(512)}, f32[512]{0:T(512)S(1)}, u32[]{:S(2)}) copy-start(f32[512]{0:T(512)S(1)} %broadcast_multiply_fusion.5) | copy-start | bytes 6148
  56.7 118.9 %copy-start.22 = (f32[512]{0:T(512)}, f32[512]{0:T(512)S(1)}, u32[]{:S(2)}) copy-start(f32[512]{0:T(512)S(1)} %add_rsqrt_fusion.1) | copy-start | bytes 6148
  56.7 118.9 %copy-start.2 = (bf16[1,512,1024]{2,1,0:T(8,128)(2,1)S(1)}, bf16[1,512,1024]{2,1,0:T(8,128)(2,1)}, u32[]{:S(2)}) copy-start(bf16[1,512,1024]{2,1,0:T(8,128)(2,1)} %param.13) | copy-start | bytes 3145732
  119.9 55.6 %copy-start.14 = (f32[1,1,1024]{2,1,0:T(1,128)}, f32[1,1,1024]{2,1,0:T(1,128)S(1)}, u32[]{:S(2)}) copy-start(f32[1,1,1024]{2,1,0:T(1,128)S(1)} %get-tuple-element.56) | copy-start | bytes 12292
  120.0 55.6 %copy-start.26 = (f32[1,1,1024]{2,1,0:T(1,128)}, f32[1,1,1024]{2,1,0:T(1,128)S(1)}, u32[]{:S(2)}) copy-start(f32[1,1,1024]{2,1,0:T(1,128)S(1)} %get-tuple-element.55) | copy-start | bytes 12292
  120.0 236.6 %copy-start.24 = (f32[1,1,1024]{2,1,0:T(1,128)}, f32[1,1,1024]{2,1,0:T(1,128)S(1)}, u32[]{:S(2)}) copy-start(f32[1,1,1024]{2,1,0:T(1,128)S(1)} %get-tuple-element.53) | copy-start | bytes 12292
  275.3 75.0 %copy-start.3 = (bf16[1,512,1024]{2,1,0:T(8,128)(2,1)S(1)}, bf16[1,512,1024]{2,1,0:T(8,128)(2,1)}, u32[]{:S(2)}) copy-start(bf16[1,512,1024]{2,1,0:T(8,128)(2,1)} %param.13) | copy-start | bytes 3145732
  287.5 54.6 %all-to-all-start.1 = ((bf16[2,2,131072]{2,1,0:T(2,128)(2,1)}), bf16[2,2,131072]{2,1,0:T(2,128)(2,1)}, u32[]{:S(2)}, u32[]{:S(2)}) async-start(bf16[2,2,131072]{2,1,0:T(2,128)(2,1)} %reshape.533), calls=%async_computation.1 | async-start | bytes 2097152 | tf_op jit(solution)/shard_map/all_to_all | solution.py:147
  324.5 30.5 %copy-start.18 = (f32[1024]{0:T(1024)}, f32[1024]{0:T(1024)S(1)}, u32[]{:S(2)}) copy-start(f32[1024]{0:T(1024)S(1)} %convert_element_type.179) | copy-start | bytes 12292
  409.8 18.1 %all-to-all-start.2 = ((bf16[1,512,2,512]{3,1,0,2:T(8,128)(2,1)}), bf16[1,512,2,512]{3,1,0,2:T(8,128)(2,1)S(1)}, u32[]{:S(2)}, u32[]{:S(2)}) async-start(bf16[1,512,2,512]{3,1,0,2:T(8,128)(2,1)} %copy.53), calls=%async_computation.2 | async-start | bytes 2097152 | tf_op jit(solution)/shard_map/all_to_all | solution.py:188
  413.3 404.9 %reduce-scatter.10.cloned.1.call-start = ((), (), s32[]{:S(2)}) async-start(), calls=%async_computation.16 | async-start | bytes 4456448 | tf_op jit(solution)/shard_map/reduce_scatter | solution.py:229
  418.4 408.6 %reduce-scatter.8.cloned.1.call-start = ((), (), s32[]{:S(2)}) async-start(), calls=%async_computation.15 | async-start | bytes 13369344 | tf_op jit(solution)/shard_map/reduce_scatter | solution.py:227
  511.8 38.6 %copy-start.8 = (bf16[1,1024,1,1,512]{1,4,3,2,0:T(8,128)(2,1)S(1)}, bf16[1,1024,1,1,512]{1,4,3,2,0:T(8,128)(2,1)}, u32[]{:S(2)}) copy-start(bf16[1,1024,1,1,512]{1,4,3,2,0:T(8,128)(2,1)} %copy.49) | copy-start | bytes 3145732
  581.1 37.5 %copy-start.5 = (bf16[1,1024,1,1,512]{4,2,3,0,1:T(2,128)(2,1)S(1)}, bf16[1,1024,1,1,512]{4,2,3,0,1:T(2,128)(2,1)}, u32[]{:S(2)}) copy-start(bf16[1,1024,1,1,512]{4,2,3,0,1:T(2,128)(2,1)} %copy.58) | copy-start | bytes 3145732
  581.1 37.5 %copy-start.6 = (bf16[1,512,1,1,512]{4,2,3,0,1:T(2,128)(2,1)S(1)}, bf16[1,512,1,1,512]{4,2,3,0,1:T(2,128)(2,1)}, u32[]{:S(2)}) copy-start(bf16[1,512,1,1,512]{4,2,3,0,1:T(2,128)(2,1)} %copy.56) | copy-start | bytes 1572868
  691.6 316.1 %reduce-scatter.14.cloned.1.call-start = ((), (), s32[]{:S(2)}) async-start(), calls=%async_computation.18 | async-start | bytes 17825792 | tf_op jit(solution)/shard_map/reduce_scatter | solution.py:233
  710.2 478.1 %reduce-scatter.12.cloned.1.call-start = ((), (), s32[]{:S(2)}) async-start(), calls=%async_computation.17 | async-start | bytes 17825792 | tf_op jit(solution)/shard_map/reduce_scatter | solution.py:231
  725.9 600.6 %reduce-scatter.6.cloned.1.call-start = ((), (), s32[]{:S(2)}) async-start(), calls=%async_computation.14 | async-start | bytes 13369344 | tf_op jit(solution)/shard_map/reduce_scatter | solution.py:219
  818.2 595.9 %all-reduce.13.cloned.1.call-start = ((), (), s32[]{:S(2)}) async-start(), calls=%async_computation.19 | async-start | bytes 6291456 | tf_op jit(solution)/shard_map/psum | solution.py:237
  (27 other events, 240.6 us)
Sparse Core Ops, SparseCore 0:
  10.3 103.2 all-gather.8
  115.9 59.6 all-gather.10
  177.7 40.1 all-gather.12
  219.9 73.0 all-gather.14
  295.0 73.1 all-gather.16
  418.5 72.8 reduce-scatter.9
  691.7 135.2 reduce-scatter.7
  831.1 176.5 reduce-scatter.13
  1011.9 176.4 reduce-scatter.11
  1192.2 134.2 reduce-scatter.5
  1328.9 85.0 all-reduce.12
where the time goes:
time: 1440 us; the launch traced here: 1430 us
  waiting for transfers between devices  647 us (45%)
  matrix products  326 us (23%)
  blocking collectives  313 us (22%)
  local copies, waits for them, and re-layouts  73.4 us (5%)
  other arithmetic  42.9 us (3%)
  between operations  17.8 us (1%)
    reduce_scatter x1, waiting for transfers between devices, on_device(): lax.psum_scatter(grad_fc2, 'fsdp', scatter_dimension=0, tiled=True)  181 us
    reduce_scatter x1, waiting for transfers between devices, on_device(): lax.psum_scatter(grad_fc1, 'fsdp', scatter_dimension=0, tiled=True)  181 us
    unnamed x3, blocking collectives  153 us
    psum x1, waiting for transfers between devices, on_device(): lax.psum((shard_qkv, shard_bqv, shard_proj, shard_bproj, shard_fc1, shard...  85.2 us
    dot_general x2, matrix products, attend_backward(): jnp.einsum('bhqk,bkhd->bqhd', d_raw, keys_all, preferred_element_type=jnp...  73.6 us
    reduce_scatter x1, waiting for transfers between devices, on_device(): lax.psum_scatter(grad_ada.astype(jnp.bfloat16), 'fsdp', scatter_dimension...  67 us
    dot_general x2, matrix products, attend_backward(): jnp.einsum('bhqk,bqhd->bkhd', d_raw, q_block, preferred_element_type=jnp....  62.2 us
    all_gather x1, waiting for transfers between devices, on_device(): lax.all_gather(w_ada, 'fsdp', axis=0, tiled=True)  56.9 us
  transfers between devices with their start and end apart: 13, of which 8 were waited for; matrix products, arithmetic and copies ran while one was open for 27% of the time, Pallas kernels for 0%

commit v1 on v0

v1 whole, which is shorter than its diff:
```python
from functools import partial

import jax
import jax.numpy as jnp
from jax import lax
from jax.experimental import pallas as pl
from jax.experimental.pallas import tpu as pltpu
from jax.sharding import PartitionSpec as P

HD = 64
norm_eps = 1e-06
f32 = jnp.float32
bf16 = jnp.bfloat16
MESH = pl.DeviceIdType.MESH


def grid_of(n):
    b = 2 if n == 16 else 4
    return n // (2 * b), b


def nt(a, b):
    return lax.dot_general(a, b, (((1,), (1,)), ((), ())), preferred_element_type=f32)


def nn(a, b):
    return lax.dot_general(a, b, (((1,), (0,)), ((), ())), preferred_element_type=f32)


def tn(a, b):
    return lax.dot_general(a, b, (((0,), (0,)), ((), ())), preferred_element_type=f32)


def gather_weights(shards, chunks, n, s):
    A, B = grid_of(n)
    nc, ns = len(chunks), len(shards)
    NB = (A - 1) + (B - 1)
    steps = 2 * NB + 1

    def kern(*refs):
        ins, outs = refs[:ns], refs[ns : 2 * ns]
        own_sem, send, recv = refs[2 * ns :]
        me, x = lax.axis_index("fsdp"), lax.axis_index("seq")
        a, b, c = me // (2 * B), (me // 2) % B, me % 2

        def dev(a, b, c):
            return {"fsdp": (a * B + b) * 2 + c}

        apeers = [lax.rem(a + k, A) for k in range(1, A)]
        bpeers = [lax.rem(b + k, B) for k in range(1, B)]
        peers = [dev(p, b, c) for p in apeers] + [dev(a, p, c) for p in bpeers]
        peers.append(dev(a, b, 1 - c))
        if s == 2:
            peers.append({"seq": 1 - x})
        bar = pltpu.get_barrier_semaphore()
        for p in peers:
            pl.semaphore_signal(bar, inc=1, device_id=p, device_id_type=MESH)
        pl.semaphore_wait(bar, len(peers))
        owns = [pltpu.make_async_copy(ins[i], outs[i].at[a, b, c], own_sem.at[i]) for i in range(ns)]
        for o in owns:
            o.start()

        def cp(i, k, src, dst, d):
            r = pltpu.make_async_remote_copy(
                src_ref=src,
                dst_ref=dst,
                send_sem=send.at[i, k],
                recv_sem=recv.at[i, k],
                device_id=d,
                device_id_type=MESH,
            )
            r.start()
            return r

        za, zb, zx, zc = {}, {}, {}, {}

        def part(i):
            w, lo, sz, sh = chunks[i]
            if sh and s == 2:
                return w, pl.ds(pl.multiple_of(lo + x * (sz // 2), 128), sz // 2)
            return w, pl.ds(lo, sz)

        for i in range(nc):
            w, cols = part(i)
            za[i] = [
                cp(i, k, ins[w].at[:, cols], outs[w].at[a, b, c, :, cols], dev(p, b, c))
                for k, p in enumerate(apeers)
            ]
        for o in owns:
            o.wait()

        def phase_b(i):
            w, cols = part(i)
            for r in za[i]:
                r.wait_recv()
            sl = outs[w].at[:, b, c, :, cols]
            zb[i] = [cp(i, A - 1 + k, sl, sl, dev(a, p, c)) for k, p in enumerate(bpeers)]

        def phase_x(i):
            w, cols = part(i)
            for r in zb[i]:
                r.wait_recv()
            zx[i] = []
            if chunks[i][3] and s == 2:
                for k, p in enumerate(apeers):
                    sl = outs[w].at[p, :, c, :, cols]
                    zx[i].append(cp(i, NB + k, sl, sl, {"seq": 1 - x}))
                for k, p in enumerate(bpeers):
                    sl = outs[w].at[a, p, c, :, cols]
                    zx[i].append(cp(i, NB + A - 1 + k, sl, sl, {"seq": 1 - x}))

        def phase_c(i):
            w, lo, sz, sh = chunks[i]
            for r in zx[i]:
                r.wait_recv()
            sl = outs[w].at[:, :, c, :, pl.ds(lo, sz)]
            zc[i] = cp(i, 2 * NB, sl, sl, dev(a, b, 1 - c))

        for i in range(nc + 2):
            if i < nc:
                phase_b(i)
            if 0 <= i - 1 < nc:
                phase_x(i - 1)
            if 0 <= i - 2 < nc:
                phase_c(i - 2)
        for i in range(nc):
            zc[i].wait_recv()
            for r in za[i] + zb[i] + zx[i] + [zc[i]]:
                r.wait_send()

    res = pl.pallas_call(
        kern,
        out_shape=[jax.ShapeDtypeStruct((A, B, 2) + w.shape, w.dtype) for w in shards],
        in_specs=[pl.BlockSpec(memory_space=pltpu.VMEM)] * ns,
        out_specs=[pl.BlockSpec(memory_space=pl.ANY)] * ns,
        scratch_shapes=[
            pltpu.SemaphoreType.DMA((ns,)),
            pltpu.SemaphoreType.DMA((nc, steps)),
            pltpu.SemaphoreType.DMA((nc, steps)),
        ],
        compiler_params=pltpu.CompilerParams(collective_id=0, has_side_effects=True),
        name="gather_weights",
    )(*shards)
    return [r.reshape((n * w.shape[0], w.shape[1])) for r, w in zip(res, shards)]


def fsdp_peers(n, me):
    return [lax.rem(me + k, n) for k in range(1, n)]


def modulation_forward(lifted, w_ada, bias, n):
    rows, E = w_ada.shape
    m = bias.shape[-1]

    def kern(l_ref, w_ref, bias_ref, mod_ref, lf_ref, bout_ref, part, acc, send, recv):
        me = lax.axis_index("fsdp")
        peers = fsdp_peers(n, me)
        bar = pltpu.get_barrier_semaphore()
        for p in peers:
            pl.semaphore_signal(bar, inc=1, device_id={"fsdp": p}, device_id_type=MESH)
        pl.semaphore_wait(bar, n - 1)

        def cp(i, k, src, dst):
            r = pltpu.make_async_remote_copy(
                src_ref=src,
                dst_ref=dst,
                send_sem=send.at[i, k],
                recv_sem=recv.at[i, k],
                device_id={"fsdp": peers[k]},
                device_id_type=MESH,
            )
            r.start()
            return r

        lf_ref[me] = l_ref[me]
        bout_ref[me] = bias_ref[...]
        first = [cp(0, k, l_ref.at[p], lf_ref.at[me]) for k, p in enumerate(peers)]
        other = [cp(1, k, bias_ref, bout_ref.at[me]) for k, p in enumerate(peers)]
        for r in first:
            r.wait_recv()
        lf = lf_ref[...].reshape(n, rows).astype(bf16)
        part[...] = nn(lf, w_ref[...]).reshape(n, 1, E)
        acc[0] = part[me]
        last = [cp(2, k, part.at[p], acc.at[k + 1]) for k, p in enumerate(peers)]
        for r in last:
            r.wait_recv()
        mod_ref[...] = jnp.sum(acc[...], axis=0)
        for r in other:
            r.wait_recv()
        for r in first + other + last:
            r.wait_send()

    vm = pl.BlockSpec(memory_space=pltpu.VMEM)
    return pl.pallas_call(
        kern,
        out_shape=[
            jax.ShapeDtypeStruct((1, E), f32),
            jax.ShapeDtypeStruct((n, 1, rows), f32),
            jax.ShapeDtypeStruct((n, 1, m), f32),
        ],
        in_specs=[vm] * 3,
        out_specs=[vm] * 3,
        scratch_shapes=[
            pltpu.VMEM((n, 1, E), f32),
            pltpu.VMEM((n, 1, E), f32),
            pltpu.SemaphoreType.DMA((3, n - 1)),
            pltpu.SemaphoreType.DMA((3, n - 1)),
        ],
        compiler_params=pltpu.CompilerParams(collective_id=1, has_side_effects=True),
        name="modulation_forward",
    )(lifted, w_ada, bias)


def modulation_backward(d_part, bias_part, lf, w_ada, n, s):
    rows, E = w_ada.shape
    m = bias_part.shape[-1]

    def kern(d_ref, bp_ref, lf_ref, w_ref, gw_ref, gb_ref, dl_ref, bo_ref, dx, dm, lp, bx, bs, bsx, send, recv, xsend, xrecv):
        me, x = lax.axis_index("fsdp"), lax.axis_index("seq")
        peers = fsdp_peers(n, me)
        xpeers = [lax.rem(x + k, s) for k in range(1, s)]
        bar = pltpu.get_barrier_semaphore()
        for p in peers:
            pl.semaphore_signal(bar, inc=1, device_id={"fsdp": p}, device_id_type=MESH)
        for p in xpeers:
            pl.semaphore_signal(bar, inc=1, device_id={"seq": p}, device_id_type=MESH)
        pl.semaphore_wait(bar, n - 1 + s - 1)

        def cp(i, k, src, dst):
            r = pltpu.make_async_remote_copy(
                src_ref=src,
                dst_ref=dst,
                send_sem=send.at[i, k],
                recv_sem=recv.at[i, k],
                device_id={"fsdp": peers[k]},
                device_id_type=MESH,
            )
            r.start()
            return r

        def cpx(i, k, src, dst):
            r = pltpu.make_async_remote_copy(
                src_ref=src,
                dst_ref=dst,
                send_sem=xsend.at[i, k],
                recv_sem=xrecv.at[i, k],
                device_id={"seq": xpeers[k]},
                device_id_type=MESH,
            )
            r.start()
            return r

        q0 = [cpx(0, k, d_ref, dx.at[x]) for k in range(s - 1)]
        q1 = [cp(0, k, bp_ref.at[p], bx.at[me]) for k, p in enumerate(peers)]
        dx[x] = d_ref[...]
        bx[me] = bp_ref[me]
        for r in q0:
            r.wait_recv()
        dm[me] = jnp.sum(dx[...], axis=0).astype(bf16).astype(f32)
        q2 = [cp(1, k, dm.at[me], dm.at[me]) for k, p in enumerate(peers)]
        for r in q1:
            r.wait_recv()
        bs[...] = jnp.sum(bx[...], axis=0)
        bsx[x] = bs[...]
        q3 = [cpx(1, k, bs, bsx.at[x]) for k in range(s - 1)]
        for r in q2:
            r.wait_recv()
        dmod = dm[...].reshape(n, E).astype(bf16)
        lp[...] = nt(dmod, w_ref[...]).reshape(n, 1, rows)
        dl_ref[me] = lp[me]
        q4 = [cp(2, k, lp.at[p], dl_ref.at[me]) for k, p in enumerate(peers)]
        gw_ref[...] = tn(lf_ref[...].reshape(n, rows).astype(bf16), dmod)
        gb_ref[...] = jnp.sum(dm[...], axis=0)
        for r in q3:
            r.wait_recv()
        bo_ref[...] = jnp.sum(bsx[...], axis=0)
        for r in q4:
            r.wait_recv()
        for r in q0 + q1 + q2 + q3 + q4:
            r.wait_send()

    vm = pl.BlockSpec(memory_space=pltpu.VMEM)
    return pl.pallas_call(
        kern,
        out_shape=[
            jax.ShapeDtypeStruct((rows, E), f32),
            jax.ShapeDtypeStruct((1, E), f32),
            jax.ShapeDtypeStruct((n, 1, rows), f32),
            jax.ShapeDtypeStruct((1, m), f32),
        ],
        in_specs=[vm] * 4,
        out_specs=[vm] * 4,
        scratch_shapes=[
            pltpu.VMEM((s, 1, E), f32),
            pltpu.VMEM((n, 1, E), f32),
            pltpu.VMEM((n, 1, rows), f32),
            pltpu.VMEM((n, 1, m), f32),
            pltpu.VMEM((1, m), f32),
            pltpu.VMEM((s, 1, m), f32),
            pltpu.SemaphoreType.DMA((3, n - 1)),
            pltpu.SemaphoreType.DMA((3, n - 1)),
            pltpu.SemaphoreType.DMA((2, s - 1)),
            pltpu.SemaphoreType.DMA((2, s - 1)),
        ],
        compiler_params=pltpu.CompilerParams(collective_id=2, has_side_effects=True),
        name="modulation_backward",
    )(d_part, bias_part, lf, w_ada)


def head_mask(ref_shape, h):
    low = lax.broadcasted_iota(jnp.int32, ref_shape, 1) < HD
    return low if h == 0 else ~low


def pick(values, h):
    return jnp.where(head_mask(values.shape, h), values, jnp.zeros_like(values))


def attend_forward_kernel(n, q_ref, *refs):
    k_refs, v_refs, (o_ref, lse_ref) = refs[:n], refs[n : 2 * n], refs[2 * n :]
    q = q_ref[...] * bf16(HD**-0.5)
    total = None
    for h in range(2):
        qh = pick(q, h)
        scores = [nt(k[...], qh) for k in k_refs]
        top = scores[0].max(axis=0, keepdims=True)
        for sc in scores[1:]:
            top = jnp.maximum(top, sc.max(axis=0, keepdims=True))
        mass, out = None, None
        for sc, v in zip(scores, v_refs):
            p = jnp.exp(sc - top)
            part = p.sum(axis=0, keepdims=True)
            mass = part if mass is None else mass + part
            o = tn(pick(v[...], h), p.astype(bf16))
            out = o if out is None else out + o
        out = out * (1.0 / mass)
        total = out if total is None else total + out
        lse_ref[0, h : h + 1, :] = top + jnp.log(mass)
    o_ref[...] = total.T.astype(bf16)


def attend_forward(q, ks, vs):
    T, D = q.shape
    n = len(ks)

    def col(rows):
        return pl.BlockSpec((rows, 128), lambda i: (0, i))

    keys = sum(k.shape[0] for k in ks)
    return pl.pallas_call(
        partial(attend_forward_kernel, n),
        grid=(D // 128,),
        in_specs=[col(T)] + [col(k.shape[0]) for k in ks] * 2,
        out_specs=[col(T), pl.BlockSpec((1, 2, T), lambda i: (i, 0, 0))],
        out_shape=[jax.ShapeDtypeStruct((T, D), bf16), jax.ShapeDtypeStruct((D // 128, 2, T), f32)],
        cost_estimate=pl.CostEstimate(flops=16 * T * keys * D, bytes_accessed=4 * (T + keys) * D, transcendentals=0),
        name="attend_forward",
    )(q, *ks, *vs)


def attend_backward_kernel(n, q_ref, e_ref, lse_ref, *refs):
    k_refs, v_refs = refs[:n], refs[n : 2 * n]
    dq_ref, dk_refs, dv_refs = refs[2 * n], refs[2 * n + 1 : 3 * n + 1], refs[3 * n + 1 :]
    q, e = q_ref[...] * bf16(HD**-0.5), e_ref[...]
    dqt = None
    dks, dvs = [None] * n, [None] * n
    for h in range(2):
        qh, eh = pick(q, h), pick(e, h)
        lse = lse_ref[0, h : h + 1, :]
        probs, dprobs, cross = [], [], None
        for j in range(n):
            p = jnp.exp(nt(k_refs[j][...], qh) - lse)
            dp = nt(v_refs[j][...], eh)
            part = (p * dp).sum(axis=0, keepdims=True)
            cross = part if cross is None else cross + part
            dv = nn(p.astype(bf16), eh)
            dvs[j] = dv if dvs[j] is None else dvs[j] + dv
            probs.append(p)
            dprobs.append(dp)
        for j in range(n):
            ds = (probs[j] * (dprobs[j] - cross)).astype(bf16)
            dk = nn(ds, qh)
            dks[j] = dk if dks[j] is None else dks[j] + dk
            t = tn(pick(k_refs[j][...], h), ds)
            dqt = t if dqt is None else dqt + t
    dq_ref[...] = (dqt * (HD**-0.5)).T.astype(bf16)
    for j in range(n):
        dk_refs[j][...] = dks[j].astype(dk_refs[j].dtype)
        dv_refs[j][...] = dvs[j].astype(dv_refs[j].dtype)


def attend_backward(q, e, lse, ks, vs):
    T, D = q.shape
    n = len(ks)

    def col(rows):
        return pl.BlockSpec((rows, 128), lambda i: (0, i))

    keys = sum(k.shape[0] for k in ks)
    cols = [col(k.shape[0]) for k in ks]
    kv = [jax.ShapeDtypeStruct(k.shape, f32 if j == 0 else bf16) for j, k in enumerate(ks)]
    res = pl.pallas_call(
        partial(attend_backward_kernel, n),
        grid=(D // 128,),
        in_specs=[col(T), col(T), pl.BlockSpec((1, 2, T), lambda i: (i, 0, 0))] + cols * 2,
        out_specs=[col(T)] + cols * 2,
        out_shape=[jax.ShapeDtypeStruct((T, D), bf16)] + kv * 2,
        cost_estimate=pl.CostEstimate(flops=30 * T * keys * D, bytes_accessed=8 * (T + keys) * D, transcendentals=0),
        name="attend_backward",
    )(q, e, lse, *ks, *vs)
    return res[0], res[1 : n + 1], res[n + 1 :]


def seq_shift(value, k, s):
    return lax.ppermute(value, "seq", [(i, (i + k) % s) for i in range(s)])


def reduce_rows(make, mine_c, n, s):
    A, B = grid_of(n)

    def at(a, b, c):
        return (a * B + b) * 2 + c

    every = [(a, b, c) for a in range(A) for b in range(B) for c in range(2)]
    me = lax.axis_index("fsdp")
    a, b, c = me // (2 * B), (me // 2) % B, me % 2
    away = make(1 - c).astype(bf16)
    away = lax.ppermute(away, "fsdp", [(at(*p), at(p[0], p[1], 1 - p[2])) for p in every])
    total = make(c) + away.astype(f32)
    parts = []
    for k in range(1, B):
        send = lax.dynamic_index_in_dim(total, (b + k) % B, 1, keepdims=False).astype(bf16)
        parts.append(lax.ppermute(send, "fsdp", [(at(*p), at(p[0], (p[1] + k) % B, p[2])) for p in every]))
    total = lax.dynamic_index_in_dim(total, b, 1, keepdims=False)
    for p in parts:
        total = total + p.astype(f32)
    parts = []
    for k in range(1, A):
        send = lax.dynamic_index_in_dim(total, (a + k) % A, 0, keepdims=False).astype(bf16)
        parts.append(lax.ppermute(send, "fsdp", [(at(*p), at((p[0] + k) % A, p[1], p[2])) for p in every]))
    total = lax.dynamic_index_in_dim(total, a, 0, keepdims=False)
    for p in parts:
        total = total + p.astype(f32)
    if s != 2:
        return lax.psum(total, "seq")
    total = total.astype(bf16)
    return total.astype(f32) + seq_shift(total, 1, 2).astype(f32)


def weight_grad(lhs, rhs, n, s):
    A, B = grid_of(n)
    T, R = lhs.shape
    r = R // n
    split = lhs.reshape(T, A * B, 2, r)

    def make(c):
        rows = lax.dynamic_index_in_dim(split, c, 2, keepdims=False).reshape(T, A * B * r)
        return tn(rows, rhs).reshape(A, B, r, rhs.shape[1])

    return reduce_rows(make, None, n, s)


def layer_norm(values):
    center = values - jnp.mean(values, axis=-1, keepdims=True)
    rscale = lax.rsqrt(jnp.mean(center * center, axis=-1, keepdims=True) + norm_eps)
    return (center * rscale, rscale)


def norm_back(upstream, normed, rscale):
    mean_up = jnp.mean(upstream, axis=-1, keepdims=True)
    mean_cross = jnp.mean(upstream * normed, axis=-1, keepdims=True)
    return rscale * (upstream - mean_up - normed * mean_cross)


def on_device(
    tokens,
    condition,
    w_ada,
    b_ada,
    w_qkv,
    b_qv,
    w_proj,
    b_proj,
    w_fc1,
    b_fc1,
    w_fc2,
    b_fc2,
    cotangent,
):
    n, s = lax.axis_size("fsdp"), lax.axis_size("seq")
    width = tokens.shape[-1]
    T = tokens.shape[1]
    tokens_f = tokens[0].astype(f32)
    grad_out = cotangent[0].astype(f32)

    lifted, silu_back = jax.vjp(jax.nn.silu, condition.astype(f32))
    lifted_q = lifted.astype(bf16).astype(f32).reshape(n, 1, width // n)
    packed = [b_qv, b_proj, b_fc1, b_fc2, b_ada]
    edges = [sum(v.shape[0] for v in packed[:i]) for i in range(6)]
    modulation, lf, biases = modulation_forward(lifted_q, w_ada, jnp.concatenate(packed).astype(f32)[None], n)
    qv_b, proj_b, fc1_b, fc2_b, ada_b = [biases[:, 0, edges[i] : edges[i + 1]].reshape(1, -1) for i in range(5)]
    modulation = modulation + ada_b
    shift_one, scale_one, gate_one, shift_two, scale_two, gate_two = jnp.split(modulation, 6, axis=-1)

    h, q4 = w_fc1.shape[1], w_fc2.shape[1]
    chunks = [(0, width, width, True), (0, 2 * width, width, True), (0, 0, width, True), (1, 0, width, True)]
    chunks += [(3, i * (q4 // 4), q4 // 4, i != 2) for i in range(4)]
    chunks += [(2, i * (h // 8), h // 8, i % 2 == 0) for i in range(8)]
    qkv_w, proj_w, fc1_w, fc2_w = gather_weights([w_qkv, w_proj, w_fc1, w_fc2], chunks, n, s)

    normed_one, rscale_one = layer_norm(tokens_f)
    hidden_one = (normed_one * (1.0 + scale_one) + shift_one).astype(bf16)
    keys = nn(hidden_one, qkv_w[:, width : 2 * width]).astype(bf16)
    values = (nn(hidden_one, qkv_w[:, 2 * width :]) + qv_b[:, width:]).astype(bf16)
    ks = [keys] + [seq_shift(keys, k, s) for k in range(1, s)]
    vs = [values] + [seq_shift(values, k, s) for k in range(1, s)]
    queries = (nn(hidden_one, qkv_w[:, :width]) + qv_b[:, :width]).astype(bf16)
    attn, lse = attend_forward(queries, ks, vs)
    branch = nn(attn, proj_w) + proj_b
    middle = tokens_f + gate_one * branch

    normed_two, rscale_two = layer_norm(middle)
    hidden_two = (normed_two * (1.0 + scale_two) + shift_two).astype(bf16)
    pre_act = nn(hidden_two, fc1_w) + fc1_b
    act_f, gelu_back = jax.vjp(partial(jax.nn.gelu, approximate=True), pre_act)
    act_b = act_f.astype(bf16)
    mlp_out = nn(act_b, fc2_w) + fc2_b
    result = (middle + gate_two * mlp_out).astype(bf16)

    d_gate_two = jnp.sum(grad_out * mlp_out, axis=0, keepdims=True)
    d_mlp = (grad_out * gate_two).astype(bf16)
    total_fc2 = weight_grad(act_b, d_mlp, n, s)
    bias_fc2 = jnp.sum(d_mlp, axis=0, dtype=f32)
    d_act = nt(d_mlp, fc2_w)
    d_pre = gelu_back(d_act)[0].astype(bf16)
    total_fc1 = weight_grad(hidden_two, d_pre, n, s)
    bias_fc1 = jnp.sum(d_pre, axis=0, dtype=f32)
    d_hidden_two = nt(d_pre, fc1_w)
    d_shift_two = jnp.sum(d_hidden_two, axis=0, keepdims=True)
    d_scale_two = jnp.sum(d_hidden_two * normed_two, axis=0, keepdims=True)
    d_middle = grad_out + norm_back(d_hidden_two * (1.0 + scale_two), normed_two, rscale_two)

    d_gate_one = jnp.sum(d_middle * branch, axis=0, keepdims=True)
    d_branch = (d_middle * gate_one).astype(bf16)
    total_proj = weight_grad(attn, d_branch, n, s)
    bias_proj = jnp.sum(d_branch, axis=0, dtype=f32)
    d_attn = nt(d_branch, proj_w).astype(bf16)
    grad_q, dks, dvs = attend_backward(queries, d_attn, lse, ks, vs)
    grad_k, grad_v = dks[0], dvs[0]
    for k in range(1, s):
        grad_k = grad_k + seq_shift(dks[k], s - k, s).astype(f32)
        grad_v = grad_v + seq_shift(dvs[k], s - k, s).astype(f32)
    d_qkv = jnp.concatenate([grad_q, grad_k.astype(bf16), grad_v.astype(bf16)], axis=1)
    total_qkv = weight_grad(hidden_one, d_qkv, n, s)
    column_sums = jnp.sum(d_qkv, axis=0, dtype=f32)
    bias_qv = jnp.concatenate([column_sums[:width], column_sums[2 * width :]])
    d_hidden_one = nt(d_qkv, qkv_w)
    d_shift_one = jnp.sum(d_hidden_one, axis=0, keepdims=True)
    d_scale_one = jnp.sum(d_hidden_one * normed_one, axis=0, keepdims=True)
    grad_input = d_middle + norm_back(d_hidden_one * (1.0 + scale_one), normed_one, rscale_one)

    d_part = jnp.concatenate(
        [d_shift_one, d_scale_one, d_gate_one, d_shift_two, d_scale_two, d_gate_two], axis=-1
    )
    bias_part = jnp.concatenate(
        [bias_qv.reshape(n, -1), bias_proj.reshape(n, -1), bias_fc1.reshape(n, -1), bias_fc2.reshape(n, -1)], axis=1
    )[:, None, :]
    total_ada, sums_ada, d_lifted, total_bias = modulation_backward(d_part, bias_part, lf, w_ada, n, s)
    share = b_ada.shape[0]
    total_bada = lax.dynamic_slice_in_dim(sums_ada[0], lax.axis_index("fsdp") * share, share)
    grad_condition = silu_back(d_lifted.reshape(1, width))[0]
    total_bqv, total_bproj, total_bfc1, total_bfc2 = [total_bias[0, edges[i] : edges[i + 1]] for i in range(4)]
    return (
        result[None],
        grad_input[None],
        grad_condition,
        total_ada,
        total_bada,
        total_qkv,
        total_bqv,
        total_proj,
        total_bproj,
        total_fc1,
        total_bfc1,
        total_fc2,
        total_bfc2,
    )


def solution(mesh):
    weights = (P("fsdp", None), P("fsdp")) * 5
    return jax.shard_map(
        on_device,
        mesh=mesh,
        in_specs=(P("fsdp", "seq", None), P("fsdp", None)) + weights + (P("fsdp", "seq", None),),
        out_specs=(P("fsdp", "seq", None), P("fsdp", "seq", None), P("fsdp", None)) + weights,
        check_vma=False,
    )
```

time: 1440 us -> 647 us (0.45)
  waiting for transfers between devices: 647 us -> 200 us
  blocking collectives: 313 us -> 0 us
  Pallas kernels: 0 us -> 226 us
  matrix products: 326 us -> 103 us
  other arithmetic: 42.9 us -> 23 us
  starting transfers between devices: 8.89 us -> 27.1 us
  between operations: 17.8 us -> 1.81 us
    reduce_scatter x5 -> x0, waiting for transfers between devices: 437 us -> none  [the longest x1 181 us: on_device(): lax.psum_scatter(grad_fc2, 'fsdp', scatter_dimension=0, tiled=True)]
    pallas_call x0 -> x5, Pallas kernels: none -> 226 us  [the longest x1 127 us: gather_weights(): pl.pallas_call(kern, out_shape=[jax.ShapeDtypeStruct((A, B, 2) + w.shape,...]
    dot_general x26 -> x18, matrix products: 326 us -> 103 us  [the longest x6 43.2 us: nn(): lax.dot_general(a, b, (((1,), (0,)), ((), ())), preferred_element_type=f32)]
    ppermute x0 -> x28, waiting for transfers between devices: none -> 200 us  [the longest x4 79.3 us: reduce_rows(): lax.ppermute(send, 'fsdp', [(at(*p), at(p[0], (p[1] + k) % B, p[2])) for...]
    unnamed x3 -> x0, blocking collectives: 153 us -> none
    all_gather x5 -> x0, waiting for transfers between devices: 112 us -> none  [the longest x1 56.9 us: on_device(): lax.all_gather(w_ada, 'fsdp', axis=0, tiled=True)]
    all_to_all x2 -> x0, blocking collectives: 90 us -> none  [the longest x1 50.3 us: on_device(): lax.all_to_all(d_spread, 'seq', split_axis=1, concat_axis=3, tiled=True)]
    psum x1 -> x0, waiting for transfers between devices: 85.2 us -> none  [on_device(): lax.psum((shard_qkv, shard_bqv, shard_proj, shard_bproj, shard_fc1, shard...]
  transfers between devices with their start and end apart: 13 -> 28, of which waited for: 8 -> 13; matrix products, arithmetic and copies ran while one was open for 27% -> 16% of each run, Pallas kernels for 0% -> 5%
where the time goes in v1:
time: 647 us; the launch traced here: 641 us
  Pallas kernels  226 us (35%)
  waiting for transfers between devices  200 us (31%)
  matrix products  103 us (16%)
  local copies, waits for them, and re-layouts  59.5 us (9%)
  starting transfers between devices  27.1 us (4%)
  other arithmetic  23 us (4%)
    pallas_call x1, Pallas kernels, gather_weights(): pl.pallas_call(kern, out_shape=[jax.ShapeDtypeStruct((A, B, 2) + w.shape,...  127 us
    ppermute x4, waiting for transfers between devices, reduce_rows(): lax.ppermute(send, 'fsdp', [(at(*p), at(p[0], (p[1] + k) % B, p[2])) for...  79.3 us
    ppermute x12, waiting for transfers between devices, reduce_rows(): lax.ppermute(send, 'fsdp', [(at(*p), at((p[0] + k) % A, p[1], p[2])) for...  73.4 us
    ppermute x8, waiting for transfers between devices, seq_shift(): return lax.ppermute(value, 'seq', [(i, (i + k) % s) for i in range(s)])  47.7 us
    dot_general x6, matrix products, nn(): lax.dot_general(a, b, (((1,), (0,)), ((), ())), preferred_element_type=f32)  43.2 us
    dot_general x8, matrix products, tn(): lax.dot_general(a, b, (((0,), (0,)), ((), ())), preferred_element_type=f32)  30.8 us
    pallas_call x1, Pallas kernels, attend_backward(): pl.pallas_call(partial(attend_backward_kernel, n), grid=(D // 128,), in_s...  30.3 us
    pallas_call x1, Pallas kernels, modulation_backward(): pl.pallas_call(kern, out_shape=[jax.ShapeDtypeStruct((rows, E), f32), jax...  29.7 us
  transfers between devices with their start and end apart: 28, of which 13 were waited for; matrix products, arithmetic and copies ran while one was open for 16% of the time, Pallas kernels for 5%

profile of v1, /device:TPU:0, one launch (start us, length us, event | category | flops | bytes accessed | tf_op | source)
XLA Modules:
  0.0 640.9 jit_solution(13276111433760377696)
XLA Ops:
  4.8 20.6 %modulation_forward.1 = (f32[1,6144]{1,0:T(1,128)}, f32[16,1,64]{2,1,0:T(1,128)}, f32[16,1,896]{2,1,0:T(1,128)}) custom-call(f32[16,1,64]{2,1,0:T(1,128)} %reshape.329.l_ref, bf16[64,6144]{1,0:T(8,128)(2,1)} %w_ref.3, f32[1,896]{1,0:T(1,128)} %convert_element_type.315.bias_ref), custom_call_target="tpu_custom_call" | custom-call | tf_op jit(solution)/shard_map/modulation_forward/pallas_call | solution.py:194
  28.9 127.5 %gather_weights.1 = (bf16[4,2,2,64,3072]{4,3,2,1,0:T(8,128)(2,1)}, bf16[4,2,2,64,1024]{4,3,2,1,0:T(8,128)(2,1)}, bf16[4,2,2,64,4096]{4,3,2,1,0:T(8,128)(2,1)}, bf16[4,2,2,256,1024]{4,3,2,1,0:T(8,128)(2,1)}) custom-call(bf16[64,3072]{1,0:T(8,128)(2,1)} %refs_0_.1, bf16[64,1024]{1,0:T(8,128)(2,1)} %refs_1_.1, bf16[64,4096]{1,0:T(8,128)(2,1)} %refs_2_.1, ...), custom_call_target="tpu_custom_call" | custom-call | tf_op jit(solution)/shard_map/gather_weights/pallas_call | solution.py:131
  172.9 13.7 %collective-permute-done.refs_1_ = bf16[512,1024]{1,0:T(8,128)(2,1)} collective-permute-done((bf16[512,1024]{1,0:T(8,128)(2,1)}, bf16[512,1024]{1,0:T(8,128)(2,1)}, u32[]{:S(2)}, u32[]{:S(2)}) %collective-permute-start) | collective-permute-done | bytes 1048608 | tf_op jit(solution)/shard_map/ppermute | solution.py:415
  186.6 21.9 %collective-permute-done.1.refs_3_ = bf16[512,1024]{1,0:T(8,128)(2,1)} collective-permute-done((bf16[512,1024]{1,0:T(8,128)(2,1)}, bf16[512,1024]{1,0:T(8,128)(2,1)}, u32[]{:S(2)}, u32[]{:S(2)}) %collective-permute-start.1) | collective-permute-done | bytes 1048608 | tf_op jit(solution)/shard_map/ppermute | solution.py:415
  208.5 17.8 %attend_forward.1 = (bf16[512,1024]{1,0:T(8,128)(2,1)}, f32[8,2,512]{2,1,0:T(2,128)}) custom-call(bf16[512,1024]{1,0:T(8,128)(2,1)} %add_convert_fusion.6.q_ref, bf16[512,1024]{1,0:T(8,128)(2,1)} %fusion.37.refs_0_, bf16[512,1024]{1,0:T(8,128)(2,1)} %collective-permute-done.refs_1_, bf16[512,1024]{1,0:T(8,128)(2,1)} %add_convert_fusion.5.refs_2_, ...), custom_call_target="tpu_custom_call" | custom-call | flops 8589934592 | bytes 6291456 | tf_op jit(solution)/shard_map/attend_forward/pallas_call | solution.py:350
  237.1 14.6 %multiply_convert_fusion = (bf16[512,4096]{1,0:T(8,128)(2,1)}, f32[512,4096]{1,0:T(8,128)}) fusion(f32[4096]{0:T(1024)S(1)} %bitcast.275, bf16[512,1024]{1,0:T(8,128)(2,1)} %add_convert_fusion.4, bf16[1024,4096]{1,0:T(8,128)(2,1)} %bitcast.299), kind=kOutput, calls=%fused_computation.12 | convolution fusion | flops 4315938816 | bytes 22036480 | tf_op jit(solution)/shard_map/dot_general | solution.py:27
  251.7 13.7 %convert_reduce_fusion = (f32[4096]{0:T(1024)S(1)}, bf16[512,4096]{1,0:T(8,128)(2,1)S(1)}) fusion(f32[512,4096]{1,0:T(8,128)} %get-tuple-element.110, f32[4096]{0:T(1024)S(1)} %bitcast.276, bf16[4096,1024]{1,0:T(8,128)(2,1)} %bitcast.297, f32[1024]{0:T(1024)S(1)} %bitcast.277, bf16[1,512,1024]{2,1,0:T(8,128)(2,1)S(1)} %copy-done.30), kind=kOutput, calls=%fused_computation.11 | convolution fusion | flops 4344770560 | bytes 22056960 | tf_op jit(solution)/shard_map/dot_general | solution.py:23
  265.5 6.3 multiply_reduce_fusion
  271.8 8.0 %reshape.325 = bf16[512,8,2,256]{3,2,1,0:T(2,128)(2,1)} reshape(bf16[512,4096]{1,0:T(8,128)(2,1)} %get-tuple-element.109) | data formatting | bytes 8388608 | tf_op jit(solution)/shard_map/reshape | solution.py:454
  279.8 12.4 %convert_reduce_fusion.2 = (f32[1024]{0:T(1024)S(1)}, f32[1024]{0:T(1024)S(1)}, bf16[1,512,1024]{2,1,0:T(8,128)(2,1)}, f32[1024]{0:T(1024)S(1)}, bf16[512,1024]{1,0:T(8,128)(2,1)S(1)}, /*index=5*/f32[512,1024]{1,0:T(8,128)}) fusion(bf16[1,512,1024]{2,1,0:T(8,128)(2,1)} %param.25, f32[1024]{0:T(1024)S(1)} %bitcast.278, f32[1024]{0:T(1024)S(1)} %add.357, ...), kind=kOutput, calls=%fused_computation.51 | convolution fusion | flops 4307022848 | bytes 22056960 | tf_op jit(solution)/shard_map/dot_general | solution.py:27
  294.5 30.3 %attend_backward.1 = (bf16[512,1024]{1,0:T(8,128)(2,1)}, f32[512,1024]{1,0:T(8,128)}, bf16[512,1024]{1,0:T(8,128)(2,1)}, f32[512,1024]{1,0:T(8,128)}, bf16[512,1024]{1,0:T(8,128)(2,1)}) custom-call(bf16[512,1024]{1,0:T(8,128)(2,1)} %add_convert_fusion.6.q_ref, bf16[512,1024]{1,0:T(8,128)(2,1)} %convolution_convert_fusion.3.e_ref, ...), custom_call_target="tpu_custom_call" | custom-call | flops 16106127360 | bytes 12582912 | tf_op jit(solution)/shard_map/attend_backward/pallas_call | solution.py:402
  336.4 10.1 %constant_dynamic-slice_fusion.1 = (bf16[512,8,1,256]{3,2,1,0:T(2,128)(2,1)}, bf16[512,8,1,256]{3,2,1,0:T(2,128)(2,1)}) fusion(bf16[512,8,2,256]{3,2,1,0:T(2,128)(2,1)S(1)} %copy-done, s32[]{:T(128)S(6)} %select_n.139, s32[]{:T(128)S(6)} %select_n.140), kind=kLoop, calls=%fused_computation.142 | loop fusion | bytes 8388616 | tf_op jit(solution)/shard_map/jit(dynamic_index_in_dim)/dynamic_slice | solution.py:457
  346.5 9.0 %copy.36 = bf16[512,8,1,256]{0,3,1,2:T(8,128)(2,1)S(1)} copy(bf16[512,8,1,256]{3,2,1,0:T(2,128)(2,1)} %get-tuple-element.74) | data formatting | bytes 4194304
  355.5 10.5 %copy.35 = bf16[512,8,1,256]{0,3,1,2:T(8,128)(2,1)} copy(bf16[512,8,1,256]{3,2,1,0:T(2,128)(2,1)} %get-tuple-element.73) | data formatting | bytes 4194304
  380.6 7.0 %multiply_reduce_fusion.2 = (f32[1024]{0:T(1024)S(1)}, f32[512]{0:T(512)S(1)}, f32[512]{0:T(512)S(1)}, f32[1024]{0:T(1024)S(1)}, f32[512,1024]{1,0:T(8,128)S(1)}) fusion(bf16[1,512,1024]{2,1,0:T(8,128)(2,1)S(1)} %copy-done.1, f32[512]{0:T(512)S(1)} %add_rsqrt_fusion.1, f32[512]{0:T(512)S(1)} %broadcast_multiply_fusion.5, f32[1024]{0:T(1024)S(1)} %bitcast.268, ...), kind=kOutput, calls=%fused_computation.55 | convolution fusion | flops 3235902464 | bytes 12603392 | tf_op jit(solution)/shard_map/dot_general | solution.py:23
  395.4 29.7 %modulation_backward.1 = (f32[64,6144]{1,0:T(8,128)}, f32[1,6144]{1,0:T(1,128)}, f32[16,1,64]{2,1,0:T(1,128)}, f32[1,512]{1,0:T(1,128)}) custom-call(f32[1,6144]{1,0:T(1,128)} %copy-done.26, f32[16,1,512]{2,1,0:T(1,128)} %broadcast_in_dim.44.bp_ref, f32[16,1,64]{2,1,0:T(1,128)} %get-tuple-element.44.lf_ref, bf16[64,6144]{1,0:T(8,128)(2,1)} %w_ref.3), custom_call_target="tpu_custom_call" | custom-call | tf_op jit(solution)/shard_map/modulation_backward/pallas_call | solution.py:283
  437.1 8.3 %collective-permute-done.13 = bf16[64,1024]{1,0:T(8,128)(2,1)S(1)} collective-permute-done((bf16[64,1024]{1,0:T(8,128)(2,1)S(1)}, bf16[64,1024]{1,0:T(8,128)(2,1)S(1)}, u32[]{:S(2)}, u32[]{:S(2)}) %collective-permute-start.13) | collective-permute-done | bytes 131104 | tf_op jit(solution)/shard_map/ppermute | solution.py:440
  463.2 30.2 %collective-permute-done.5 = bf16[4,64,3072]{2,1,0:T(8,128)(2,1)S(1)} collective-permute-done((bf16[4,64,3072]{2,1,0:T(8,128)(2,1)S(1)}, bf16[4,64,3072]{2,1,0:T(8,128)(2,1)S(1)}, u32[]{:S(2)}, u32[]{:S(2)}) %collective-permute-start.5) | collective-permute-done | bytes 1572896 | tf_op jit(solution)/shard_map/ppermute | solution.py:433
  504.1 21.2 %collective-permute-done.7 = bf16[64,3072]{1,0:T(8,128)(2,1)S(1)} collective-permute-done((bf16[64,3072]{1,0:T(8,128)(2,1)S(1)}, bf16[64,3072]{1,0:T(8,128)(2,1)S(1)}, u32[]{:S(2)}, u32[]{:S(2)}) %collective-permute-start.7) | collective-permute-done | bytes 393248 | tf_op jit(solution)/shard_map/ppermute | solution.py:440
  526.6 11.7 %collective-permute-done.17 = bf16[4,64,4096]{2,1,0:T(8,128)(2,1)S(1)} collective-permute-done((bf16[4,64,4096]{2,1,0:T(8,128)(2,1)S(1)}, bf16[4,64,4096]{2,1,0:T(8,128)(2,1)S(1)}, u32[]{:S(2)}, u32[]{:S(2)}) %collective-permute-start.17) | collective-permute-done | bytes 2097184 | tf_op jit(solution)/shard_map/ppermute | solution.py:433
  543.1 37.4 %collective-permute-done.23 = bf16[4,256,1024]{2,1,0:T(8,128)(2,1)S(1)} collective-permute-done((bf16[4,256,1024]{2,1,0:T(8,128)(2,1)S(1)}, bf16[4,256,1024]{2,1,0:T(8,128)(2,1)S(1)}, u32[]{:S(2)}, u32[]{:S(2)}) %collective-permute-start.23) | collective-permute-done | bytes 2097184 | tf_op jit(solution)/shard_map/ppermute | solution.py:433
  588.1 6.2 collective-permute-done.26
  594.2 32.8 %collective-permute-done.25 = bf16[256,1024]{1,0:T(8,128)(2,1)S(1)} collective-permute-done((bf16[256,1024]{1,0:T(8,128)(2,1)S(1)}, bf16[256,1024]{1,0:T(8,128)(2,1)S(1)}, u32[]{:S(2)}, u32[]{:S(2)}) %collective-permute-start.25) | collective-permute-done | bytes 524320 | tf_op jit(solution)/shard_map/ppermute | solution.py:440
  629.5 8.6 %collective-permute-done.27 = bf16[256,1024]{1,0:T(8,128)(2,1)S(1)} collective-permute-done((bf16[256,1024]{1,0:T(8,128)(2,1)S(1)}, bf16[256,1024]{1,0:T(8,128)(2,1)S(1)}, u32[]{:S(2)}, u32[]{:S(2)}) %collective-permute-start.27) | collective-permute-done | bytes 524320 | tf_op jit(solution)/shard_map/ppermute | solution.py:415
  (207 shorter events, 129.8 us)
Async XLA Ops:
  160.2 26.3 %collective-permute-start = (bf16[512,1024]{1,0:T(8,128)(2,1)}, bf16[512,1024]{1,0:T(8,128)(2,1)}, u32[]{:S(2)}, u32[]{:S(2)}) collective-permute-start(bf16[512,1024]{1,0:T(8,128)(2,1)} %fusion.37.refs_0_), channel_id=1, source_target_pairs={{0,1},{1,0},{2,3},{3,2},{4,5},{5,4},{6,7},{7,6},{8,9},{9,8},{10,11... | collective-permute-start | bytes 3145736 | tf_op jit(solution)/shard_map/ppermute | solution.py:415
  165.2 43.2 %collective-permute-start.1 = (bf16[512,1024]{1,0:T(8,128)(2,1)}, bf16[512,1024]{1,0:T(8,128)(2,1)}, u32[]{:S(2)}, u32[]{:S(2)}) collective-permute-start(bf16[512,1024]{1,0:T(8,128)(2,1)} %add_convert_fusion.5.refs_2_), channel_id=1, source_target_pairs={{0,1},{1,0},{2,3},{3,2},{4,5},{5,4},{6,7},{7,6},{8,9},{9,8},{10,11... | collective-permute-start | bytes 3145736 | tf_op jit(solution)/shard_map/ppermute | solution.py:415
  324.8 46.9 %collective-permute-start.3 = (bf16[512,1024]{1,0:T(8,128)(2,1)}, bf16[512,1024]{1,0:T(8,128)(2,1)}, u32[]{:S(2)}, u32[]{:S(2)}) collective-permute-start(bf16[512,1024]{1,0:T(8,128)(2,1)} %get-tuple-element.43), channel_id=1, source_target_pairs={{0,1},{1,0},{2,3},{3,2},{4,5},{5,4},{6,7},{7,6},{8,9},{9,8},{10,11... | collective-permute-start | bytes 3145736 | tf_op jit(solution)/shard_map/ppermute | solution.py:415
  326.0 47.4 %collective-permute-start.2 = (bf16[512,1024]{1,0:T(8,128)(2,1)}, bf16[512,1024]{1,0:T(8,128)(2,1)}, u32[]{:S(2)}, u32[]{:S(2)}) collective-permute-start(bf16[512,1024]{1,0:T(8,128)(2,1)} %get-tuple-element.41), channel_id=1, source_target_pairs={{0,1},{1,0},{2,3},{3,2},{4,5},{5,4},{6,7},{7,6},{8,9},{9,8},{10,11... | collective-permute-start | bytes 3145736 | tf_op jit(solution)/shard_map/ppermute | solution.py:415
  331.6 56.0 %collective-permute-start.10 = (bf16[4,2,64,1024]{3,2,1,0:T(8,128)(2,1)}, bf16[4,2,64,1024]{3,2,1,0:T(8,128)(2,1)}, u32[]{:S(2)}, u32[]{:S(2)}) collective-permute-start(bf16[4,2,64,1024]{3,2,1,0:T(8,128)(2,1)} %convolution_convert_fusion.4), channel_id=1, source_target_pairs={{0,2},{2,0},{4,6},{6,4},{8,10},{10,8},{12,14},{14,12},{16,18},{18,... | collective-permute-start | bytes 3145736 | tf_op jit(solution)/shard_map/ppermute | solution.py:428
  335.9 120.7 %collective-permute-start.16 = (bf16[4,2,64,4096]{3,2,1,0:T(8,128)(2,1)}, bf16[4,2,64,4096]{3,2,1,0:T(8,128)(2,1)}, u32[]{:S(2)}, u32[]{:S(2)}) collective-permute-start(bf16[4,2,64,4096]{3,2,1,0:T(8,128)(2,1)} %convolution_convert_fusion), channel_id=1, source_target_pairs={{0,2},{2,0},{4,6},{6,4},{8,10},{10,8},{12,14},{14,12},{16,18},{18,... | collective-permute-start | bytes 12582920 | tf_op jit(solution)/shard_map/ppermute | solution.py:428
  380.6 70.7 %collective-permute-start.4 = (bf16[4,2,64,3072]{3,2,1,0:T(8,128)(2,1)}, bf16[4,2,64,3072]{3,2,1,0:T(8,128)(2,1)}, u32[]{:S(2)}, u32[]{:S(2)}) collective-permute-start(bf16[4,2,64,3072]{3,2,1,0:T(8,128)(2,1)} %convolution_convert_fusion.1), channel_id=1, source_target_pairs={{0,2},{2,0},{4,6},{6,4},{8,10},{10,8},{12,14},{14,12},{16,18},{18,... | collective-permute-start | bytes 9437192 | tf_op jit(solution)/shard_map/ppermute | solution.py:428
  391.4 38.9 %collective-permute-start.11 = (bf16[4,64,1024]{2,1,0:T(8,128)(2,1)}, bf16[4,64,1024]{2,1,0:T(8,128)(2,1)}, u32[]{:S(2)}, u32[]{:S(2)}) collective-permute-start(bf16[4,64,1024]{2,1,0:T(8,128)(2,1)} %fusion.67), channel_id=1, source_target_pairs={{0,4},{2,6},{4,0},{6,2},{8,12},{10,14},{12,8},{14,10},{16,20},{18,... | collective-permute-start | bytes 1572872 | tf_op jit(solution)/shard_map/ppermute | solution.py:433
  433.1 12.3 %collective-permute-start.13 = (bf16[64,1024]{1,0:T(8,128)(2,1)S(1)}, bf16[64,1024]{1,0:T(8,128)(2,1)S(1)}, u32[]{:S(2)}, u32[]{:S(2)}) collective-permute-start(bf16[64,1024]{1,0:T(8,128)(2,1)S(1)} %get-tuple-element.91), channel_id=1, source_target_pairs={{0,16},{2,18},{4,20},{6,22},{8,24},{10,26},{12,28},{14,30},{16,0},... | collective-permute-start | bytes 393224 | tf_op jit(solution)/shard_map/ppermute | solution.py:440
  433.7 11.7 %collective-permute-start.12 = (bf16[64,1024]{1,0:T(8,128)(2,1)S(1)}, bf16[64,1024]{1,0:T(8,128)(2,1)S(1)}, u32[]{:S(2)}, u32[]{:S(2)}) collective-permute-start(bf16[64,1024]{1,0:T(8,128)(2,1)S(1)} %get-tuple-element.89), channel_id=1, source_target_pairs={{0,8},{2,10},{4,12},{6,14},{8,16},{10,18},{12,20},{14,22},{16,24},... | collective-permute-start | bytes 393224 | tf_op jit(solution)/shard_map/ppermute | solution.py:440
  437.1 60.8 %collective-permute-start.22 = (bf16[4,2,256,1024]{3,2,1,0:T(8,128)(2,1)}, bf16[4,2,256,1024]{3,2,1,0:T(8,128)(2,1)S(1)}, u32[]{:S(2)}, u32[]{:S(2)}) collective-permute-start(bf16[4,2,256,1024]{3,2,1,0:T(8,128)(2,1)} %convolution_convert_fusion.2), channel_id=1, source_target_pairs={{0,2},{2,0},{4,6},{6,4},{8,10},{10,8},{12,14},{14,12},{16,18},{18,... | collective-permute-start | bytes 12582920 | tf_op jit(solution)/shard_map/ppermute | solution.py:428
  456.0 37.3 %collective-permute-start.5 = (bf16[4,64,3072]{2,1,0:T(8,128)(2,1)S(1)}, bf16[4,64,3072]{2,1,0:T(8,128)(2,1)S(1)}, u32[]{:S(2)}, u32[]{:S(2)}) collective-permute-start(bf16[4,64,3072]{2,1,0:T(8,128)(2,1)S(1)} %fusion.32), channel_id=1, source_target_pairs={{0,4},{2,6},{4,0},{6,2},{8,12},{10,14},{12,8},{14,10},{16,20},{18,... | collective-permute-start | bytes 4718600 | tf_op jit(solution)/shard_map/ppermute | solution.py:433
  461.8 76.5 %collective-permute-start.17 = (bf16[4,64,4096]{2,1,0:T(8,128)(2,1)S(1)}, bf16[4,64,4096]{2,1,0:T(8,128)(2,1)S(1)}, u32[]{:S(2)}, u32[]{:S(2)}) collective-permute-start(bf16[4,64,4096]{2,1,0:T(8,128)(2,1)S(1)} %fusion.23), channel_id=1, source_target_pairs={{0,4},{2,6},{4,0},{6,2},{8,12},{10,14},{12,8},{14,10},{16,20},{18,... | collective-permute-start | bytes 6291464 | tf_op jit(solution)/shard_map/ppermute | solution.py:433
  494.6 30.7 %collective-permute-start.7 = (bf16[64,3072]{1,0:T(8,128)(2,1)S(1)}, bf16[64,3072]{1,0:T(8,128)(2,1)S(1)}, u32[]{:S(2)}, u32[]{:S(2)}) collective-permute-start(bf16[64,3072]{1,0:T(8,128)(2,1)S(1)} %get-tuple-element.80), channel_id=1, source_target_pairs={{0,16},{2,18},{4,20},{6,22},{8,24},{10,26},{12,28},{14,30},{16,0},... | collective-permute-start | bytes 1179656 | tf_op jit(solution)/shard_map/ppermute | solution.py:440
  496.0 29.3 %collective-permute-start.6 = (bf16[64,3072]{1,0:T(8,128)(2,1)S(1)}, bf16[64,3072]{1,0:T(8,128)(2,1)S(1)}, u32[]{:S(2)}, u32[]{:S(2)}) collective-permute-start(bf16[64,3072]{1,0:T(8,128)(2,1)S(1)} %get-tuple-element.78), channel_id=1, source_target_pairs={{0,8},{2,10},{4,12},{6,14},{8,16},{10,18},{12,20},{14,22},{16,24},... | collective-permute-start | bytes 1179656 | tf_op jit(solution)/shard_map/ppermute | solution.py:440
  500.7 79.7 %collective-permute-start.23 = (bf16[4,256,1024]{2,1,0:T(8,128)(2,1)S(1)}, bf16[4,256,1024]{2,1,0:T(8,128)(2,1)S(1)}, u32[]{:S(2)}, u32[]{:S(2)}) collective-permute-start(bf16[4,256,1024]{2,1,0:T(8,128)(2,1)S(1)} %fusion.24), channel_id=1, source_target_pairs={{0,4},{2,6},{4,0},{6,2},{8,12},{10,14},{12,8},{14,10},{16,20},{18,... | collective-permute-start | bytes 6291464 | tf_op jit(solution)/shard_map/ppermute | solution.py:433
  525.5 61.6 %collective-permute-start.9 = (bf16[64,3072]{1,0:T(8,128)(2,1)S(1)}, bf16[64,3072]{1,0:T(8,128)(2,1)S(1)}, u32[]{:S(2)}, u32[]{:S(2)}) collective-permute-start(bf16[64,3072]{1,0:T(8,128)(2,1)S(1)} %fusion.66), channel_id=1, source_target_pairs={{0,1},{1,0},{2,3},{3,2},{4,5},{5,4},{6,7},{7,6},{8,9},{9,8},{10,11... | collective-permute-start | bytes 1179656 | tf_op jit(solution)/shard_map/ppermute | solution.py:415
  539.2 42.6 %collective-permute-start.20 = (bf16[64,4096]{1,0:T(8,128)(2,1)S(1)}, bf16[64,4096]{1,0:T(8,128)(2,1)S(1)}, u32[]{:S(2)}, u32[]{:S(2)}) collective-permute-start(bf16[64,4096]{1,0:T(8,128)(2,1)S(1)} %get-tuple-element.76), channel_id=1, source_target_pairs={{0,24},{2,26},{4,28},{6,30},{8,0},{10,2},{12,4},{14,6},{16,8},{18,... | collective-permute-start | bytes 1572872 | tf_op jit(solution)/shard_map/ppermute | solution.py:440
  539.8 44.1 %collective-permute-start.19 = (bf16[64,4096]{1,0:T(8,128)(2,1)S(1)}, bf16[64,4096]{1,0:T(8,128)(2,1)S(1)}, u32[]{:S(2)}, u32[]{:S(2)}) collective-permute-start(bf16[64,4096]{1,0:T(8,128)(2,1)S(1)} %get-tuple-element.77), channel_id=1, source_target_pairs={{0,16},{2,18},{4,20},{6,22},{8,24},{10,26},{12,28},{14,30},{16,0},... | collective-permute-start | bytes 1572872 | tf_op jit(solution)/shard_map/ppermute | solution.py:440
  541.1 44.7 %collective-permute-start.18 = (bf16[64,4096]{1,0:T(8,128)(2,1)S(1)}, bf16[64,4096]{1,0:T(8,128)(2,1)S(1)}, u32[]{:S(2)}, u32[]{:S(2)}) collective-permute-start(bf16[64,4096]{1,0:T(8,128)(2,1)S(1)} %get-tuple-element.75), channel_id=1, source_target_pairs={{0,8},{2,10},{4,12},{6,14},{8,16},{10,18},{12,20},{14,22},{16,24},... | collective-permute-start | bytes 1572872 | tf_op jit(solution)/shard_map/ppermute | solution.py:440
  581.8 12.5 %collective-permute-start.26 = (bf16[256,1024]{1,0:T(8,128)(2,1)S(1)}, bf16[256,1024]{1,0:T(8,128)(2,1)S(1)}, u32[]{:S(2)}, u32[]{:S(2)}) collective-permute-start(bf16[256,1024]{1,0:T(8,128)(2,1)S(1)} %get-tuple-element.71), channel_id=1, source_target_pairs={{0,24},{2,26},{4,28},{6,30},{8,0},{10,2},{12,4},{14,6},{16,8},{18,... | collective-permute-start | bytes 1572872 | tf_op jit(solution)/shard_map/ppermute | solution.py:440
  581.8 45.2 %collective-permute-start.25 = (bf16[256,1024]{1,0:T(8,128)(2,1)S(1)}, bf16[256,1024]{1,0:T(8,128)(2,1)S(1)}, u32[]{:S(2)}, u32[]{:S(2)}) collective-permute-start(bf16[256,1024]{1,0:T(8,128)(2,1)S(1)} %get-tuple-element.72), channel_id=1, source_target_pairs={{0,16},{2,18},{4,20},{6,22},{8,24},{10,26},{12,28},{14,30},{16,0},... | collective-permute-start | bytes 1572872 | tf_op jit(solution)/shard_map/ppermute | solution.py:440
  583.8 43.2 %collective-permute-start.24 = (bf16[256,1024]{1,0:T(8,128)(2,1)S(1)}, bf16[256,1024]{1,0:T(8,128)(2,1)S(1)}, u32[]{:S(2)}, u32[]{:S(2)}) collective-permute-start(bf16[256,1024]{1,0:T(8,128)(2,1)S(1)} %get-tuple-element.70), channel_id=1, source_target_pairs={{0,8},{2,10},{4,12},{6,14},{8,16},{10,18},{12,20},{14,22},{16,24},... | collective-permute-start | bytes 1572872 | tf_op jit(solution)/shard_map/ppermute | solution.py:440
  586.0 42.4 %collective-permute-start.21 = (bf16[64,4096]{1,0:T(8,128)(2,1)S(1)}, bf16[64,4096]{1,0:T(8,128)(2,1)S(1)}, u32[]{:S(2)}, u32[]{:S(2)}) collective-permute-start(bf16[64,4096]{1,0:T(8,128)(2,1)S(1)} %fusion.51), channel_id=1, source_target_pairs={{0,1},{1,0},{2,3},{3,2},{4,5},{5,4},{6,7},{7,6},{8,9},{9,8},{10,11... | collective-permute-start | bytes 1572872 | tf_op jit(solution)/shard_map/ppermute | solution.py:415
  (38 other events, 421.5 us)

commit v2 on v1

--- a/solution.py
+++ b/solution.py
@@ -415,49 +415,81 @@
     return lax.ppermute(value, "seq", [(i, (i + k) % s) for i in range(s)])
 
 
-def reduce_rows(make, mine_c, n, s):
-    A, B = grid_of(n)
-
-    def at(a, b, c):
-        return (a * B + b) * 2 + c
-
-    every = [(a, b, c) for a in range(A) for b in range(B) for c in range(2)]
-    me = lax.axis_index("fsdp")
-    a, b, c = me // (2 * B), (me // 2) % B, me % 2
-    away = make(1 - c).astype(bf16)
-    away = lax.ppermute(away, "fsdp", [(at(*p), at(p[0], p[1], 1 - p[2])) for p in every])
-    total = make(c) + away.astype(f32)
-    parts = []
-    for k in range(1, B):
-        send = lax.dynamic_index_in_dim(total, (b + k) % B, 1, keepdims=False).astype(bf16)
-        parts.append(lax.ppermute(send, "fsdp", [(at(*p), at(p[0], (p[1] + k) % B, p[2])) for p in every]))
-    total = lax.dynamic_index_in_dim(total, b, 1, keepdims=False)
-    for p in parts:
-        total = total + p.astype(f32)
-    parts = []
-    for k in range(1, A):
-        send = lax.dynamic_index_in_dim(total, (a + k) % A, 0, keepdims=False).astype(bf16)
-        parts.append(lax.ppermute(send, "fsdp", [(at(*p), at((p[0] + k) % A, p[1], p[2])) for p in every]))
-    total = lax.dynamic_index_in_dim(total, a, 0, keepdims=False)
-    for p in parts:
-        total = total + p.astype(f32)
-    if s != 2:
-        return lax.psum(total, "seq")
-    total = total.astype(bf16)
-    return total.astype(f32) + seq_shift(total, 1, 2).astype(f32)
-
-
-def weight_grad(lhs, rhs, n, s):
-    A, B = grid_of(n)
-    T, R = lhs.shape
-    r = R // n
-    split = lhs.reshape(T, A * B, 2, r)
-
-    def make(c):
-        rows = lax.dynamic_index_in_dim(split, c, 2, keepdims=False).reshape(T, A * B * r)
-        return tn(rows, rhs).reshape(A, B, r, rhs.shape[1])
-
-    return reduce_rows(make, None, n, s)
+def tie(*values):
+    return lax.optimization_barrier(values)
+
+
+class Exchange:
+    def __init__(self, grad, n, s):
+        A, B = grid_of(n)
+        self.A, self.B, self.s = A, B, s
+        self.grad = grad.reshape(A, B, 2, grad.shape[0] // n, grad.shape[1])
+        me = lax.axis_index("fsdp")
+        self.a, self.b, self.c = me // (2 * B), (me // 2) % B, me % 2
+
+    def shift(self, value, da, db, dc):
+        A, B = self.A, self.B
+
+        def at(a, b, c):
+            return (a * B + b) * 2 + c
+
+        pairs = [
+            (at(a, b, c), at((a + da) % A, (b + db) % B, (c + dc) % 2))
+            for a in range(A)
+            for b in range(B)
+            for c in range(2)
+        ]
+        return lax.ppermute(value, "fsdp", pairs)
+
+    def take(self, value, index, axis):
+        return lax.dynamic_index_in_dim(value, index, axis, keepdims=False)
+
+    def c_send(self):
+        self.out = [self.take(self.grad, 1 - self.c, 2)]
+        return self.out
+
+    def c_start(self, out):
+        self.into = self.shift(out[0], 0, 0, 1)
+
+    def b_sum(self, index):
+        mine = self.take(self.take(self.grad, self.c, 2), index, 1)
+        return mine.astype(f32) + self.take(self.into, index, 1).astype(f32)
+
+    def b_send(self):
+        return [self.b_sum((self.b + k) % self.B).astype(bf16) for k in range(1, self.B)]
+
+    def b_start(self, out):
+        self.from_b = [self.shift(v, 0, k + 1, 0) for k, v in enumerate(out)]
+
+    def a_send(self):
+        total = self.b_sum(self.b)
+        for v in self.from_b:
+            total = total + v.astype(f32)
+        self.total = total
+        return [self.take(total, (self.a + k) % self.A, 0).astype(bf16) for k in range(1, self.A)]
+
+    def a_start(self, out):
+        self.from_a = [self.shift(v, k + 1, 0, 0) for k, v in enumerate(out)]
+
+    def x_send(self):
+        total = self.take(self.total, self.a, 0)
+        for v in self.from_a:
+            total = total + v.astype(f32)
+        if self.s != 2:
+            self.total = lax.psum(total, "seq")
+            return []
+        self.total = total.astype(bf16)
+        return [self.total]
+
+    def x_start(self, out):
+        if self.s == 2:
+            self.from_x = seq_shift(out[0], 1, 2)
+            self.total = out[0]
+
+    def result(self):
+        if self.s != 2:
+            return self.total
+        return self.total.astype(f32) + self.from_x.astype(f32)
 
 
 def layer_norm(values):
@@ -524,40 +556,102 @@
     pre_act = nn(hidden_two, fc1_w) + fc1_b
     act_f, gelu_back = jax.vjp(partial(jax.nn.gelu, approximate=True), pre_act)
     act_b = act_f.astype(bf16)
-    mlp_out = nn(act_b, fc2_w) + fc2_b
-    result = (middle + gate_two * mlp_out).astype(bf16)
-
-    d_gate_two = jnp.sum(grad_out * mlp_out, axis=0, keepdims=True)
     d_mlp = (grad_out * gate_two).astype(bf16)
-    total_fc2 = weight_grad(act_b, d_mlp, n, s)
+    half_d, half_f = width // 2, fc1_w.shape[1] // 2
+
+    def exchange(lhs, rhs):
+        return Exchange(tn(lhs, rhs).astype(bf16), n, s)
+
+    fc2a, fc2b = exchange(act_b, d_mlp[:, :half_d]), exchange(act_b, d_mlp[:, half_d:])
+    d_mlp, sa, sb = tie(d_mlp, fc2a.c_send(), fc2b.c_send())
+    fc2a.c_start(sa)
+    fc2b.c_start(sb)
     bias_fc2 = jnp.sum(d_mlp, axis=0, dtype=f32)
-    d_act = nt(d_mlp, fc2_w)
-    d_pre = gelu_back(d_act)[0].astype(bf16)
-    total_fc1 = weight_grad(hidden_two, d_pre, n, s)
+    d_pre = gelu_back(nt(d_mlp, fc2_w))[0].astype(bf16)
+    d_pre, sa, sb = tie(d_pre, fc2a.b_send(), fc2b.b_send())
+    fc2a.b_start(sa)
+    fc2b.b_start(sb)
+    fc1a, fc1b = exchange(hidden_two, d_pre[:, :half_f]), exchange(hidden_two, d_pre[:, half_f:])
     bias_fc1 = jnp.sum(d_pre, axis=0, dtype=f32)
+    d_pre, sa, sb = tie(d_pre, fc1a.c_send(), fc1b.c_send())
+    fc1a.c_start(sa)
+    fc1b.c_start(sb)
     d_hidden_two = nt(d_pre, fc1_w)
     d_shift_two = jnp.sum(d_hidden_two, axis=0, keepdims=True)
     d_scale_two = jnp.sum(d_hidden_two * normed_two, axis=0, keepdims=True)
     d_middle = grad_out + norm_back(d_hidden_two * (1.0 + scale_two), normed_two, rscale_two)
-
     d_gate_one = jnp.sum(d_middle * branch, axis=0, keepdims=True)
     d_branch = (d_middle * gate_one).astype(bf16)
-    total_proj = weight_grad(attn, d_branch, n, s)
+    d_branch, sa, sb, sc = tie(d_branch, fc1a.b_send(), fc1b.b_send(), fc2a.a_send())
+    fc1a.b_start(sa)
+    fc1b.b_start(sb)
+    fc2a.a_start(sc)
+    proj = exchange(attn, d_branch)
     bias_proj = jnp.sum(d_branch, axis=0, dtype=f32)
     d_attn = nt(d_branch, proj_w).astype(bf16)
-    grad_q, dks, dvs = attend_backward(queries, d_attn, lse, ks, vs)
-    grad_k, grad_v = dks[0], dvs[0]
-    for k in range(1, s):
-        grad_k = grad_k + seq_shift(dks[k], s - k, s).astype(f32)
-        grad_v = grad_v + seq_shift(dvs[k], s - k, s).astype(f32)
-    d_qkv = jnp.concatenate([grad_q, grad_k.astype(bf16), grad_v.astype(bf16)], axis=1)
-    total_qkv = weight_grad(hidden_one, d_qkv, n, s)
-    column_sums = jnp.sum(d_qkv, axis=0, dtype=f32)
-    bias_qv = jnp.concatenate([column_sums[:width], column_sums[2 * width :]])
+    d_attn, sa = tie(d_attn, proj.c_send())
+    proj.c_start(sa)
+    halves = []
+    lo = slice(0, half_d)
+    hi = slice(half_d, width)
+
+    def attention(part):
+        heads = slice(part.start // 128, part.stop // 128)
+        grads = attend_backward(
+            queries[:, part], d_attn[:, part], lse[heads], [k[:, part] for k in ks], [v[:, part] for v in vs]
+        )
+        return grads
+
+    def back(dk):
+        return [seq_shift(dk[k], s - k, s) for k in range(1, s)]
+
+    q1, dk1, dv1 = attention(lo)
+    q1, dk1, dv1, sa, sb = tie(q1, dk1, dv1, proj.b_send(), fc2b.a_send())
+    rk1, rv1 = back(dk1), back(dv1)
+    proj.b_start(sa)
+    fc2b.a_start(sb)
+    d_attn, q1 = tie(d_attn, q1)
+    q2, dk2, dv2 = attention(hi)
+    q2, dk2, dv2, sa, sb = tie(q2, dk2, dv2, fc1a.a_send(), fc2a.x_send())
+    rk2, rv2 = back(dk2), back(dv2)
+    fc1a.a_start(sa)
+    fc2a.x_start(sb)
+
+    def joined(q, dk, rk, dv, rv):
+        gk, gv = dk[0], dv[0]
+        for v in rk:
+            gk = gk + v.astype(f32)
+        for v in rv:
+            gv = gv + v.astype(f32)
+        return jnp.concatenate([q, gk.astype(bf16), gv.astype(bf16)], axis=1)
+
+    d1 = joined(q1, dk1, rk1, dv1, rv1)
+    qkv1 = exchange(hidden_one, d1)
+    act_b, sa = tie(act_b, qkv1.c_send())
+    qkv1.c_start(sa)
+    mlp_out = nn(act_b, fc2_w) + fc2_b
+    result = (middle + gate_two * mlp_out).astype(bf16)
+    d_gate_two = jnp.sum(grad_out * mlp_out, axis=0, keepdims=True)
+    d_gate_two, sa, sb, sc = tie(d_gate_two, qkv1.b_send(), fc1b.a_send(), fc2b.x_send())
+    qkv1.b_start(sa)
+    fc1b.a_start(sb)
+    fc2b.x_start(sc)
+    d2 = joined(q2, dk2, rk2, dv2, rv2)
+    hidden_one_, d_gate_two = tie(hidden_one, d_gate_two)
+    qkv2 = exchange(hidden_one_, d2)
+    d2, sa = tie(d2, qkv2.c_send())
+    qkv2.c_start(sa)
+    sums1, sums2 = jnp.sum(d1, axis=0, dtype=f32), jnp.sum(d2, axis=0, dtype=f32)
+    bias_qv = jnp.concatenate([sums1[:half_d], sums2[:half_d], sums1[width:], sums2[width:]])
+    d_qkv = jnp.concatenate([v[:, i * half_d : (i + 1) * half_d] for i in range(3) for v in (d1, d2)], axis=1)
     d_hidden_one = nt(d_qkv, qkv_w)
     d_shift_one = jnp.sum(d_hidden_one, axis=0, keepdims=True)
     d_scale_one = jnp.sum(d_hidden_one * normed_one, axis=0, keepdims=True)
     grad_input = d_middle + norm_back(d_hidden_one * (1.0 + scale_one), normed_one, rscale_one)
+    d_scale_one, sa, sb, sc = tie(d_scale_one, qkv2.b_send(), proj.a_send(), fc1a.x_send())
+    qkv2.b_start(sa)
+    proj.a_start(sb)
+    fc1a.x_start(sc)
 
     d_part = jnp.concatenate(
         [d_shift_one, d_scale_one, d_gate_one, d_shift_two, d_scale_two, d_gate_two], axis=-1
@@ -569,6 +663,18 @@
     share = b_ada.shape[0]
     total_bada = lax.dynamic_slice_in_dim(sums_ada[0], lax.axis_index("fsdp") * share, share)
     grad_condition = silu_back(d_lifted.reshape(1, width))[0]
+    total_bias, sa, sb, sc = tie(total_bias, qkv1.a_send(), fc1b.x_send(), proj.x_send())
+    qkv1.a_start(sa)
+    fc1b.x_start(sb)
+    proj.x_start(sc)
+    qkv2.a_start(qkv2.a_send())
+    qkv1.x_start(qkv1.x_send())
+    qkv2.x_start(qkv2.x_send())
+    total_fc2 = jnp.concatenate([fc2a.result(), fc2b.result()], axis=1)
+    total_fc1 = jnp.concatenate([fc1a.result(), fc1b.result()], axis=1)
+    total_proj = proj.result()
+    r1, r2 = qkv1.result(), qkv2.result()
+    total_qkv = jnp.concatenate([v[:, i * half_d : (i + 1) * half_d] for i in range(3) for v in (r1, r2)], axis=1)
     total_bqv, total_bproj, total_bfc1, total_bfc2 = [total_bias[0, edges[i] : edges[i + 1]] for i in range(4)]
     return (
         result[None],

time: 647 us -> 624 us (0.964)
  waiting for transfers between devices: 200 us -> 141 us
  starting transfers between devices: 27.1 us -> 63.6 us
  other arithmetic: 23 us -> 58.8 us
  matrix products: 103 us -> 78.9 us
  local copies, waits for them, and re-layouts: 59.5 us -> 47.7 us
    ppermute x20 -> x35, waiting for transfers between devices: 153 us -> 63.9 us  [shift(): return lax.ppermute(value, 'fsdp', pairs)]
    ppermute x20 -> x35, starting transfers between devices: 18.6 us -> 50.2 us  [shift(): return lax.ppermute(value, 'fsdp', pairs)]
    ppermute x8 -> x13, waiting for transfers between devices: 47.7 us -> 77.3 us  [seq_shift(): return lax.ppermute(value, 'seq', [(i, (i + k) % s) for i in range(s)])]
    convert_element_type x7 -> x20, other arithmetic: 5.78 us -> 24.7 us  [the longest x7 16.6 us: b_send(): self.b_sum((self.b + k) % self.B).astype(bf16)]
    dot_general x8 -> x7, matrix products: 30.8 us -> 15.1 us  [tn(): lax.dot_general(a, b, (((0,), (0,)), ((), ())), preferred_element_type=f32)]
    unnamed x76 -> x154, local copies, waits for them, and re-layouts: 22.5 us -> 11.3 us
    slice x1 -> x9, local copies, waits for them, and re-layouts: 0.01 us -> 10.7 us  [the longest x2 5.11 us: attention(): v[:, part]]
    dot_general x6, matrix products: 43.2 us -> 33.4 us  [nn(): lax.dot_general(a, b, (((1,), (0,)), ((), ())), preferred_element_type=f32)]
  transfers between devices with their start and end apart: 28 -> 48, of which waited for: 13 -> 17; matrix products, arithmetic and copies ran while one was open for 16% -> 20% of each run, Pallas kernels for 5% -> 9%
where the time goes in v2:
time: 624 us; the launch traced here: 616 us
  Pallas kernels  224 us (36%)
  waiting for transfers between devices  141 us (23%)
  matrix products  78.9 us (13%)
  starting transfers between devices  63.6 us (10%)
  other arithmetic  58.8 us (9%)
  local copies, waits for them, and re-layouts  47.7 us (8%)
    pallas_call x1, Pallas kernels, gather_weights(): pl.pallas_call(kern, out_shape=[jax.ShapeDtypeStruct((A, B, 2) + w.shape,...  128 us
    ppermute x13, waiting for transfers between devices, seq_shift(): return lax.ppermute(value, 'seq', [(i, (i + k) % s) for i in range(s)])  77.3 us
    ppermute x35, waiting for transfers between devices, shift(): return lax.ppermute(value, 'fsdp', pairs)  63.9 us
    ppermute x35, starting transfers between devices, shift(): return lax.ppermute(value, 'fsdp', pairs)  50.2 us
    dot_general x6, matrix products, nn(): lax.dot_general(a, b, (((1,), (0,)), ((), ())), preferred_element_type=f32)  33.4 us
    pallas_call x2, Pallas kernels, attend_backward(): pl.pallas_call(partial(attend_backward_kernel, n), grid=(D // 128,), in_s...  32.5 us
    dot_general x4, matrix products, nt(): lax.dot_general(a, b, (((1,), (1,)), ((), ())), preferred_element_type=f32)  30.5 us
    pallas_call x1, Pallas kernels, modulation_backward(): pl.pallas_call(kern, out_shape=[jax.ShapeDtypeStruct((rows, E), f32), jax...  25 us
  transfers between devices with their start and end apart: 48, of which 17 were waited for; matrix products, arithmetic and copies ran while one was open for 20% of the time, Pallas kernels for 9%

profile of v2, /device:TPU:0, one launch (start us, length us, event | category | flops | bytes accessed | tf_op | source)
XLA Modules:
  0.0 616.5 jit_solution(9986134164598423296)
XLA Ops:
  7.9 20.6 %modulation_forward.1 = (f32[1,6144]{1,0:T(1,128)}, f32[16,1,64]{2,1,0:T(1,128)}, f32[16,1,896]{2,1,0:T(1,128)}) custom-call(f32[16,1,64]{2,1,0:T(1,128)} %reshape.351.l_ref, bf16[64,6144]{1,0:T(8,128)(2,1)} %w_ref.3, f32[1,896]{1,0:T(1,128)} %convert_element_type.588.bias_ref), custom_call_target="tpu_custom_call" | custom-call | tf_op jit(solution)/shard_map/modulation_forward/pallas_call | solution.py:194
  31.1 127.8 %gather_weights.1 = (bf16[4,2,2,64,3072]{4,3,2,1,0:T(8,128)(2,1)}, bf16[4,2,2,64,1024]{4,3,2,1,0:T(8,128)(2,1)}, bf16[4,2,2,64,4096]{4,3,2,1,0:T(8,128)(2,1)}, bf16[4,2,2,256,1024]{4,3,2,1,0:T(8,128)(2,1)}) custom-call(bf16[64,3072]{1,0:T(8,128)(2,1)} %refs_0_.1, bf16[64,1024]{1,0:T(8,128)(2,1)} %refs_1_.1, bf16[64,4096]{1,0:T(8,128)(2,1)} %refs_2_.1, ...), custom_call_target="tpu_custom_call" | custom-call | tf_op jit(solution)/shard_map/gather_weights/pallas_call | solution.py:131
  178.6 10.5 %collective-permute-done.refs_1_ = bf16[512,1024]{1,0:T(8,128)(2,1)S(1)} collective-permute-done((bf16[512,1024]{1,0:T(8,128)(2,1)}, bf16[512,1024]{1,0:T(8,128)(2,1)S(1)}, u32[]{:S(2)}, u32[]{:S(2)}) %collective-permute-start) | collective-permute-done | bytes 1048608 | tf_op jit(solution)/shard_map/ppermute | solution.py:415
  189.0 22.0 %collective-permute-done.1.refs_3_ = bf16[512,1024]{1,0:T(8,128)(2,1)} collective-permute-done((bf16[512,1024]{1,0:T(8,128)(2,1)}, bf16[512,1024]{1,0:T(8,128)(2,1)}, u32[]{:S(2)}, u32[]{:S(2)}) %collective-permute-start.1) | collective-permute-done | bytes 1048608 | tf_op jit(solution)/shard_map/ppermute | solution.py:415
  211.0 18.3 %attend_forward.1 = (bf16[512,1024]{1,0:T(8,128)(2,1)}, f32[8,2,512]{2,1,0:T(2,128)}) custom-call(bf16[512,1024]{1,0:T(8,128)(2,1)} %copy-done.36, bf16[512,1024]{1,0:T(8,128)(2,1)} %fusion.50.refs_0_, bf16[512,1024]{1,0:T(8,128)(2,1)} %copy-done.29, bf16[512,1024]{1,0:T(8,128)(2,1)} %add_convert_fusion.2.refs_2_, ...), custom_call_target="tpu_custom_call" | custom-call | flops 8589934592 | bytes 6291456 | tf_op jit(solution)/shard_map/attend_forward/pallas_call | solution.py:350
  234.4 9.1 %multiply_convert_fusion = (bf16[512,4096]{1,0:T(8,128)(2,1)S(1)}, f32[512,4096]{1,0:T(8,128)}) fusion(f32[4096]{0:T(1024)S(1)} %bitcast.379, bf16[1024,4096]{1,0:T(8,128)(2,1)S(1)} %bitcast.400, f32[512,1024]{1,0:T(8,128)S(1)} %get-tuple-element.194, f32[1024]{0:T(1024)S(1)} %bitcast.381, f32[1024]{0:T(1024)S(1)} %bitcast.372, f32[512]{0:T(512)S(1)} %add_rsqrt_fusion, ...), kind=kOutput, calls=%fused_computation.10 | convolution fusion | flops 4318560256 | bytes 23097344 | tf_op jit(solution)/shard_map/dot_general | solution.py:27
  258.3 12.9 %fusion.6 = bf16[512,4096]{1,0:T(8,128)(2,1)S(1)} fusion(f32[512,4096]{1,0:T(8,128)} %get-tuple-element.248, f32[4096]{0:T(1024)S(1)} %bitcast.380, bf16[512,1024]{1,0:T(8,128)(2,1)S(1)} %copy-done.10, bf16[4096,1024]{1,0:T(8,128)(2,1)} %bitcast.395), kind=kOutput, calls=%fused_computation.8 | convolution fusion | flops 4339007488 | bytes 22036480 | tf_op jit(solution)/shard_map/dot_general | solution.py:23
  289.1 10.2 %multiply_reduce_fusion = (f32[1024]{0:T(1024)}, f32[512]{0:T(512)S(1)}, f32[512]{0:T(512)S(1)}, f32[1024]{0:T(1024)}, f32[512,1024]{1,0:T(8,128)}) fusion(f32[512,1024]{1,0:T(8,128)S(1)} %get-tuple-element.194, f32[512]{0:T(512)S(1)} %add_rsqrt_fusion, f32[512]{0:T(512)S(1)} %broadcast_multiply_fusion.4, f32[1024]{0:T(1024)S(1)} %bitcast.375, ...), kind=kOutput, calls=%fused_computation.71 | convolution fusion | flops 4299682816 | bytes 16797696 | tf_op jit(solution)/shard_map/dot_general | solution.py:23
  313.9 17.8 %collective-permute-done.8 = bf16[4,256,512]{2,1,0:T(8,128)(2,1)S(1)} collective-permute-done((bf16[4,256,512]{2,1,0:T(8,128)(2,1)}, bf16[4,256,512]{2,1,0:T(8,128)(2,1)S(1)}, u32[]{:S(2)}, u32[]{:S(2)}) %collective-permute-start.8) | collective-permute-done | bytes 1048608 | tf_op jit(solution)/shard_map/ppermute | solution.py:442
  343.4 8.6 %collective-permute-start.12 = (bf16[256,512]{1,0:T(8,128)(2,1)}, bf16[256,512]{1,0:T(8,128)(2,1)}, u32[]{:S(2)}, u32[]{:S(2)}) collective-permute-start(bf16[256,512]{1,0:T(8,128)(2,1)} %get-tuple-element.136), channel_id=1, source_target_pairs={{0,8},{2,10},{4,12},{6,14},{8,16},{10,18},{12,20},{14,22},{16,24},... | collective-permute-start | bytes 786440 | tf_op jit(solution)/shard_map/ppermute | solution.py:442
  357.5 16.0 %attend_backward.2 = (bf16[512,512]{1,0:T(8,128)(2,1)}, f32[512,512]{1,0:T(8,128)}, bf16[512,512]{1,0:T(8,128)(2,1)}, f32[512,512]{1,0:T(8,128)}, bf16[512,512]{1,0:T(8,128)(2,1)}) custom-call(bf16[512,512]{1,0:T(8,128)(2,1)} %get-tuple-element.229.q_ref, bf16[512,512]{1,0:T(8,128)(2,1)} %slice.189.e_ref, f32[4,2,512]{2,1,0:T(2,128)} %get-tuple-element.231.lse_ref, ...), custom_call_target="tpu_custom_call" | custom-call | flops 8053063680 | bytes 6291456 | tf_op jit(solution)/shard_map/attend_backward/pallas_call | solution.py:402
  388.8 16.4 %attend_backward.3 = (bf16[512,512]{1,0:T(8,128)(2,1)}, f32[512,512]{1,0:T(8,128)}, bf16[512,512]{1,0:T(8,128)(2,1)}, f32[512,512]{1,0:T(8,128)}, bf16[512,512]{1,0:T(8,128)(2,1)}) custom-call(bf16[512,512]{1,0:T(8,128)(2,1)} %get-tuple-element.228.q_ref, bf16[512,512]{1,0:T(8,128)(2,1)} %slice.197.e_ref, f32[4,2,512]{2,1,0:T(2,128)} %get-tuple-element.230.lse_ref, ...), custom_call_target="tpu_custom_call" | custom-call | flops 8053063680 | bytes 6291456 | tf_op jit(solution)/shard_map/attend_backward/pallas_call | solution.py:402
  416.6 9.7 %collective-permute-done.25 = bf16[64,2048]{1,0:T(8,128)(2,1)S(1)} collective-permute-done((bf16[64,2048]{1,0:T(8,128)(2,1)}, bf16[64,2048]{1,0:T(8,128)(2,1)S(1)}, u32[]{:S(2)}, u32[]{:S(2)}) %collective-permute-start.25) | collective-permute-done | bytes 262176 | tf_op jit(solution)/shard_map/ppermute | solution.py:442
  429.5 16.2 %collective-permute-done.46 = bf16[256,512]{1,0:T(8,128)(2,1)S(1)} collective-permute-done((bf16[256,512]{1,0:T(8,128)(2,1)}, bf16[256,512]{1,0:T(8,128)(2,1)S(1)}, u32[]{:S(2)}, u32[]{:S(2)}) %collective-permute-start.46) | collective-permute-done | bytes 262176 | tf_op jit(solution)/shard_map/ppermute | solution.py:415
  452.3 8.2 %collective-permute-done.10 = bf16[512,512]{1,0:T(8,128)(2,1)S(1)} collective-permute-done((bf16[512,512]{1,0:T(8,128)(2,1)S(1)}, bf16[512,512]{1,0:T(8,128)(2,1)S(1)}, u32[]{:S(2)}, u32[]{:S(2)}) %collective-permute-start.10) | collective-permute-done | bytes 524320 | tf_op jit(solution)/shard_map/ppermute | solution.py:415
  465.3 6.4 %collective-permute-done.15 = bf16[512,512]{1,0:T(8,128)(2,1)S(1)} collective-permute-done((bf16[512,512]{1,0:T(8,128)(2,1)S(1)}, bf16[512,512]{1,0:T(8,128)(2,1)S(1)}, u32[]{:S(2)}, u32[]{:S(2)}) %collective-permute-start.15) | collective-permute-done | bytes 524320 | tf_op jit(solution)/shard_map/ppermute | solution.py:415
  471.9 9.2 %collective-permute-done.16 = bf16[512,512]{1,0:T(8,128)(2,1)S(1)} collective-permute-done((bf16[512,512]{1,0:T(8,128)(2,1)S(1)}, bf16[512,512]{1,0:T(8,128)(2,1)S(1)}, u32[]{:S(2)}, u32[]{:S(2)}) %collective-permute-start.16) | collective-permute-done | bytes 524320 | tf_op jit(solution)/shard_map/ppermute | solution.py:415
  483.1 9.1 %fusion.25 = (f32[1024]{0:T(1024)S(1)}, bf16[1,512,1024]{2,1,0:T(8,128)(2,1)}) fusion(bf16[1,512,1024]{2,1,0:T(8,128)(2,1)S(1)} %copy-done.7, f32[1024]{0:T(1024)S(1)} %copy-done.56, f32[512,1024]{1,0:T(8,128)S(1)} %copy-done.2, f32[1024]{0:T(1024)S(1)} %bitcast.369, bf16[512,4096]{1,0:T(8,128)(2,1)S(1)} %copy-done.66, bf16[4096,1024]{1,0:T(8,128)(2,1)} %bitcast.396), kind=kOutput, calls=%fused_computation.42 | convolution fusion | flops 4298636288 | bytes 16789504 | tf_op jit(solution)/shard_map/dot_general | solution.py:27
  492.4 6.9 %collective-permute-start.28 = (bf16[64,2048]{1,0:T(8,128)(2,1)S(1)}, bf16[64,2048]{1,0:T(8,128)(2,1)S(1)}, u32[]{:S(2)}, u32[]{:S(2)}) collective-permute-start(bf16[64,2048]{1,0:T(8,128)(2,1)S(1)} %get-tuple-element.165), channel_id=1, source_target_pairs={{0,8},{2,10},{4,12},{6,14},{8,16},{10,18},{12,20},{14,22},{16,24},... | collective-permute-start | bytes 786440 | tf_op jit(solution)/shard_map/ppermute | solution.py:442
  508.8 6.1 fusion.22
  533.5 25.0 %modulation_backward.1 = (f32[64,6144]{1,0:T(8,128)}, f32[1,6144]{1,0:T(1,128)}, f32[16,1,64]{2,1,0:T(1,128)}, f32[1,512]{1,0:T(1,128)}) custom-call(f32[1,6144]{1,0:T(1,128)} %constant_dynamic-update-slice_fusion.3.d_ref, f32[16,1,512]{2,1,0:T(1,128)} %broadcast_in_dim.44.bp_ref, f32[16,1,64]{2,1,0:T(1,128)} %get-tuple-element.159.lf_ref, ...), custom_call_target="tpu_custom_call" | custom-call | tf_op jit(solution)/shard_map/modulation_backward/pallas_call | solution.py:283
  577.0 7.1 %collective-permute-done.35 = bf16[64,1536]{1,0:T(8,128)(2,1)S(1)} collective-permute-done((bf16[64,1536]{1,0:T(8,128)(2,1)}, bf16[64,1536]{1,0:T(8,128)(2,1)S(1)}, u32[]{:S(2)}, u32[]{:S(2)}) %collective-permute-start.35) | collective-permute-done | bytes 196640 | tf_op jit(solution)/shard_map/ppermute | solution.py:442
  601.4 7.0 %collective-permute-done.40 = bf16[64,1536]{1,0:T(8,128)(2,1)S(1)} collective-permute-done((bf16[64,1536]{1,0:T(8,128)(2,1)S(1)}, bf16[64,1536]{1,0:T(8,128)(2,1)S(1)}, u32[]{:S(2)}, u32[]{:S(2)}) %collective-permute-start.40) | collective-permute-done | bytes 196640 | tf_op jit(solution)/shard_map/ppermute | solution.py:442
  609.8 4.9 collective-permute-done.42
  (361 shorter events, 208.6 us)
Async XLA Ops:
  162.8 26.2 %collective-permute-start = (bf16[512,1024]{1,0:T(8,128)(2,1)}, bf16[512,1024]{1,0:T(8,128)(2,1)S(1)}, u32[]{:S(2)}, u32[]{:S(2)}) collective-permute-start(bf16[512,1024]{1,0:T(8,128)(2,1)} %fusion.50.refs_0_), channel_id=1, source_target_pairs={{0,1},{1,0},{2,3},{3,2},{4,5},{5,4},{6,7},{7,6},{8,9},{9,8},{10,11... | collective-permute-start | bytes 3145736 | tf_op jit(solution)/shard_map/ppermute | solution.py:415
  167.7 43.3 %collective-permute-start.1 = (bf16[512,1024]{1,0:T(8,128)(2,1)}, bf16[512,1024]{1,0:T(8,128)(2,1)}, u32[]{:S(2)}, u32[]{:S(2)}) collective-permute-start(bf16[512,1024]{1,0:T(8,128)(2,1)} %add_convert_fusion.2.refs_2_), channel_id=1, source_target_pairs={{0,1},{1,0},{2,3},{3,2},{4,5},{5,4},{6,7},{7,6},{8,9},{9,8},{10,11... | collective-permute-start | bytes 3145736 | tf_op jit(solution)/shard_map/ppermute | solution.py:415
  283.9 26.4 %collective-permute-start.6 = (bf16[4,256,512]{2,1,0:T(8,128)(2,1)}, bf16[4,256,512]{2,1,0:T(8,128)(2,1)}, u32[]{:S(2)}, u32[]{:S(2)}) collective-permute-start(bf16[4,256,512]{2,1,0:T(8,128)(2,1)} %fusion.39), channel_id=1, source_target_pairs={{0,4},{2,6},{4,0},{6,2},{8,12},{10,14},{12,8},{14,10},{16,20},{18,... | collective-permute-start | bytes 3145736 | tf_op jit(solution)/shard_map/ppermute | solution.py:442
  289.1 45.3 %collective-permute-start.4 = (bf16[4,2,64,2048]{3,2,0,1:T(8,128)(2,1)}, bf16[4,2,64,2048]{3,2,0,1:T(8,128)(2,1)}, u32[]{:S(2)}, u32[]{:S(2)}) collective-permute-start(bf16[4,2,64,2048]{3,2,0,1:T(8,128)(2,1)} %bitcast.341), channel_id=1, source_target_pairs={{0,2},{2,0},{4,6},{6,4},{8,10},{10,8},{12,14},{14,12},{16,18},{18,... | collective-permute-start | bytes 6291464 | tf_op jit(solution)/shard_map/ppermute | solution.py:442
  299.3 32.5 %collective-permute-start.8 = (bf16[4,256,512]{2,1,0:T(8,128)(2,1)}, bf16[4,256,512]{2,1,0:T(8,128)(2,1)S(1)}, u32[]{:S(2)}, u32[]{:S(2)}) collective-permute-start(bf16[4,256,512]{2,1,0:T(8,128)(2,1)} %fusion.38), channel_id=1, source_target_pairs={{0,4},{2,6},{4,0},{6,2},{8,12},{10,14},{12,8},{14,10},{16,20},{18,... | collective-permute-start | bytes 3145736 | tf_op jit(solution)/shard_map/ppermute | solution.py:442
  300.4 36.9 %collective-permute-start.5 = (bf16[4,2,64,2048]{3,2,0,1:T(8,128)(2,1)}, bf16[4,2,64,2048]{3,2,0,1:T(8,128)(2,1)S(1)}, u32[]{:S(2)}, u32[]{:S(2)}) collective-permute-start(bf16[4,2,64,2048]{3,2,0,1:T(8,128)(2,1)} %bitcast.363), channel_id=1, source_target_pairs={{0,2},{2,0},{4,6},{6,4},{8,10},{10,8},{12,14},{14,12},{16,18},{18,... | collective-permute-start | bytes 6291464 | tf_op jit(solution)/shard_map/ppermute | solution.py:442
  343.4 32.2 %collective-permute-start.12 = (bf16[256,512]{1,0:T(8,128)(2,1)}, bf16[256,512]{1,0:T(8,128)(2,1)}, u32[]{:S(2)}, u32[]{:S(2)}) collective-permute-start(bf16[256,512]{1,0:T(8,128)(2,1)} %get-tuple-element.136), channel_id=1, source_target_pairs={{0,8},{2,10},{4,12},{6,14},{8,16},{10,18},{12,20},{14,22},{16,24},... | collective-permute-start | bytes 786440 | tf_op jit(solution)/shard_map/ppermute | solution.py:442
  352.0 24.5 %collective-permute-start.13 = (bf16[256,512]{1,0:T(8,128)(2,1)}, bf16[256,512]{1,0:T(8,128)(2,1)}, u32[]{:S(2)}, u32[]{:S(2)}) collective-permute-start(bf16[256,512]{1,0:T(8,128)(2,1)} %get-tuple-element.137), channel_id=1, source_target_pairs={{0,16},{2,18},{4,20},{6,22},{8,24},{10,26},{12,28},{14,30},{16,0},... | collective-permute-start | bytes 786440 | tf_op jit(solution)/shard_map/ppermute | solution.py:442
  352.0 24.5 %collective-permute-start.14 = (bf16[256,512]{1,0:T(8,128)(2,1)S(1)}, bf16[256,512]{1,0:T(8,128)(2,1)}, u32[]{:S(2)}, u32[]{:S(2)}) collective-permute-start(bf16[256,512]{1,0:T(8,128)(2,1)S(1)} %get-tuple-element.138), channel_id=1, source_target_pairs={{0,24},{2,26},{4,28},{6,30},{8,0},{10,2},{12,4},{14,6},{16,8},{18,... | collective-permute-start | bytes 786440 | tf_op jit(solution)/shard_map/ppermute | solution.py:442
  356.4 27.8 %collective-permute-start.11 = (bf16[4,64,2048]{2,1,0:T(8,128)(2,1)}, bf16[4,64,2048]{2,1,0:T(8,128)(2,1)}, u32[]{:S(2)}, u32[]{:S(2)}) collective-permute-start(bf16[4,64,2048]{2,1,0:T(8,128)(2,1)} %fusion.37), channel_id=1, source_target_pairs={{0,4},{2,6},{4,0},{6,2},{8,12},{10,14},{12,8},{14,10},{16,20},{18,... | collective-permute-start | bytes 3145736 | tf_op jit(solution)/shard_map/ppermute | solution.py:442
  375.6 31.6 %collective-permute-start.18 = (bf16[4,64,2048]{2,1,0:T(8,128)(2,1)}, bf16[4,64,2048]{2,1,0:T(8,128)(2,1)}, u32[]{:S(2)}, u32[]{:S(2)}) collective-permute-start(bf16[4,64,2048]{2,1,0:T(8,128)(2,1)} %fusion.36), channel_id=1, source_target_pairs={{0,4},{2,6},{4,0},{6,2},{8,12},{10,14},{12,8},{14,10},{16,20},{18,... | collective-permute-start | bytes 3145736 | tf_op jit(solution)/shard_map/ppermute | solution.py:442
  381.7 66.0 %collective-permute-start.19 = (bf16[256,512]{1,0:T(8,128)(2,1)}, bf16[256,512]{1,0:T(8,128)(2,1)}, u32[]{:S(2)}, u32[]{:S(2)}) collective-permute-start(bf16[256,512]{1,0:T(8,128)(2,1)} %get-tuple-element.146), channel_id=1, source_target_pairs={{0,8},{2,10},{4,12},{6,14},{8,16},{10,18},{12,20},{14,22},{16,24},... | collective-permute-start | bytes 786440 | tf_op jit(solution)/shard_map/ppermute | solution.py:442
  381.7 67.0 %collective-permute-start.20 = (bf16[256,512]{1,0:T(8,128)(2,1)}, bf16[256,512]{1,0:T(8,128)(2,1)}, u32[]{:S(2)}, u32[]{:S(2)}) collective-permute-start(bf16[256,512]{1,0:T(8,128)(2,1)} %get-tuple-element.147), channel_id=1, source_target_pairs={{0,16},{2,18},{4,20},{6,22},{8,24},{10,26},{12,28},{14,30},{16,0},... | collective-permute-start | bytes 786440 | tf_op jit(solution)/shard_map/ppermute | solution.py:442
  416.6 33.3 %collective-permute-start.21 = (bf16[256,512]{1,0:T(8,128)(2,1)}, bf16[256,512]{1,0:T(8,128)(2,1)S(1)}, u32[]{:S(2)}, u32[]{:S(2)}) collective-permute-start(bf16[256,512]{1,0:T(8,128)(2,1)} %get-tuple-element.148), channel_id=1, source_target_pairs={{0,24},{2,26},{4,28},{6,30},{8,0},{10,2},{12,4},{14,6},{16,8},{18,... | collective-permute-start | bytes 786440 | tf_op jit(solution)/shard_map/ppermute | solution.py:442
  426.3 25.8 %collective-permute-start.9 = (bf16[512,512]{1,0:T(8,128)(2,1)S(1)}, bf16[512,512]{1,0:T(8,128)(2,1)S(1)}, u32[]{:S(2)}, u32[]{:S(2)}) collective-permute-start(bf16[512,512]{1,0:T(8,128)(2,1)S(1)} %copy-done.61), channel_id=1, source_target_pairs={{0,1},{1,0},{2,3},{3,2},{4,5},{5,4},{6,7},{7,6},{8,9},{9,8},{10,11... | collective-permute-start | bytes 1572872 | tf_op jit(solution)/shard_map/ppermute | solution.py:415
  448.7 23.0 %collective-permute-start.15 = (bf16[512,512]{1,0:T(8,128)(2,1)S(1)}, bf16[512,512]{1,0:T(8,128)(2,1)S(1)}, u32[]{:S(2)}, u32[]{:S(2)}) collective-permute-start(bf16[512,512]{1,0:T(8,128)(2,1)S(1)} %copy-done.63), channel_id=1, source_target_pairs={{0,1},{1,0},{2,3},{3,2},{4,5},{5,4},{6,7},{7,6},{8,9},{9,8},{10,11... | collective-permute-start | bytes 1572872 | tf_op jit(solution)/shard_map/ppermute | solution.py:415
  449.9 31.1 %collective-permute-start.16 = (bf16[512,512]{1,0:T(8,128)(2,1)S(1)}, bf16[512,512]{1,0:T(8,128)(2,1)S(1)}, u32[]{:S(2)}, u32[]{:S(2)}) collective-permute-start(bf16[512,512]{1,0:T(8,128)(2,1)S(1)} %copy-done.62), channel_id=1, source_target_pairs={{0,1},{1,0},{2,3},{3,2},{4,5},{5,4},{6,7},{7,6},{8,9},{9,8},{10,11... | collective-permute-start | bytes 1572872 | tf_op jit(solution)/shard_map/ppermute | solution.py:415
  465.3 27.0 %collective-permute-start.17 = (bf16[4,2,64,1536]{3,2,0,1:T(8,128)(2,1)S(1)}, bf16[4,2,64,1536]{3,2,0,1:T(8,128)(2,1)S(1)}, u32[]{:S(2)}, u32[]{:S(2)}) collective-permute-start(bf16[4,2,64,1536]{3,2,0,1:T(8,128)(2,1)S(1)} %copy_bitcast_fusion.5), channel_id=1, source_target_pairs={{0,2},{2,0},{4,6},{6,4},{8,10},{10,8},{12,14},{14,12},{16,18},{18,... | collective-permute-start | bytes 4718600 | tf_op jit(solution)/shard_map/ppermute | solution.py:442
  492.4 26.3 %collective-permute-start.28 = (bf16[64,2048]{1,0:T(8,128)(2,1)S(1)}, bf16[64,2048]{1,0:T(8,128)(2,1)S(1)}, u32[]{:S(2)}, u32[]{:S(2)}) collective-permute-start(bf16[64,2048]{1,0:T(8,128)(2,1)S(1)} %get-tuple-element.165), channel_id=1, source_target_pairs={{0,8},{2,10},{4,12},{6,14},{8,16},{10,18},{12,20},{14,22},{16,24},... | collective-permute-start | bytes 786440 | tf_op jit(solution)/shard_map/ppermute | solution.py:442
  524.0 38.3 %collective-permute-start.31 = (bf16[64,1024]{1,0:T(8,128)(2,1)}, bf16[64,1024]{1,0:T(8,128)(2,1)S(1)}, u32[]{:S(2)}, u32[]{:S(2)}) collective-permute-start(bf16[64,1024]{1,0:T(8,128)(2,1)} %get-tuple-element.168), channel_id=1, source_target_pairs={{0,8},{2,10},{4,12},{6,14},{8,16},{10,18},{12,20},{14,22},{16,24},... | collective-permute-start | bytes 393224 | tf_op jit(solution)/shard_map/ppermute | solution.py:442
  525.8 36.6 %collective-permute-start.32 = (bf16[64,1024]{1,0:T(8,128)(2,1)}, bf16[64,1024]{1,0:T(8,128)(2,1)S(1)}, u32[]{:S(2)}, u32[]{:S(2)}) collective-permute-start(bf16[64,1024]{1,0:T(8,128)(2,1)} %get-tuple-element.169), channel_id=1, source_target_pairs={{0,16},{2,18},{4,20},{6,22},{8,24},{10,26},{12,28},{14,30},{16,0},... | collective-permute-start | bytes 393224 | tf_op jit(solution)/shard_map/ppermute | solution.py:442
  526.0 36.4 %collective-permute-start.33 = (bf16[64,1024]{1,0:T(8,128)(2,1)S(1)}, bf16[64,1024]{1,0:T(8,128)(2,1)S(1)}, u32[]{:S(2)}, u32[]{:S(2)}) collective-permute-start(bf16[64,1024]{1,0:T(8,128)(2,1)S(1)} %get-tuple-element.170), channel_id=1, source_target_pairs={{0,24},{2,26},{4,28},{6,30},{8,0},{10,2},{12,4},{14,6},{16,8},{18,... | collective-permute-start | bytes 393224 | tf_op jit(solution)/shard_map/ppermute | solution.py:442
  528.4 42.6 %collective-permute-start.44 = (bf16[64,2048]{1,0:T(8,128)(2,1)S(1)}, bf16[64,2048]{1,0:T(8,128)(2,1)S(1)}, u32[]{:S(2)}, u32[]{:S(2)}) collective-permute-start(bf16[64,2048]{1,0:T(8,128)(2,1)S(1)} %fusion.63), channel_id=1, source_target_pairs={{0,1},{1,0},{2,3},{3,2},{4,5},{5,4},{6,7},{7,6},{8,9},{9,8},{10,11... | collective-permute-start | bytes 786440 | tf_op jit(solution)/shard_map/ppermute | solution.py:415
  529.5 56.6 %collective-permute-start.38 = (bf16[4,64,1536]{2,1,0:T(8,128)(2,1)}, bf16[4,64,1536]{2,1,0:T(8,128)(2,1)}, u32[]{:S(2)}, u32[]{:S(2)}) collective-permute-start(bf16[4,64,1536]{2,1,0:T(8,128)(2,1)} %fusion.44), channel_id=1, source_target_pairs={{0,4},{2,6},{4,0},{6,2},{8,12},{10,14},{12,8},{14,10},{16,20},{18,... | collective-permute-start | bytes 2359304 | tf_op jit(solution)/shard_map/ppermute | solution.py:442
  (93 other events, 1709.1 us)

commit v3 on v2

--- a/solution.py
+++ b/solution.py
@@ -423,9 +423,23 @@
     def __init__(self, grad, n, s):
         A, B = grid_of(n)
         self.A, self.B, self.s = A, B, s
-        self.grad = grad.reshape(A, B, 2, grad.shape[0] // n, grad.shape[1])
+        self.into = None
+        if grad.ndim == 2:
+            self.grad = grad.reshape(A, B, 2, -1, grad.shape[1])
         me = lax.axis_index("fsdp")
         self.a, self.b, self.c = me // (2 * B), (me // 2) % B, me % 2
+
+    @staticmethod
+    def halved(grad, n, s):
+        ex = Exchange(grad, n, s)
+        ex.half = grad.reshape((ex.A, ex.B) + grad.shape[1:])
+        return ex
+
+    @staticmethod
+    def summed(grad, n, s):
+        ex = Exchange(grad[None], n, s)
+        ex.total, ex.a, ex.from_a = grad[None], 0, []
+        return ex
 
     def shift(self, value, da, db, dc):
         A, B = self.A, self.B
@@ -452,6 +466,8 @@
         self.into = self.shift(out[0], 0, 0, 1)
 
     def b_sum(self, index):
+        if self.into is None:
+            return self.take(self.half, index, 1).astype(f32)
         mine = self.take(self.take(self.grad, self.c, 2), index, 1)
         return mine.astype(f32) + self.take(self.into, index, 1).astype(f32)
 
@@ -472,7 +488,7 @@
         self.from_a = [self.shift(v, k + 1, 0, 0) for k, v in enumerate(out)]
 
     def x_send(self):
-        total = self.take(self.total, self.a, 0)
+        total = self.take(self.total, self.a, 0).astype(f32)
         for v in self.from_a:
             total = total + v.astype(f32)
         if self.s != 2:
@@ -490,6 +506,297 @@
         if self.s != 2:
             return self.total
         return self.total.astype(f32) + self.from_x.astype(f32)
+
+
+def remote(src, dst, send, recv, device):
+    return pltpu.make_async_remote_copy(
+        src_ref=src, dst_ref=dst, send_sem=send, recv_sem=recv, device_id=device, device_id_type=MESH
+    )
+
+
+def greet(devices):
+    bar = pltpu.get_barrier_semaphore()
+    for d in devices:
+        pl.semaphore_signal(bar, inc=1, device_id=d, device_id_type=MESH)
+    pl.semaphore_wait(bar, len(devices))
+
+
+class Place:
+    def __init__(self, n):
+        self.A, self.B = grid_of(n)
+        me = lax.axis_index("fsdp")
+        self.me = me
+        self.a, self.b, self.c = me // (2 * self.B), lax.rem(me // 2, self.B), lax.rem(me, 2)
+
+    def dev(self, a, b, c):
+        return {"fsdp": (a * self.B + b) * 2 + c}
+
+    def at_a(self, k):
+        return self.dev(lax.rem(self.a + k, self.A), self.b, self.c)
+
+    def at_b(self, k):
+        return self.dev(self.a, lax.rem(self.b + k, self.B), self.c)
+
+    def sibling(self):
+        return self.dev(self.a, self.b, 1 - self.c)
+
+    def all(self):
+        return [self.at_a(k) for k in range(1, self.A)] + [self.at_b(k) for k in range(1, self.B)] + [self.sibling()]
+
+
+def add32(*values):
+    total = values[0].astype(f32)
+    for v in values[1:]:
+        total = total + v.astype(f32)
+    return total
+
+
+def gelu_both(x):
+    k = 0.7978845608028654
+    sq = x * x
+    th = jnp.tanh(k * (x + 0.044715 * (sq * x)))
+    half = 0.5 * (1.0 + th)
+    slope = half + (0.5 * k) * x * (1.0 - th * th) * (1.0 + (3 * 0.044715) * sq)
+    return x * half, slope
+
+
+def normalize(v):
+    center = v - jnp.mean(v, axis=-1, keepdims=True)
+    rscale = lax.rsqrt(jnp.mean(center * center, axis=-1, keepdims=True) + norm_eps)
+    return center * rscale, rscale
+
+
+def feed_forward(middle, branch, attn, g, vectors, b_fc1, proj_w, w1, w2, n):
+    T, D = middle.shape
+    FF = w1.shape[1]
+    A, B = grid_of(n)
+    J, r1, r2 = A * B, D // n, FF // n
+    W = 2 * r2
+    RB = min(T, 64)
+
+    def kern(
+        mid_ref, br_ref, attn_ref, g_ref, vec_ref, b1_ref, pw_ref, w1_ref, w2_ref,
+        out_ref, dmid_ref, dattn_ref, sums_ref, bfc1_ref, gproj_ref, g1_ref, g2_ref,
+        h2, h2t, dm, dh2, mlp, dbr, w1b, w2b, gb, cr, ys, yr, zs, zr, t1, c1, s1,
+        wsem, osem, cs, crs, c1s, c1r, yss, yrs, zss, zrs,
+    ):
+        at = Place(n)
+        greet(at.all())
+        shift2, scale2, gate2, gate1, bias2 = [vec_ref[i : i + 1, :] for i in range(5)]
+
+        def tile(t):
+            k, m = t // B, lax.rem(t, B)
+            return lax.rem(at.a + 1 + k, A) * B + lax.rem(at.b + 1 + m, B)
+
+        def weights(t, slot):
+            lo = pl.multiple_of(tile(t) * W, W)
+            return (
+                pltpu.make_async_copy(w1_ref.at[:, pl.ds(lo, W)], w1b.at[slot], wsem.at[0, slot]),
+                pltpu.make_async_copy(w2_ref.at[pl.ds(lo, W), :], w2b.at[slot], wsem.at[1, slot]),
+            )
+
+        for w in weights(0, 0):
+            w.start()
+
+        def head(i, _):
+            rows = pl.ds(pl.multiple_of(i * RB, RB), RB)
+            normed, _r = normalize(mid_ref[rows, :])
+            h2[rows, :] = (normed * (1.0 + scale2) + shift2).astype(bf16)
+            dm[rows, :] = (g_ref[rows, :].astype(f32) * gate2).astype(bf16)
+            return 0
+
+        lax.fori_loop(0, T // RB, head, 0)
+        for i in range(0, D, 256):
+            h2t[i : i + 256, :] = h2[:, i : i + 256].T
+        dh2[...] = jnp.zeros_like(dh2)
+        mlp[...] = jnp.zeros_like(mlp)
+        sums_ref[...] = jnp.zeros_like(sums_ref)
+
+        def c2_copy(t):
+            return remote(gb.at[t, 1 - at.c], cr.at[t], cs.at[t], crs.at[t], at.sibling())
+
+        def c1_copy(t, slot):
+            return remote(t1.at[slot, :, 1 - at.c], c1.at[t], c1s.at[t], c1r.at[t], at.sibling())
+
+        def y_copy(k, m):
+            return remote(ys.at[k, m], yr.at[k, m], yss.at[k, m], yrs.at[k, m], at.at_b(m + 1))
+
+        def z_copy(k):
+            return remote(zs.at[k], zr.at[k], zss.at[k], zrs.at[k], at.at_a(k + 1))
+
+        def s1_copy(t, slot):
+            lo = pl.multiple_of(tile(t) * W, W)
+            return pltpu.make_async_copy(s1.at[slot], g1_ref.at[:, :, pl.ds(lo, W)], osem.at[slot])
+
+        def chip_sum1(t, slot, first):
+            c1_copy(t, slot).wait()
+
+            @pl.when(jnp.logical_not(first))
+            def _():
+                s1_copy(t, slot).wait()
+
+            def part(i, _):
+                s1[slot, i] = add32(t1[slot, i, at.c], c1[t, i]).astype(bf16)
+                return 0
+
+            lax.fori_loop(0, J, part, 0)
+            s1_copy(t, slot).start()
+
+        R2 = min(r2, 64)
+
+        def own_sum(t, k):
+            c2_copy(t).wait()
+            for m in range(B - 1):
+                y_copy(k, m).wait()
+
+        def send_y(k, m):
+            t = k * B + m
+            c2_copy(t).wait()
+
+            def part(i, _):
+                rows = pl.ds(pl.multiple_of(i * R2, R2), R2)
+                ys[k, m, rows, :] = add32(gb[t, at.c, rows, :], cr[t, rows, :]).astype(bf16)
+                return 0
+
+            lax.fori_loop(0, r2 // R2, part, 0)
+            y_copy(k, m).start()
+
+        def send_z(k):
+            t = k * B + B - 1
+            own_sum(t, k)
+
+            def part(i, _):
+                rows = pl.ds(pl.multiple_of(i * R2, R2), R2)
+                total = add32(gb[t, at.c, rows, :], cr[t, rows, :], *[yr[k, m, rows, :] for m in range(B - 1)])
+                zs[k, rows, :] = total.astype(bf16)
+                return 0
+
+            lax.fori_loop(0, r2 // R2, part, 0)
+            z_copy(k).start()
+
+        def pair(k, _):
+            for m in range(B):
+                t = k * B + m
+                slot = m % 2
+                for w in weights(t, slot):
+                    w.wait()
+
+                @pl.when(t + 1 < J)
+                def _():
+                    for w in weights(t + 1, 1 - slot):
+                        w.start()
+
+                j = tile(t)
+                act, slope = gelu_both(nn(h2[...], w1b[slot]) + b1_ref[j])
+                act = act.astype(bf16)
+                g2t = tn(act, dm[...]).astype(bf16)
+                gb[t, 0] = g2t[:r2]
+                gb[t, 1] = g2t[r2:]
+                c2_copy(t).start()
+                dpre = (nt(dm[...], w2b[slot]) * slope).astype(bf16)
+                bfc1_ref[j] = jnp.sum(dpre.astype(f32), axis=0, keepdims=True)
+                t1[slot] = nn(h2t[...], dpre).astype(bf16).reshape(J, 2, r1, W)
+                c1_copy(t, slot).start()
+                mlp[...] += nn(act, w2b[slot])
+                dh2[...] += nt(dpre, w1b[slot])
+                if m > 0:
+                    chip_sum1(t - 1, 1 - slot, jnp.logical_and(k == 0, m < 3))
+                    send_y(k, m - 1)
+                else:
+
+                    @pl.when(k > 0)
+                    def _():
+                        chip_sum1(t - 1, 1 - slot, k * B < 3)
+
+                if m == B - 1:
+
+                    @pl.when(k > 0)
+                    def _():
+                        send_z(k - 1)
+
+            return 0
+
+        lax.fori_loop(0, A, pair, 0)
+        chip_sum1(J - 1, (B - 1) % 2, jnp.bool_(J < 3))
+
+        def back(i, _):
+            rows = pl.ds(pl.multiple_of(i * RB, RB), RB)
+            mid = mid_ref[rows, :]
+            gf = g_ref[rows, :].astype(f32)
+            normed, rscale = normalize(mid)
+            dh = dh2[rows, :]
+            up = dh * (1.0 + scale2)
+            dmid = gf + rscale * (
+                up
+                - jnp.mean(up, axis=-1, keepdims=True)
+                - normed * jnp.mean(up * normed, axis=-1, keepdims=True)
+            )
+            dmid_ref[rows, :] = dmid
+            db = (dmid * gate1).astype(bf16)
+            dbr[rows, :] = db
+            ml = mlp[rows, :] + bias2
+            out_ref[rows, :] = (mid + gate2 * ml).astype(bf16)
+            for row, v in enumerate((dh, dh * normed, gf * ml, dmid * br_ref[rows, :], dm[rows, :], db)):
+                sums_ref[row : row + 1, :] += jnp.sum(v.astype(f32), axis=0, keepdims=True)
+            return 0
+
+        lax.fori_loop(0, T // RB, back, 0)
+        dattn_ref[...] = nt(dbr[...], pw_ref[...]).astype(bf16)
+
+        def proj(i, _):
+            cols = pl.ds(pl.multiple_of(i * 256, 256), 256)
+            gproj_ref[cols, :] = tn(attn_ref[:, cols], dbr[...]).astype(bf16)
+            return 0
+
+        lax.fori_loop(0, D // 256, proj, 0)
+
+        last = J - 1
+        own_sum(last, A - 1)
+        for k in range(A - 1):
+            z_copy(k).wait()
+
+        def part(i, _):
+            rows = pl.ds(pl.multiple_of(i * R2, R2), R2)
+            total = add32(
+                gb[last, at.c, rows, :],
+                cr[last, rows, :],
+                *[yr[A - 1, m, rows, :] for m in range(B - 1)],
+                *[zr[k, rows, :] for k in range(A - 1)],
+            )
+            g2_ref[rows, :] = total.astype(bf16)
+            return 0
+
+        lax.fori_loop(0, r2 // R2, part, 0)
+        s1_copy(J - 2, 0).wait()
+        s1_copy(J - 1, 1).wait()
+
+    vm, hbm = pl.BlockSpec(memory_space=pltpu.VMEM), pl.BlockSpec(memory_space=pl.ANY)
+    sds = jax.ShapeDtypeStruct
+    dma = pltpu.SemaphoreType.DMA
+    return pl.pallas_call(
+        kern,
+        out_shape=[
+            sds((T, D), bf16), sds((T, D), f32), sds((T, D), bf16), sds((8, D), f32), sds((J, 1, W), f32),
+            sds((D, D), bf16), sds((J, r1, FF), bf16), sds((r2, D), bf16),
+        ],
+        in_specs=[vm] * 7 + [hbm] * 2,
+        out_specs=[vm] * 6 + [hbm, vm],
+        scratch_shapes=[
+            pltpu.VMEM((T, D), bf16), pltpu.VMEM((D, T), bf16), pltpu.VMEM((T, D), bf16),
+            pltpu.VMEM((T, D), f32), pltpu.VMEM((T, D), f32), pltpu.VMEM((T, D), bf16),
+            pltpu.VMEM((2, D, W), bf16), pltpu.VMEM((2, W, D), bf16),
+            pltpu.VMEM((J, 2, r2, D), bf16), pltpu.VMEM((J, r2, D), bf16),
+            pltpu.VMEM((A, B - 1, r2, D), bf16), pltpu.VMEM((A, B - 1, r2, D), bf16),
+            pltpu.VMEM((A - 1, r2, D), bf16), pltpu.VMEM((A - 1, r2, D), bf16),
+            pltpu.VMEM((2, J, 2, r1, W), bf16), pltpu.VMEM((J, J, r1, W), bf16), pltpu.VMEM((2, J, r1, W), bf16),
+            dma((2, 2)), dma((2,)), dma((J,)), dma((J,)), dma((J,)), dma((J,)),
+            dma((A, B - 1)), dma((A, B - 1)), dma((A - 1,)), dma((A - 1,)),
+        ],
+        compiler_params=pltpu.CompilerParams(
+            collective_id=3, has_side_effects=True, vmem_limit_bytes=64 * 1024 * 1024 - 65536
+        ),
+        name="feed_forward",
+    )(middle, branch, attn, g, vectors, b_fc1.reshape(J, 1, W), proj_w, w1, w2)
 
 
 def layer_norm(values):
@@ -551,46 +858,26 @@
     branch = nn(attn, proj_w) + proj_b
     middle = tokens_f + gate_one * branch
 
-    normed_two, rscale_two = layer_norm(middle)
-    hidden_two = (normed_two * (1.0 + scale_two) + shift_two).astype(bf16)
-    pre_act = nn(hidden_two, fc1_w) + fc1_b
-    act_f, gelu_back = jax.vjp(partial(jax.nn.gelu, approximate=True), pre_act)
-    act_b = act_f.astype(bf16)
-    d_mlp = (grad_out * gate_two).astype(bf16)
-    half_d, half_f = width // 2, fc1_w.shape[1] // 2
+    half_d = width // 2
 
     def exchange(lhs, rhs):
         return Exchange(tn(lhs, rhs).astype(bf16), n, s)
 
-    fc2a, fc2b = exchange(act_b, d_mlp[:, :half_d]), exchange(act_b, d_mlp[:, half_d:])
-    d_mlp, sa, sb = tie(d_mlp, fc2a.c_send(), fc2b.c_send())
-    fc2a.c_start(sa)
-    fc2b.c_start(sb)
-    bias_fc2 = jnp.sum(d_mlp, axis=0, dtype=f32)
-    d_pre = gelu_back(nt(d_mlp, fc2_w))[0].astype(bf16)
-    d_pre, sa, sb = tie(d_pre, fc2a.b_send(), fc2b.b_send())
-    fc2a.b_start(sa)
-    fc2b.b_start(sb)
-    fc1a, fc1b = exchange(hidden_two, d_pre[:, :half_f]), exchange(hidden_two, d_pre[:, half_f:])
-    bias_fc1 = jnp.sum(d_pre, axis=0, dtype=f32)
-    d_pre, sa, sb = tie(d_pre, fc1a.c_send(), fc1b.c_send())
-    fc1a.c_start(sa)
-    fc1b.c_start(sb)
-    d_hidden_two = nt(d_pre, fc1_w)
-    d_shift_two = jnp.sum(d_hidden_two, axis=0, keepdims=True)
-    d_scale_two = jnp.sum(d_hidden_two * normed_two, axis=0, keepdims=True)
-    d_middle = grad_out + norm_back(d_hidden_two * (1.0 + scale_two), normed_two, rscale_two)
-    d_gate_one = jnp.sum(d_middle * branch, axis=0, keepdims=True)
-    d_branch = (d_middle * gate_one).astype(bf16)
-    d_branch, sa, sb, sc = tie(d_branch, fc1a.b_send(), fc1b.b_send(), fc2a.a_send())
-    fc1a.b_start(sa)
-    fc1b.b_start(sb)
-    fc2a.a_start(sc)
-    proj = exchange(attn, d_branch)
-    bias_proj = jnp.sum(d_branch, axis=0, dtype=f32)
-    d_attn = nt(d_branch, proj_w).astype(bf16)
-    d_attn, sa = tie(d_attn, proj.c_send())
-    proj.c_start(sa)
+    vectors = jnp.concatenate([shift_two, scale_two, gate_two, gate_one, fc2_b, jnp.zeros((3, width), f32)], axis=0)
+    result, d_middle, d_attn, sums, bias_fc1, grad_proj, half_fc1, sum_fc2 = feed_forward(
+        middle, branch, attn, cotangent[0], vectors, fc1_b, proj_w, fc1_w, fc2_w, n
+    )
+    d_shift_two, d_scale_two, d_gate_two, d_gate_one, bias_fc2, bias_proj = [sums[i : i + 1] for i in range(6)]
+    bias_fc1 = bias_fc1.reshape(-1)
+    fc2 = Exchange.summed(sum_fc2, n, s)
+    sum_fc2 = fc2.x_send()
+    fc2.x_start(sum_fc2)
+    half_f = fc1_w.shape[1] // 2
+    fc1a, fc1b = Exchange.halved(half_fc1[:, :, :half_f], n, s), Exchange.halved(half_fc1[:, :, half_f:], n, s)
+    proj = Exchange(grad_proj, n, s)
+    fc1a.b_start(fc1a.b_send())
+    fc1b.b_start(fc1b.b_send())
+    proj.c_start(proj.c_send())
     halves = []
     lo = slice(0, half_d)
     hi = slice(half_d, width)
@@ -606,16 +893,16 @@
         return [seq_shift(dk[k], s - k, s) for k in range(1, s)]
 
     q1, dk1, dv1 = attention(lo)
-    q1, dk1, dv1, sa, sb = tie(q1, dk1, dv1, proj.b_send(), fc2b.a_send())
+    q1, dk1, dv1, sa, sb = tie(q1, dk1, dv1, proj.b_send(), fc1a.a_send())
     rk1, rv1 = back(dk1), back(dv1)
     proj.b_start(sa)
-    fc2b.a_start(sb)
+    fc1a.a_start(sb)
     d_attn, q1 = tie(d_attn, q1)
     q2, dk2, dv2 = attention(hi)
-    q2, dk2, dv2, sa, sb = tie(q2, dk2, dv2, fc1a.a_send(), fc2a.x_send())
+    q2, dk2, dv2, sa, sb = tie(q2, dk2, dv2, fc1b.a_send(), proj.a_send())
     rk2, rv2 = back(dk2), back(dv2)
-    fc1a.a_start(sa)
-    fc2a.x_start(sb)
+    fc1b.a_start(sa)
+    proj.a_start(sb)
 
     def joined(q, dk, rk, dv, rv):
         gk, gv = dk[0], dv[0]
@@ -627,20 +914,12 @@
 
     d1 = joined(q1, dk1, rk1, dv1, rv1)
     qkv1 = exchange(hidden_one, d1)
-    act_b, sa = tie(act_b, qkv1.c_send())
+    d2, sa = tie(joined(q2, dk2, rk2, dv2, rv2), qkv1.c_send())
     qkv1.c_start(sa)
-    mlp_out = nn(act_b, fc2_w) + fc2_b
-    result = (middle + gate_two * mlp_out).astype(bf16)
-    d_gate_two = jnp.sum(grad_out * mlp_out, axis=0, keepdims=True)
-    d_gate_two, sa, sb, sc = tie(d_gate_two, qkv1.b_send(), fc1b.a_send(), fc2b.x_send())
+    qkv2 = exchange(hidden_one, d2)
+    d2, sa, sb = tie(d2, qkv1.b_send(), qkv2.c_send())
     qkv1.b_start(sa)
-    fc1b.a_start(sb)
-    fc2b.x_start(sc)
-    d2 = joined(q2, dk2, rk2, dv2, rv2)
-    hidden_one_, d_gate_two = tie(hidden_one, d_gate_two)
-    qkv2 = exchange(hidden_one_, d2)
-    d2, sa = tie(d2, qkv2.c_send())
-    qkv2.c_start(sa)
+    qkv2.c_start(sb)
     sums1, sums2 = jnp.sum(d1, axis=0, dtype=f32), jnp.sum(d2, axis=0, dtype=f32)
     bias_qv = jnp.concatenate([sums1[:half_d], sums2[:half_d], sums1[width:], sums2[width:]])
     d_qkv = jnp.concatenate([v[:, i * half_d : (i + 1) * half_d] for i in range(3) for v in (d1, d2)], axis=1)
@@ -648,9 +927,9 @@
     d_shift_one = jnp.sum(d_hidden_one, axis=0, keepdims=True)
     d_scale_one = jnp.sum(d_hidden_one * normed_one, axis=0, keepdims=True)
     grad_input = d_middle + norm_back(d_hidden_one * (1.0 + scale_one), normed_one, rscale_one)
-    d_scale_one, sa, sb, sc = tie(d_scale_one, qkv2.b_send(), proj.a_send(), fc1a.x_send())
+    d_scale_one, sa, sb, sc = tie(d_scale_one, qkv2.b_send(), proj.x_send(), fc1a.x_send())
     qkv2.b_start(sa)
-    proj.a_start(sb)
+    proj.x_start(sb)
     fc1a.x_start(sc)
 
     d_part = jnp.concatenate(
@@ -663,14 +942,13 @@
     share = b_ada.shape[0]
     total_bada = lax.dynamic_slice_in_dim(sums_ada[0], lax.axis_index("fsdp") * share, share)
     grad_condition = silu_back(d_lifted.reshape(1, width))[0]
-    total_bias, sa, sb, sc = tie(total_bias, qkv1.a_send(), fc1b.x_send(), proj.x_send())
+    total_bias, sa, sb = tie(total_bias, qkv1.a_send(), fc1b.x_send())
     qkv1.a_start(sa)
     fc1b.x_start(sb)
-    proj.x_start(sc)
     qkv2.a_start(qkv2.a_send())
     qkv1.x_start(qkv1.x_send())
     qkv2.x_start(qkv2.x_send())
-    total_fc2 = jnp.concatenate([fc2a.result(), fc2b.result()], axis=1)
+    total_fc2 = fc2.result()
     total_fc1 = jnp.concatenate([fc1a.result(), fc1b.result()], axis=1)
     total_proj = proj.result()
     r1, r2 = qkv1.result(), qkv2.result()

time: 624 us -> 562 us (0.901)
  Pallas kernels: 224 us -> 306 us
  matrix products: 78.9 us -> 23.3 us
  waiting for transfers between devices: 141 us -> 107 us
  other arithmetic: 58.8 us -> 28.8 us
  starting transfers between devices: 63.6 us -> 40.4 us
    pallas_call x0 -> x1, Pallas kernels: none -> 85.2 us  [feed_forward(): pl.pallas_call(kern, out_shape=[sds((T, D), bf16), sds((T, D), f32), sds(...]
    ppermute x13 -> x12, waiting for transfers between devices: 77.3 us -> 49.8 us  [seq_shift(): return lax.ppermute(value, 'seq', [(i, (i + k) % s) for i in range(s)])]
    dot_general x4 -> x1, matrix products: 30.5 us -> 4 us  [nt(): lax.dot_general(a, b, (((1,), (1,)), ((), ())), preferred_element_type=f32)]
    ppermute x35 -> x23, starting transfers between devices: 50.2 us -> 27.9 us  [shift(): return lax.ppermute(value, 'fsdp', pairs)]
    dot_general x6 -> x4, matrix products: 33.4 us -> 15.2 us  [nn(): lax.dot_general(a, b, (((1,), (0,)), ((), ())), preferred_element_type=f32)]
    convert_element_type x7 -> x3, other arithmetic: 16.6 us -> 3.17 us  [b_send(): self.b_sum((self.b + k) % self.B).astype(bf16)]
    dot_general x7 -> x2, matrix products: 15.1 us -> 4.13 us  [tn(): lax.dot_general(a, b, (((0,), (0,)), ((), ())), preferred_element_type=f32)]
    reduce_sum x4 -> x0, other arithmetic: 7.45 us -> none  [the longest x1 4.85 us: on_device(): d_gate_one = jnp.sum(d_middle * branch, axis=0, keepdims=True)]
  transfers between devices with their start and end apart: 48 -> 35, of which waited for: 17 -> 12; matrix products, arithmetic and copies ran while one was open for 20% -> 10% of each run, Pallas kernels for 9% -> 6%
where the time goes in v3:
time: 562 us; the launch traced here: 555 us
  Pallas kernels  306 us (54%)
  waiting for transfers between devices  107 us (19%)
  local copies, waits for them, and re-layouts  47.4 us (8%)
  starting transfers between devices  40.4 us (7%)
  other arithmetic  28.8 us (5%)
  matrix products  23.3 us (4%)
    pallas_call x1, Pallas kernels, gather_weights(): pl.pallas_call(kern, out_shape=[jax.ShapeDtypeStruct((A, B, 2) + w.shape,...  127 us
    pallas_call x1, Pallas kernels, feed_forward(): pl.pallas_call(kern, out_shape=[sds((T, D), bf16), sds((T, D), f32), sds(...  85.2 us
    ppermute x23, waiting for transfers between devices, shift(): return lax.ppermute(value, 'fsdp', pairs)  57.6 us
    ppermute x12, waiting for transfers between devices, seq_shift(): return lax.ppermute(value, 'seq', [(i, (i + k) % s) for i in range(s)])  49.8 us
    pallas_call x2, Pallas kernels, attend_backward(): pl.pallas_call(partial(attend_backward_kernel, n), grid=(D // 128,), in_s...  32 us
    ppermute x23, starting transfers between devices, shift(): return lax.ppermute(value, 'fsdp', pairs)  27.9 us
    pallas_call x1, Pallas kernels, modulation_backward(): pl.pallas_call(kern, out_shape=[jax.ShapeDtypeStruct((rows, E), f32), jax...  22.8 us
    pallas_call x1, Pallas kernels, modulation_forward(): pl.pallas_call(kern, out_shape=[jax.ShapeDtypeStruct((1, E), f32), jax.Sh...  20.6 us
  transfers between devices with their start and end apart: 35, of which 12 were waited for; matrix products, arithmetic and copies ran while one was open for 10% of the time, Pallas kernels for 6%

profile of v3, /device:TPU:0, one launch (start us, length us, event | category | flops | bytes accessed | tf_op | source)
XLA Modules:
  0.0 554.9 jit_solution(116597961736671437)
XLA Ops:
  5.4 20.6 %modulation_forward.1 = (f32[1,6144]{1,0:T(1,128)}, f32[16,1,64]{2,1,0:T(1,128)}, f32[16,1,896]{2,1,0:T(1,128)}) custom-call(f32[16,1,64]{2,1,0:T(1,128)} %bitcast.248, bf16[64,6144]{1,0:T(8,128)(2,1)} %w_ref.3, f32[1,896]{1,0:T(1,128)} %convert_element_type.375.bias_ref), custom_call_target="tpu_custom_call" | custom-call | tf_op jit(solution)/shard_map/modulation_forward/pallas_call | solution.py:194
  29.5 127.5 %gather_weights.1 = (bf16[4,2,2,64,3072]{4,3,2,1,0:T(8,128)(2,1)}, bf16[4,2,2,64,1024]{4,3,2,1,0:T(8,128)(2,1)}, bf16[4,2,2,64,4096]{4,3,2,1,0:T(8,128)(2,1)}, bf16[4,2,2,256,1024]{4,3,2,1,0:T(8,128)(2,1)}) custom-call(bf16[64,3072]{1,0:T(8,128)(2,1)} %refs_0_.1, bf16[64,1024]{1,0:T(8,128)(2,1)} %refs_1_.1, bf16[64,4096]{1,0:T(8,128)(2,1)} %refs_2_.1, ...), custom_call_target="tpu_custom_call" | custom-call | tf_op jit(solution)/shard_map/gather_weights/pallas_call | solution.py:131
  156.9 3.9 fusion.31.refs_0_
  162.0 3.9 add_convert_fusion.refs_2_
  175.3 11.8 %collective-permute-done.refs_1_ = bf16[512,1024]{1,0:T(8,128)(2,1)} collective-permute-done((bf16[512,1024]{1,0:T(8,128)(2,1)}, bf16[512,1024]{1,0:T(8,128)(2,1)}, u32[]{:S(2)}, u32[]{:S(2)}) %collective-permute-start) | collective-permute-done | bytes 1048608 | tf_op jit(solution)/shard_map/ppermute | solution.py:415
  187.2 21.9 %collective-permute-done.1.refs_3_ = bf16[512,1024]{1,0:T(8,128)(2,1)} collective-permute-done((bf16[512,1024]{1,0:T(8,128)(2,1)}, bf16[512,1024]{1,0:T(8,128)(2,1)}, u32[]{:S(2)}, u32[]{:S(2)}) %collective-permute-start.1) | collective-permute-done | bytes 1048608 | tf_op jit(solution)/shard_map/ppermute | solution.py:415
  209.1 17.9 %attend_forward.1 = (bf16[512,1024]{1,0:T(8,128)(2,1)}, f32[8,2,512]{2,1,0:T(2,128)}) custom-call(bf16[512,1024]{1,0:T(8,128)(2,1)} %copy-done.16, bf16[512,1024]{1,0:T(8,128)(2,1)} %fusion.31.refs_0_, bf16[512,1024]{1,0:T(8,128)(2,1)} %collective-permute-done.refs_1_, bf16[512,1024]{1,0:T(8,128)(2,1)} %add_convert_fusion.refs_2_, ...), custom_call_target="tpu_custom_call" | custom-call | flops 8589934592 | bytes 6291456 | tf_op jit(solution)/shard_map/attend_forward/pallas_call | solution.py:350
  227.0 4.5 fusion
  231.5 85.2 %feed_forward.1 = (bf16[512,1024]{1,0:T(8,128)(2,1)}, f32[512,1024]{1,0:T(8,128)}, bf16[512,1024]{1,0:T(8,128)(2,1)}, f32[8,1024]{1,0:T(8,128)}, f32[8,1,512]{2,...) custom-call(f32[512,1024]{1,0:T(8,128)} %get-tuple-element.201.mid_ref, ...), custom_call_target="tpu_custom_call" | custom-call | tf_op jit(solution)/shard_map/feed_forward/pallas_call | solution.py:776
  333.7 16.0 %attend_backward.2 = (bf16[512,512]{1,0:T(8,128)(2,1)}, f32[512,512]{1,0:T(8,128)}, bf16[512,512]{1,0:T(8,128)(2,1)}, f32[512,512]{1,0:T(8,128)}, bf16[512,512]{1,0:T(8,128)(2,1)}) custom-call(bf16[512,512]{1,0:T(8,128)(2,1)} %get-tuple-element.183.q_ref, bf16[512,512]{1,0:T(8,128)(2,1)} %slice.198.e_ref, f32[4,2,512]{2,1,0:T(2,128)} %get-tuple-element.186.lse_ref, ...), custom_call_target="tpu_custom_call" | custom-call | flops 8053063680 | bytes 6291456 | tf_op jit(solution)/shard_map/attend_backward/pallas_call | solution.py:402
  363.5 16.0 %attend_backward.3 = (bf16[512,512]{1,0:T(8,128)(2,1)}, f32[512,512]{1,0:T(8,128)}, bf16[512,512]{1,0:T(8,128)(2,1)}, f32[512,512]{1,0:T(8,128)}, bf16[512,512]{1,0:T(8,128)(2,1)}) custom-call(bf16[512,512]{1,0:T(8,128)(2,1)} %get-tuple-element.182.q_ref, bf16[512,512]{1,0:T(8,128)(2,1)} %slice.206.e_ref, f32[4,2,512]{2,1,0:T(2,128)} %get-tuple-element.185.lse_ref, ...), custom_call_target="tpu_custom_call" | custom-call | flops 8053063680 | bytes 6291456 | tf_op jit(solution)/shard_map/attend_backward/pallas_call | solution.py:402
  382.5 5.6 %collective-permute-done.15 = bf16[64,2048]{1,0:T(8,128)(2,1)S(1)} collective-permute-done((bf16[64,2048]{1,0:T(8,128)(2,1)S(1)}, bf16[64,2048]{1,0:T(8,128)(2,1)S(1)}, u32[]{:S(2)}, u32[]{:S(2)}) %collective-permute-start.15) | collective-permute-done | bytes 262176 | tf_op jit(solution)/shard_map/ppermute | solution.py:456
  401.7 5.4 collective-permute-done.7
  407.1 4.1 collective-permute-start.21
  411.4 4.9 collective-permute-done.6
  421.6 13.1 %collective-permute-done.20 = bf16[64,2048]{1,0:T(8,128)(2,1)S(1)} collective-permute-done((bf16[64,2048]{1,0:T(8,128)(2,1)S(1)}, bf16[64,2048]{1,0:T(8,128)(2,1)S(1)}, u32[]{:S(2)}, u32[]{:S(2)}) %collective-permute-start.20) | collective-permute-done | bytes 262176 | tf_op jit(solution)/shard_map/ppermute | solution.py:456
  441.0 4.0 fusion.15
  449.7 15.9 %collective-permute-done.18 = bf16[4,64,1536]{2,1,0:T(8,128)(2,1)S(1)} collective-permute-done((bf16[4,64,1536]{2,1,0:T(8,128)(2,1)S(1)}, bf16[4,64,1536]{2,1,0:T(8,128)(2,1)S(1)}, u32[]{:S(2)}, u32[]{:S(2)}) %collective-permute-start.18) | collective-permute-done | bytes 786464 | tf_op jit(solution)/shard_map/ppermute | solution.py:456
  475.5 22.8 %modulation_backward.1 = (f32[64,6144]{1,0:T(8,128)}, f32[1,6144]{1,0:T(1,128)}, f32[16,1,64]{2,1,0:T(1,128)}, f32[1,512]{1,0:T(1,128)}) custom-call(f32[1,6144]{1,0:T(1,128)} %get-tuple-element.184.d_ref, f32[16,1,512]{2,1,0:T(1,128)} %broadcast_in_dim.29.bp_ref, f32[16,1,64]{2,1,0:T(1,128)} %get-tuple-element.129.lf_ref, bf16[64,6144]{1,0:T(8,128)(2,1)} %w_ref.3), custom_call_target="tpu_custom_call" | custom-call | tf_op jit(solution)/shard_map/modulation_backward/pallas_call | solution.py:283
  513.8 8.4 %collective-permute-done.23 = bf16[64,1536]{1,0:T(8,128)(2,1)S(1)} collective-permute-done((bf16[64,1536]{1,0:T(8,128)(2,1)}, bf16[64,1536]{1,0:T(8,128)(2,1)S(1)}, u32[]{:S(2)}, u32[]{:S(2)}) %collective-permute-start.23) | collective-permute-done | bytes 196640 | tf_op jit(solution)/shard_map/ppermute | solution.py:456
  527.4 4.1 collective-permute-start.29
  532.2 3.4 collective-permute-done.29
  535.6 11.0 %collective-permute-done.28 = bf16[64,1536]{1,0:T(8,128)(2,1)S(1)} collective-permute-done((bf16[64,1536]{1,0:T(8,128)(2,1)S(1)}, bf16[64,1536]{1,0:T(8,128)(2,1)S(1)}, u32[]{:S(2)}, u32[]{:S(2)}) %collective-permute-start.28) | collective-permute-done | bytes 196640 | tf_op jit(solution)/shard_map/ppermute | solution.py:456
  547.2 5.2 collective-permute-done.30
  (242 shorter events, 116.1 us)
Async XLA Ops:
  160.8 26.3 %collective-permute-start = (bf16[512,1024]{1,0:T(8,128)(2,1)}, bf16[512,1024]{1,0:T(8,128)(2,1)}, u32[]{:S(2)}, u32[]{:S(2)}) collective-permute-start(bf16[512,1024]{1,0:T(8,128)(2,1)} %fusion.31.refs_0_), channel_id=1, source_target_pairs={{0,1},{1,0},{2,3},{3,2},{4,5},{5,4},{6,7},{7,6},{8,9},{9,8},{10,11... | collective-permute-start | bytes 3145736 | tf_op jit(solution)/shard_map/ppermute | solution.py:415
  165.8 43.2 %collective-permute-start.1 = (bf16[512,1024]{1,0:T(8,128)(2,1)}, bf16[512,1024]{1,0:T(8,128)(2,1)}, u32[]{:S(2)}, u32[]{:S(2)}) collective-permute-start(bf16[512,1024]{1,0:T(8,128)(2,1)} %add_convert_fusion.refs_2_), channel_id=1, source_target_pairs={{0,1},{1,0},{2,3},{3,2},{4,5},{5,4},{6,7},{7,6},{8,9},{9,8},{10,11... | collective-permute-start | bytes 3145736 | tf_op jit(solution)/shard_map/ppermute | solution.py:415
  320.8 33.4 %collective-permute-start.2 = (bf16[4,2,64,1024]{3,2,0,1:T(8,128)(2,1)}, bf16[4,2,64,1024]{3,2,0,1:T(8,128)(2,1)}, u32[]{:S(2)}, u32[]{:S(2)}) collective-permute-start(bf16[4,2,64,1024]{3,2,0,1:T(8,128)(2,1)} %copy_bitcast_fusion.2), channel_id=1, source_target_pairs={{0,2},{2,0},{4,6},{6,4},{8,10},{10,8},{12,14},{14,12},{16,18},{18,... | collective-permute-start | bytes 3145736 | tf_op jit(solution)/shard_map/ppermute | solution.py:456
  324.6 26.3 %collective-permute-start.3 = (bf16[4,64,2048]{2,1,0:T(8,128)(2,1)}, bf16[4,64,2048]{2,1,0:T(8,128)(2,1)}, u32[]{:S(2)}, u32[]{:S(2)}) collective-permute-start(bf16[4,64,2048]{2,1,0:T(8,128)(2,1)} %dynamic-slice_bitcast_fusion.1), channel_id=1, source_target_pairs={{0,4},{2,6},{4,0},{6,2},{8,12},{10,14},{12,8},{14,10},{16,20},{18,... | collective-permute-start | bytes 3145736 | tf_op jit(solution)/shard_map/ppermute | solution.py:456
  326.6 53.0 %collective-permute-start.4 = (bf16[4,64,2048]{2,1,0:T(8,128)(2,1)}, bf16[4,64,2048]{2,1,0:T(8,128)(2,1)}, u32[]{:S(2)}, u32[]{:S(2)}) collective-permute-start(bf16[4,64,2048]{2,1,0:T(8,128)(2,1)} %dynamic-slice_bitcast_fusion), channel_id=1, source_target_pairs={{0,4},{2,6},{4,0},{6,2},{8,12},{10,14},{12,8},{14,10},{16,20},{18,... | collective-permute-start | bytes 3145736 | tf_op jit(solution)/shard_map/ppermute | solution.py:456
  327.7 22.0 %collective-permute-start.34 = (bf16[256,1024]{1,0:T(8,128)(2,1)S(1)}, bf16[256,1024]{1,0:T(8,128)(2,1)S(1)}, u32[]{:S(2)}, u32[]{:S(2)}) collective-permute-start(bf16[256,1024]{1,0:T(8,128)(2,1)S(1)} %copy-done.18), channel_id=1, source_target_pairs={{0,1},{1,0},{2,3},{3,2},{4,5},{5,4},{6,7},{7,6},{8,9},{9,8},{10,11... | collective-permute-start | bytes 1572872 | tf_op jit(solution)/shard_map/ppermute | solution.py:415
  356.9 32.6 %collective-permute-start.5 = (bf16[4,64,1024]{2,1,0:T(8,128)(2,1)S(1)}, bf16[4,64,1024]{2,1,0:T(8,128)(2,1)}, u32[]{:S(2)}, u32[]{:S(2)}) collective-permute-start(bf16[4,64,1024]{2,1,0:T(8,128)(2,1)S(1)} %fusion.35), channel_id=1, source_target_pairs={{0,4},{2,6},{4,0},{6,2},{8,12},{10,14},{12,8},{14,10},{16,20},{18,... | collective-permute-start | bytes 1572872 | tf_op jit(solution)/shard_map/ppermute | solution.py:456
  358.1 35.7 %collective-permute-start.9 = (bf16[512,512]{1,0:T(8,128)(2,1)}, bf16[512,512]{1,0:T(8,128)(2,1)}, u32[]{:S(2)}, u32[]{:S(2)}) collective-permute-start(bf16[512,512]{1,0:T(8,128)(2,1)} %get-tuple-element.115), channel_id=1, source_target_pairs={{0,1},{1,0},{2,3},{3,2},{4,5},{5,4},{6,7},{7,6},{8,9},{9,8},{10,11... | collective-permute-start | bytes 1572872 | tf_op jit(solution)/shard_map/ppermute | solution.py:415
  359.1 22.3 %collective-permute-start.17 = (bf16[64,2048]{1,0:T(8,128)(2,1)}, bf16[64,2048]{1,0:T(8,128)(2,1)}, u32[]{:S(2)}, u32[]{:S(2)}) collective-permute-start(bf16[64,2048]{1,0:T(8,128)(2,1)} %get-tuple-element.125), channel_id=1, source_target_pairs={{0,24},{2,26},{4,28},{6,30},{8,0},{10,2},{12,4},{14,6},{16,8},{18,... | collective-permute-start | bytes 786440 | tf_op jit(solution)/shard_map/ppermute | solution.py:456
  362.0 20.5 %collective-permute-start.16 = (bf16[64,2048]{1,0:T(8,128)(2,1)}, bf16[64,2048]{1,0:T(8,128)(2,1)}, u32[]{:S(2)}, u32[]{:S(2)}) collective-permute-start(bf16[64,2048]{1,0:T(8,128)(2,1)} %get-tuple-element.124), channel_id=1, source_target_pairs={{0,16},{2,18},{4,20},{6,22},{8,24},{10,26},{12,28},{14,30},{16,0},... | collective-permute-start | bytes 786440 | tf_op jit(solution)/shard_map/ppermute | solution.py:456
  391.4 15.7 %collective-permute-start.7 = (bf16[512,512]{1,0:T(8,128)(2,1)S(1)}, bf16[512,512]{1,0:T(8,128)(2,1)S(1)}, u32[]{:S(2)}, u32[]{:S(2)}) collective-permute-start(bf16[512,512]{1,0:T(8,128)(2,1)S(1)} %copy-done.35), channel_id=1, source_target_pairs={{0,1},{1,0},{2,3},{3,2},{4,5},{5,4},{6,7},{7,6},{8,9},{9,8},{10,11... | collective-permute-start | bytes 1572872 | tf_op jit(solution)/shard_map/ppermute | solution.py:415
  392.5 23.8 %collective-permute-start.6 = (bf16[512,512]{1,0:T(8,128)(2,1)S(1)}, bf16[512,512]{1,0:T(8,128)(2,1)S(1)}, u32[]{:S(2)}, u32[]{:S(2)}) collective-permute-start(bf16[512,512]{1,0:T(8,128)(2,1)S(1)} %copy-done.34), channel_id=1, source_target_pairs={{0,1},{1,0},{2,3},{3,2},{4,5},{5,4},{6,7},{7,6},{8,9},{9,8},{10,11... | collective-permute-start | bytes 1572872 | tf_op jit(solution)/shard_map/ppermute | solution.py:415
  393.5 25.4 %collective-permute-start.14 = (bf16[64,1024]{1,0:T(8,128)(2,1)S(1)}, bf16[64,1024]{1,0:T(8,128)(2,1)S(1)}, u32[]{:S(2)}, u32[]{:S(2)}) collective-permute-start(bf16[64,1024]{1,0:T(8,128)(2,1)S(1)} %get-tuple-element.122), channel_id=1, source_target_pairs={{0,24},{2,26},{4,28},{6,30},{8,0},{10,2},{12,4},{14,6},{16,8},{18,... | collective-permute-start | bytes 393224 | tf_op jit(solution)/shard_map/ppermute | solution.py:456
  393.8 27.1 %collective-permute-start.13 = (bf16[64,1024]{1,0:T(8,128)(2,1)S(1)}, bf16[64,1024]{1,0:T(8,128)(2,1)S(1)}, u32[]{:S(2)}, u32[]{:S(2)}) collective-permute-start(bf16[64,1024]{1,0:T(8,128)(2,1)S(1)} %get-tuple-element.121), channel_id=1, source_target_pairs={{0,16},{2,18},{4,20},{6,22},{8,24},{10,26},{12,28},{14,30},{16,0},... | collective-permute-start | bytes 393224 | tf_op jit(solution)/shard_map/ppermute | solution.py:456
  395.9 25.6 %collective-permute-start.12 = (bf16[64,1024]{1,0:T(8,128)(2,1)S(1)}, bf16[64,1024]{1,0:T(8,128)(2,1)S(1)}, u32[]{:S(2)}, u32[]{:S(2)}) collective-permute-start(bf16[64,1024]{1,0:T(8,128)(2,1)S(1)} %get-tuple-element.120), channel_id=1, source_target_pairs={{0,8},{2,10},{4,12},{6,14},{8,16},{10,18},{12,20},{14,22},{16,24},... | collective-permute-start | bytes 393224 | tf_op jit(solution)/shard_map/ppermute | solution.py:456
  416.3 18.4 %collective-permute-start.20 = (bf16[64,2048]{1,0:T(8,128)(2,1)S(1)}, bf16[64,2048]{1,0:T(8,128)(2,1)S(1)}, u32[]{:S(2)}, u32[]{:S(2)}) collective-permute-start(bf16[64,2048]{1,0:T(8,128)(2,1)S(1)} %get-tuple-element.136), channel_id=1, source_target_pairs={{0,16},{2,18},{4,20},{6,22},{8,24},{10,26},{12,28},{14,30},{16,0},... | collective-permute-start | bytes 786440 | tf_op jit(solution)/shard_map/ppermute | solution.py:456
  419.0 15.7 %collective-permute-start.19 = (bf16[64,2048]{1,0:T(8,128)(2,1)S(1)}, bf16[64,2048]{1,0:T(8,128)(2,1)S(1)}, u32[]{:S(2)}, u32[]{:S(2)}) collective-permute-start(bf16[64,2048]{1,0:T(8,128)(2,1)S(1)} %get-tuple-element.135), channel_id=1, source_target_pairs={{0,8},{2,10},{4,12},{6,14},{8,16},{10,18},{12,20},{14,22},{16,24},... | collective-permute-start | bytes 786440 | tf_op jit(solution)/shard_map/ppermute | solution.py:456
  420.9 16.8 %collective-permute-start.10 = (bf16[4,2,64,1536]{3,2,0,1:T(8,128)(2,1)S(1)}, bf16[4,2,64,1536]{3,2,0,1:T(8,128)(2,1)S(1)}, u32[]{:S(2)}, u32[]{:S(2)}) collective-permute-start(bf16[4,2,64,1536]{3,2,0,1:T(8,128)(2,1)S(1)} %copy_bitcast_fusion.1), channel_id=1, source_target_pairs={{0,2},{2,0},{4,6},{6,4},{8,10},{10,8},{12,14},{14,12},{16,18},{18,... | collective-permute-start | bytes 4718600 | tf_op jit(solution)/shard_map/ppermute | solution.py:456
  445.6 21.1 %collective-permute-start.11 = (bf16[4,2,64,1536]{3,2,0,1:T(8,128)(2,1)S(1)}, bf16[4,2,64,1536]{3,2,0,1:T(8,128)(2,1)S(1)}, u32[]{:S(2)}, u32[]{:S(2)}) collective-permute-start(bf16[4,2,64,1536]{3,2,0,1:T(8,128)(2,1)S(1)} %copy_bitcast_fusion), channel_id=1, source_target_pairs={{0,2},{2,0},{4,6},{6,4},{8,10},{10,8},{12,14},{14,12},{16,18},{18,... | collective-permute-start | bytes 4718600 | tf_op jit(solution)/shard_map/ppermute | solution.py:456
  445.6 20.0 %collective-permute-start.18 = (bf16[4,64,1536]{2,1,0:T(8,128)(2,1)S(1)}, bf16[4,64,1536]{2,1,0:T(8,128)(2,1)S(1)}, u32[]{:S(2)}, u32[]{:S(2)}) collective-permute-start(bf16[4,64,1536]{2,1,0:T(8,128)(2,1)S(1)} %fusion.26), channel_id=1, source_target_pairs={{0,4},{2,6},{4,0},{6,2},{8,12},{10,14},{12,8},{14,10},{16,20},{18,... | collective-permute-start | bytes 2359304 | tf_op jit(solution)/shard_map/ppermute | solution.py:456
  503.9 18.3 %collective-permute-start.23 = (bf16[64,1536]{1,0:T(8,128)(2,1)}, bf16[64,1536]{1,0:T(8,128)(2,1)S(1)}, u32[]{:S(2)}, u32[]{:S(2)}) collective-permute-start(bf16[64,1536]{1,0:T(8,128)(2,1)} %get-tuple-element.139), channel_id=1, source_target_pairs={{0,16},{2,18},{4,20},{6,22},{8,24},{10,26},{12,28},{14,30},{16,0},... | collective-permute-start | bytes 589832 | tf_op jit(solution)/shard_map/ppermute | solution.py:456
  504.8 17.5 %collective-permute-start.22 = (bf16[64,1536]{1,0:T(8,128)(2,1)}, bf16[64,1536]{1,0:T(8,128)(2,1)S(1)}, u32[]{:S(2)}, u32[]{:S(2)}) collective-permute-start(bf16[64,1536]{1,0:T(8,128)(2,1)} %get-tuple-element.138), channel_id=1, source_target_pairs={{0,8},{2,10},{4,12},{6,14},{8,16},{10,18},{12,20},{14,22},{16,24},... | collective-permute-start | bytes 589832 | tf_op jit(solution)/shard_map/ppermute | solution.py:456
  505.4 20.6 %collective-permute-start.26 = (bf16[4,64,1536]{2,1,0:T(8,128)(2,1)}, bf16[4,64,1536]{2,1,0:T(8,128)(2,1)S(1)}, u32[]{:S(2)}, u32[]{:S(2)}) collective-permute-start(bf16[4,64,1536]{2,1,0:T(8,128)(2,1)} %fusion.25), channel_id=1, source_target_pairs={{0,4},{2,6},{4,0},{6,2},{8,12},{10,14},{12,8},{14,10},{16,20},{18,... | collective-permute-start | bytes 2359304 | tf_op jit(solution)/shard_map/ppermute | solution.py:456
  531.5 15.1 %collective-permute-start.28 = (bf16[64,1536]{1,0:T(8,128)(2,1)S(1)}, bf16[64,1536]{1,0:T(8,128)(2,1)S(1)}, u32[]{:S(2)}, u32[]{:S(2)}) collective-permute-start(bf16[64,1536]{1,0:T(8,128)(2,1)S(1)} %get-tuple-element.167), channel_id=1, source_target_pairs={{0,16},{2,18},{4,20},{6,22},{8,24},{10,26},{12,28},{14,30},{16,0},... | collective-permute-start | bytes 589832 | tf_op jit(solution)/shard_map/ppermute | solution.py:456
  (49 other events, 1000.5 us)

commit v4 on v3

--- a/solution.py
+++ b/solution.py
@@ -209,102 +209,6 @@
         compiler_params=pltpu.CompilerParams(collective_id=1, has_side_effects=True),
         name="modulation_forward",
     )(lifted, w_ada, bias)
-
-
-def modulation_backward(d_part, bias_part, lf, w_ada, n, s):
-    rows, E = w_ada.shape
-    m = bias_part.shape[-1]
-
-    def kern(d_ref, bp_ref, lf_ref, w_ref, gw_ref, gb_ref, dl_ref, bo_ref, dx, dm, lp, bx, bs, bsx, send, recv, xsend, xrecv):
-        me, x = lax.axis_index("fsdp"), lax.axis_index("seq")
-        peers = fsdp_peers(n, me)
-        xpeers = [lax.rem(x + k, s) for k in range(1, s)]
-        bar = pltpu.get_barrier_semaphore()
-        for p in peers:
-            pl.semaphore_signal(bar, inc=1, device_id={"fsdp": p}, device_id_type=MESH)
-        for p in xpeers:
-            pl.semaphore_signal(bar, inc=1, device_id={"seq": p}, device_id_type=MESH)
-        pl.semaphore_wait(bar, n - 1 + s - 1)
-
-        def cp(i, k, src, dst):
-            r = pltpu.make_async_remote_copy(
-                src_ref=src,
-                dst_ref=dst,
-                send_sem=send.at[i, k],
-                recv_sem=recv.at[i, k],
-                device_id={"fsdp": peers[k]},
-                device_id_type=MESH,
-            )
-            r.start()
-            return r
-
-        def cpx(i, k, src, dst):
-            r = pltpu.make_async_remote_copy(
-                src_ref=src,
-                dst_ref=dst,
-                send_sem=xsend.at[i, k],
-                recv_sem=xrecv.at[i, k],
-                device_id={"seq": xpeers[k]},
-                device_id_type=MESH,
-            )
-            r.start()
-            return r
-
-        q0 = [cpx(0, k, d_ref, dx.at[x]) for k in range(s - 1)]
-        q1 = [cp(0, k, bp_ref.at[p], bx.at[me]) for k, p in enumerate(peers)]
-        dx[x] = d_ref[...]
-        bx[me] = bp_ref[me]
-        for r in q0:
-            r.wait_recv()
-        dm[me] = jnp.sum(dx[...], axis=0).astype(bf16).astype(f32)
-        q2 = [cp(1, k, dm.at[me], dm.at[me]) for k, p in enumerate(peers)]
-        for r in q1:
-            r.wait_recv()
-        bs[...] = jnp.sum(bx[...], axis=0)
-        bsx[x] = bs[...]
-        q3 = [cpx(1, k, bs, bsx.at[x]) for k in range(s - 1)]
-        for r in q2:
-            r.wait_recv()
-        dmod = dm[...].reshape(n, E).astype(bf16)
-        lp[...] = nt(dmod, w_ref[...]).reshape(n, 1, rows)
-        dl_ref[me] = lp[me]
-        q4 = [cp(2, k, lp.at[p], dl_ref.at[me]) for k, p in enumerate(peers)]
-        gw_ref[...] = tn(lf_ref[...].reshape(n, rows).astype(bf16), dmod)
-        gb_ref[...] = jnp.sum(dm[...], axis=0)
-        for r in q3:
-            r.wait_recv()
-        bo_ref[...] = jnp.sum(bsx[...], axis=0)
-        for r in q4:
-            r.wait_recv()
-        for r in q0 + q1 + q2 + q3 + q4:
-            r.wait_send()
-
-    vm = pl.BlockSpec(memory_space=pltpu.VMEM)
-    return pl.pallas_call(
-        kern,
-        out_shape=[
-            jax.ShapeDtypeStruct((rows, E), f32),
-            jax.ShapeDtypeStruct((1, E), f32),
-            jax.ShapeDtypeStruct((n, 1, rows), f32),
-            jax.ShapeDtypeStruct((1, m), f32),
-        ],
-        in_specs=[vm] * 4,
-        out_specs=[vm] * 4,
-        scratch_shapes=[
-            pltpu.VMEM((s, 1, E), f32),
-            pltpu.VMEM((n, 1, E), f32),
-            pltpu.VMEM((n, 1, rows), f32),
-            pltpu.VMEM((n, 1, m), f32),
-            pltpu.VMEM((1, m), f32),
-            pltpu.VMEM((s, 1, m), f32),
-            pltpu.SemaphoreType.DMA((3, n - 1)),
-            pltpu.SemaphoreType.DMA((3, n - 1)),
-            pltpu.SemaphoreType.DMA((2, s - 1)),
-            pltpu.SemaphoreType.DMA((2, s - 1)),
-        ],
-        compiler_params=pltpu.CompilerParams(collective_id=2, has_side_effects=True),
-        name="modulation_backward",
-    )(d_part, bias_part, lf, w_ada)
 
 
 def head_mask(ref_shape, h):
@@ -358,154 +262,8 @@
     )(q, *ks, *vs)
 
 
-def attend_backward_kernel(n, q_ref, e_ref, lse_ref, *refs):
-    k_refs, v_refs = refs[:n], refs[n : 2 * n]
-    dq_ref, dk_refs, dv_refs = refs[2 * n], refs[2 * n + 1 : 3 * n + 1], refs[3 * n + 1 :]
-    q, e = q_ref[...] * bf16(HD**-0.5), e_ref[...]
-    dqt = None
-    dks, dvs = [None] * n, [None] * n
-    for h in range(2):
-        qh, eh = pick(q, h), pick(e, h)
-        lse = lse_ref[0, h : h + 1, :]
-        probs, dprobs, cross = [], [], None
-        for j in range(n):
-            p = jnp.exp(nt(k_refs[j][...], qh) - lse)
-            dp = nt(v_refs[j][...], eh)
-            part = (p * dp).sum(axis=0, keepdims=True)
-            cross = part if cross is None else cross + part
-            dv = nn(p.astype(bf16), eh)
-            dvs[j] = dv if dvs[j] is None else dvs[j] + dv
-            probs.append(p)
-            dprobs.append(dp)
-        for j in range(n):
-            ds = (probs[j] * (dprobs[j] - cross)).astype(bf16)
-            dk = nn(ds, qh)
-            dks[j] = dk if dks[j] is None else dks[j] + dk
-            t = tn(pick(k_refs[j][...], h), ds)
-            dqt = t if dqt is None else dqt + t
-    dq_ref[...] = (dqt * (HD**-0.5)).T.astype(bf16)
-    for j in range(n):
-        dk_refs[j][...] = dks[j].astype(dk_refs[j].dtype)
-        dv_refs[j][...] = dvs[j].astype(dv_refs[j].dtype)
-
-
-def attend_backward(q, e, lse, ks, vs):
-    T, D = q.shape
-    n = len(ks)
-
-    def col(rows):
-        return pl.BlockSpec((rows, 128), lambda i: (0, i))
-
-    keys = sum(k.shape[0] for k in ks)
-    cols = [col(k.shape[0]) for k in ks]
-    kv = [jax.ShapeDtypeStruct(k.shape, f32 if j == 0 else bf16) for j, k in enumerate(ks)]
-    res = pl.pallas_call(
-        partial(attend_backward_kernel, n),
-        grid=(D // 128,),
-        in_specs=[col(T), col(T), pl.BlockSpec((1, 2, T), lambda i: (i, 0, 0))] + cols * 2,
-        out_specs=[col(T)] + cols * 2,
-        out_shape=[jax.ShapeDtypeStruct((T, D), bf16)] + kv * 2,
-        cost_estimate=pl.CostEstimate(flops=30 * T * keys * D, bytes_accessed=8 * (T + keys) * D, transcendentals=0),
-        name="attend_backward",
-    )(q, e, lse, *ks, *vs)
-    return res[0], res[1 : n + 1], res[n + 1 :]
-
-
 def seq_shift(value, k, s):
     return lax.ppermute(value, "seq", [(i, (i + k) % s) for i in range(s)])
-
-
-def tie(*values):
-    return lax.optimization_barrier(values)
-
-
-class Exchange:
-    def __init__(self, grad, n, s):
-        A, B = grid_of(n)
-        self.A, self.B, self.s = A, B, s
-        self.into = None
-        if grad.ndim == 2:
-            self.grad = grad.reshape(A, B, 2, -1, grad.shape[1])
-        me = lax.axis_index("fsdp")
-        self.a, self.b, self.c = me // (2 * B), (me // 2) % B, me % 2
-
-    @staticmethod
-    def halved(grad, n, s):
-        ex = Exchange(grad, n, s)
-        ex.half = grad.reshape((ex.A, ex.B) + grad.shape[1:])
-        return ex
-
-    @staticmethod
-    def summed(grad, n, s):
-        ex = Exchange(grad[None], n, s)
-        ex.total, ex.a, ex.from_a = grad[None], 0, []
-        return ex
-
-    def shift(self, value, da, db, dc):
-        A, B = self.A, self.B
-
-        def at(a, b, c):
-            return (a * B + b) * 2 + c
-
-        pairs = [
-            (at(a, b, c), at((a + da) % A, (b + db) % B, (c + dc) % 2))
-            for a in range(A)
-            for b in range(B)
-            for c in range(2)
-        ]
-        return lax.ppermute(value, "fsdp", pairs)
-
-    def take(self, value, index, axis):
-        return lax.dynamic_index_in_dim(value, index, axis, keepdims=False)
-
-    def c_send(self):
-        self.out = [self.take(self.grad, 1 - self.c, 2)]
-        return self.out
-
-    def c_start(self, out):
-        self.into = self.shift(out[0], 0, 0, 1)
-
-    def b_sum(self, index):
-        if self.into is None:
-            return self.take(self.half, index, 1).astype(f32)
-        mine = self.take(self.take(self.grad, self.c, 2), index, 1)
-        return mine.astype(f32) + self.take(self.into, index, 1).astype(f32)
-
-    def b_send(self):
-        return [self.b_sum((self.b + k) % self.B).astype(bf16) for k in range(1, self.B)]
-
-    def b_start(self, out):
-        self.from_b = [self.shift(v, 0, k + 1, 0) for k, v in enumerate(out)]
-
-    def a_send(self):
-        total = self.b_sum(self.b)
-        for v in self.from_b:
-            total = total + v.astype(f32)
-        self.total = total
-        return [self.take(total, (self.a + k) % self.A, 0).astype(bf16) for k in range(1, self.A)]
-
-    def a_start(self, out):
-        self.from_a = [self.shift(v, k + 1, 0, 0) for k, v in enumerate(out)]
-
-    def x_send(self):
-        total = self.take(self.total, self.a, 0).astype(f32)
-        for v in self.from_a:
-            total = total + v.astype(f32)
-        if self.s != 2:
-            self.total = lax.psum(total, "seq")
-            return []
-        self.total = total.astype(bf16)
-        return [self.total]
-
-    def x_start(self, out):
-        if self.s == 2:
-            self.from_x = seq_shift(out[0], 1, 2)
-            self.total = out[0]
-
-    def result(self):
-        if self.s != 2:
-            return self.total
-        return self.total.astype(f32) + self.from_x.astype(f32)
 
 
 def remote(src, dst, send, recv, device):
@@ -799,16 +557,424 @@
     )(middle, branch, attn, g, vectors, b_fc1.reshape(J, 1, W), proj_w, w1, w2)
 
 
+class RowSum:
+    @staticmethod
+    def scratch(U, r, W, A, B, cores):
+        dma = pltpu.SemaphoreType.DMA
+        shapes = [
+            pltpu.VMEM((U, B - 1, A, r, W), bf16), pltpu.VMEM((U, A - 1, r, W), bf16),
+            pltpu.VMEM((U, A - 1, r, W), bf16), pltpu.VMEM((U, r, W), bf16), pltpu.VMEM((U, r, W), bf16),
+            dma((U, B - 1)), dma((U, B - 1)), dma((U, A - 1)), dma((U, A - 1)), dma((U,)), dma((U,)),
+        ]
+        if cores:
+            shapes += [
+                pltpu.VMEM((U, A * B, r, W), bf16), pltpu.VMEM((U, B - 1, A, r, W), bf16), dma((U,)), dma((U,)),
+            ]
+        return shapes
+
+    def __init__(self, at, s, peer, refs, grad=None, half=None):
+        self.at, self.s, self.peer = at, s, peer
+        self.grad, self.half = grad, half
+        self.yr, self.zs, self.zr, self.xs, self.xr = refs[:5]
+        self.yss, self.yrs, self.zss, self.zrs, self.xss, self.xrs = refs[5:11]
+        if grad is not None:
+            self.cr, self.ys, self.css, self.crs = refs[11:]
+
+    def c_copy(self, u):
+        return remote(
+            self.grad.at[u, :, 1 - self.at.c], self.cr.at[u], self.css.at[u], self.crs.at[u], self.at.sibling()
+        )
+
+    def y_source(self, u, m):
+        return self.ys.at[u, m]
+
+    def y_copy(self, u, m):
+        src = self.y_source(u, m)
+        return remote(src, self.yr.at[u, m], self.yss.at[u, m], self.yrs.at[u, m], self.at.at_b(m + 1))
+
+    def z_copy(self, u, k):
+        return remote(self.zs.at[u, k], self.zr.at[u, k], self.zss.at[u, k], self.zrs.at[u, k], self.at.at_a(k + 1))
+
+    def x_copy(self, u):
+        return remote(self.xs.at[u], self.xr.at[u], self.xss.at[u], self.xrs.at[u], self.peer)
+
+    def chip(self, u, a, b):
+        j = a * self.at.B + b
+        return add32(self.grad[u, j, self.at.c], self.cr[u, j])
+
+    def own(self, u, a):
+        base = self.chip(u, a, self.at.b) if self.half is None else self.half(u, a)
+        return add32(base, *[self.yr[u, m, a] for m in range(self.at.B - 1)])
+
+    def send_y(self, u):
+        self.c_copy(u).wait()
+        for m in range(self.at.B - 1):
+            b = lax.rem(self.at.b + m + 1, self.at.B)
+            for a in range(self.at.A):
+                self.ys[u, m, a] = self.chip(u, a, b).astype(bf16)
+            self.y_copy(u, m).start()
+
+    def send_z(self, u):
+        for m in range(self.at.B - 1):
+            self.y_copy(u, m).wait()
+        for k in range(self.at.A - 1):
+            self.zs[u, k] = self.own(u, lax.rem(self.at.a + k + 1, self.at.A)).astype(bf16)
+            self.z_copy(u, k).start()
+
+    def send_x(self, u):
+        for k in range(self.at.A - 1):
+            self.z_copy(u, k).wait()
+        total = add32(self.own(u, self.at.a), *[self.zr[u, k] for k in range(self.at.A - 1)])
+        if self.s != 2:
+            return total
+        self.xs[u] = total.astype(bf16)
+        self.x_copy(u).start()
+        return None
+
+    def finish(self, u):
+        self.x_copy(u).wait()
+        return add32(self.xs[u], self.xr[u])
+
+
+def attention_and_sums(
+    q, ks, vs, d_attn, lse, hidden, tokens, scale, d_middle, w_qkv, half_fc1, grad_proj, sum_fc2, sums, bias_fc1, lf, w_ada, n, s
+):
+    T, D = q.shape
+    FF = half_fc1.shape[-1]
+    A, B = grid_of(n)
+    J, r1, r2 = A * B, D // n, FF // n
+    GW = 256
+    U = D // GW
+    F = FF // U
+    E = 6 * D
+    RB = min(T, 64)
+    rows_a = D // n
+    m_bias = [2 * D // n, D // n, FF // n, D // n]
+    starts = [0, 2 * D, 3 * D, 3 * D + FF]
+    NBIAS = 4 * D + FF
+    blocks = [max(v, 128) for v in m_bias]
+    offs = [sum(blocks[:i]) for i in range(4)]
+    M = sum(blocks)
+    nq = len(RowSum.scratch(U, r1, 3 * GW, A, B, True))
+    nf = len(RowSum.scratch(U, r1, F, A, B, False))
+
+    def kern(*refs):
+        it = iter(refs)
+
+        def take(count):
+            return [next(it) for _ in range(count)]
+
+        (q_ref,) = take(1)
+        k_refs, v_refs = take(s), take(s)
+        e_ref, lse_ref, h_ref, tok_ref, sc_ref, dmid_ref, w_ref, f1_ref, gp_ref, f2_ref, sum_ref, bf_ref, lf_ref, wa_ref = take(14)
+        gt_ref, oq_ref, op_ref, o1_ref, o2_ref, gw_ref, gb_ref, dl_ref, bo_ref = take(9)
+        h1t, dqg, kvl, kvs, kvr, dg, gq, wq, f1o, x2 = take(10)
+        dh1 = gt_ref
+        wsem, fsem, kss, krs, x2s, x2r = take(6)
+        scr_q, scr_p, scr_f = take(nq), take(nq), take(nf)
+        dx, dm, lp, bsum, bx, bsx = take(6)
+        asend, arecv, lsend, lrecv, bsend, brecv, xsend, xrecv = take(8)
+
+        at = Place(n)
+        me, x = at.me, lax.axis_index("seq")
+        peers = fsdp_peers(n, me)
+
+        def seq_dev(k):
+            return {"seq": lax.rem(x + k, s)}
+
+        greet([{"fsdp": p} for p in peers] + [seq_dev(k) for k in range(1, s)])
+        other = seq_dev(1)
+        sq = RowSum(at, s, other, scr_q, grad=gq)
+        sp = RowSum(at, s, other, scr_p, grad=gp_ref)
+        sf = RowSum(at, s, other, scr_f, half=lambda u, a: f1o[u, a])
+
+        def f_source(u, m):
+            b = lax.rem(at.b + m + 1, B)
+            return f1_ref.at[:, b, :, pl.ds(pl.multiple_of(u * F, F), F)]
+
+        sf.y_source = f_source
+        own_f = [
+            pltpu.make_async_copy(f1_ref.at[:, at.b, :, pl.ds(u * F, F)], f1o.at[u], fsem.at[u]) for u in range(U)
+        ]
+        sp.c_copy(0).start()
+        for u in range(U):
+            for m in range(B - 1):
+                sf.y_copy(u, m).start()
+        if s == 2:
+            x2_copy = remote(f2_ref, x2, x2s, x2r, other)
+            x2_copy.start()
+        for o in own_f:
+            o.start()
+
+        def h_copy(i):
+            k = i % 3
+            return pltpu.make_async_copy(
+                h_ref.at[:, pl.ds(i * GW, GW)], dg.at[:, pl.ds(k * GW, GW)], wsem.at[k]
+            )
+
+        for i in range(min(U, 3)):
+            h_copy(i).start()
+        for i in range(U):
+            h_copy(i).wait()
+            k = i % 3
+            h1t[i * GW : (i + 1) * GW, :] = dg[:, k * GW : (k + 1) * GW].T
+            if i + 3 < U:
+                h_copy(i + 3).start()
+        dh1[...] = jnp.zeros_like(dh1)
+        for o in own_f:
+            o.wait()
+
+        def w_copy(u, i):
+            lo = pl.multiple_of(i * D + u * GW, GW)
+            return pltpu.make_async_copy(w_ref.at[:, pl.ds(lo, GW)], wq.at[i], wsem.at[i])
+
+        def kv_copy(u, k):
+            return remote(kvs.at[u, k - 1], kvr.at[u, k - 1], kss.at[u, k - 1], krs.at[u, k - 1], seq_dev(s - k))
+
+        def attend(u):
+            slot = lax.rem(u, 2)
+            for o in range(2):
+                pair = u * 2 + o
+                cols = pl.ds(pl.multiple_of(pair * 128, 128), 128)
+                here = slice(o * 128, o * 128 + 128)
+                qv, e = q_ref[:, cols] * bf16(HD**-0.5), e_ref[:, cols]
+                dqt, dks, dvs = None, [None] * s, [None] * s
+                for h in range(2):
+                    qh, eh = pick(qv, h), pick(e, h)
+                    total = lse_ref[pair, h : h + 1, :]
+                    probs, dprobs, cross = [], [], None
+                    for j in range(s):
+                        p = jnp.exp(nt(k_refs[j][:, cols], qh) - total)
+                        dp = nt(v_refs[j][:, cols], eh)
+                        part = (p * dp).sum(axis=0, keepdims=True)
+                        cross = part if cross is None else cross + part
+                        dv = nn(p.astype(bf16), eh)
+                        dvs[j] = dv if dvs[j] is None else dvs[j] + dv
+                        probs.append(p)
+                        dprobs.append(dp)
+                    for j in range(s):
+                        ds = (probs[j] * (dprobs[j] - cross)).astype(bf16)
+                        dk = nn(ds, qh)
+                        dks[j] = dk if dks[j] is None else dks[j] + dk
+                        t = tn(pick(k_refs[j][:, cols], h), ds)
+                        dqt = t if dqt is None else dqt + t
+                dqg[slot, :, here] = (dqt * (HD**-0.5)).T.astype(bf16)
+                kvl[slot, 0, :, here] = dks[0]
+                kvl[slot, 1, :, here] = dvs[0]
+                for j in range(1, s):
+                    kvs[u, j - 1, 0, :, here] = dks[j].astype(bf16)
+                    kvs[u, j - 1, 1, :, here] = dvs[j].astype(bf16)
+            for k in range(1, s):
+                kv_copy(u, k).start()
+
+        def project(u):
+            slot = lax.rem(u, 2)
+            for k in range(1, s):
+                kv_copy(u, k).wait()
+            dg[:, :GW] = dqg[slot]
+            for i in range(2):
+                lo = (i + 1) * GW
+                dg[:, lo : lo + GW] = add32(kvl[slot, i], *[kvr[u, k, i] for k in range(s - 1)]).astype(bf16)
+            part = 256 // (2 * r1)
+            for i in range(D // 256):
+                g = nn(h1t[i * 256 : (i + 1) * 256, :], dg[...]).astype(bf16)
+                gq[u, i * part : (i + 1) * part] = g.reshape(part, 2, r1, 3 * GW)
+            sq.c_copy(u).start()
+            here = pl.ds(pl.multiple_of(u * GW, GW), GW)
+            bsum[:, here] = jnp.sum(dg[:, :GW].astype(f32), axis=0, keepdims=True)
+            there = pl.ds(pl.multiple_of(D + u * GW, GW), GW)
+            bsum[:, there] = jnp.sum(dg[:, 2 * GW :].astype(f32), axis=0, keepdims=True)
+            for i in range(3):
+                w_copy(u, i).wait()
+            total = nt(dg[:, :GW], wq[0])
+            for i in range(1, 3):
+                total = total + nt(dg[:, i * GW : (i + 1) * GW], wq[i])
+            dh1[...] += total
+
+        def step(i, _):
+            @pl.when(i < U)
+            def _():
+                attend(i)
+
+            @pl.when(jnp.logical_and(i >= 1, i <= U))
+            def _():
+                project(i - 1)
+
+            @pl.when(i < U)
+            def _():
+                for k in range(3):
+                    w_copy(i, k).start()
+
+            @pl.when(i == 0)
+            def _():
+                sp.send_y(0)
+
+            @pl.when(i < U)
+            def _():
+                sf.send_z(i)
+
+            @pl.when(i >= 2)
+            def _():
+                sq.send_y(i - 2)
+
+            return 0
+
+        lax.fori_loop(0, U + 2, step, 0)
+        sp.send_z(0)
+        for u in range(U - 2):
+            sq.send_z(u)
+
+        sums = [jnp.zeros((1, D), f32), jnp.zeros((1, D), f32)]
+        scale1 = sc_ref[...]
+
+        def back(i, carry):
+            rows = pl.ds(pl.multiple_of(i * RB, RB), RB)
+            normed, rscale = normalize(tok_ref[rows, :].astype(f32))
+            dh = dh1[rows, :]
+            up = dh * (1.0 + scale1)
+            gt_ref[rows, :] = dmid_ref[rows, :] + rscale * (
+                up
+                - jnp.mean(up, axis=-1, keepdims=True)
+                - normed * jnp.mean(up * normed, axis=-1, keepdims=True)
+            )
+            return (
+                carry[0] + jnp.sum(dh, axis=0, keepdims=True),
+                carry[1] + jnp.sum(dh * normed, axis=0, keepdims=True),
+            )
+
+        shift1_sum, scale1_sum = lax.fori_loop(0, T // RB, back, tuple(sums))
+        parts = [shift1_sum, scale1_sum, sum_ref[3:4, :], sum_ref[0:1, :], sum_ref[1:2, :], sum_ref[2:3, :]]
+        for i, v in enumerate(parts):
+            dx[x, :, i * D : (i + 1) * D] = v
+        mod_x = [remote(dx.at[x], dx.at[x], xsend.at[0, k - 1], xrecv.at[0, k - 1], seq_dev(k)) for k in range(1, s)]
+        for c in mod_x:
+            c.start()
+        bsum[:, starts[1] : starts[1] + D] = sum_ref[5:6, :]
+        bsum[:, starts[2] : starts[2] + FF] = bf_ref[...]
+        bsum[:, starts[3] : starts[3] + D] = sum_ref[4:5, :]
+
+        def block(p, i):
+            lo = starts[i] + ((p * m_bias[i]) // blocks[i]) * blocks[i]
+            return bsum.at[:, pl.ds(pl.multiple_of(lo, 128), blocks[i])]
+
+        def bias_copy(k, p, i):
+            dst = bx.at[me, :, pl.ds(offs[i], blocks[i])]
+            return remote(block(p, i), dst, bsend.at[i, k], brecv.at[i, k], {"fsdp": p})
+
+        bias_out = [bias_copy(k, p, i) for k, p in enumerate(peers) for i in range(4)]
+        for c in bias_out:
+            c.start()
+        for i in range(4):
+            lo = starts[i] + ((me * m_bias[i]) // blocks[i]) * blocks[i]
+            bx[me, :, offs[i] : offs[i] + blocks[i]] = bsum[:, pl.ds(pl.multiple_of(lo, 128), blocks[i])]
+
+        for u in range(U):
+            if s == 2:
+                sf.send_x(u)
+            else:
+                o1_ref[:, u * F : (u + 1) * F] = sf.send_x(u)
+        sq.send_z(U - 2)
+        for c in mod_x:
+            c.wait()
+        dm[me] = jnp.sum(dx[...], axis=0).astype(bf16).astype(f32)
+        mod_all = [remote(dm.at[me], dm.at[me], asend.at[k], arecv.at[k], {"fsdp": p}) for k, p in enumerate(peers)]
+        for c in mod_all:
+            c.start()
+        sq.send_z(U - 1)
+        for c in bias_out:
+            c.wait()
+        bsx[x] = jnp.sum(bx[...], axis=0)
+        bias_x = [remote(bsx.at[x], bsx.at[x], xsend.at[1, k - 1], xrecv.at[1, k - 1], seq_dev(k)) for k in range(1, s)]
+        for c in bias_x:
+            c.start()
+        if s == 2:
+            sp.send_x(0)
+        else:
+            op_ref[...] = sp.send_x(0)
+        for c in mod_all:
+            c.wait()
+        dmod = dm[...].reshape(n, E).astype(bf16)
+        lp[...] = nt(dmod, wa_ref[...]).reshape(n, 1, rows_a)
+        dl_ref[me] = lp[me]
+        lift = [remote(lp.at[p], dl_ref.at[me], lsend.at[k], lrecv.at[k], {"fsdp": p}) for k, p in enumerate(peers)]
+        for c in lift:
+            c.start()
+        gw_ref[...] = tn(lf_ref[...].reshape(n, rows_a).astype(bf16), dmod)
+        gb_ref[...] = jnp.sum(dm[...], axis=0)
+
+        def put_q(u, value):
+            for i in range(3):
+                oq_ref[:, i * D + u * GW : i * D + (u + 1) * GW] = value[:, i * GW : (i + 1) * GW]
+
+        for u in range(U):
+            value = sq.send_x(u)
+            if s != 2:
+                put_q(u, value)
+        if s == 2:
+            x2_copy.wait()
+            o2_ref[...] = add32(f2_ref[...], x2[...])
+            for u in range(U):
+                o1_ref[:, u * F : (u + 1) * F] = sf.finish(u)
+            op_ref[...] = sp.finish(0)
+            for u in range(U):
+                put_q(u, sq.finish(u))
+        else:
+            o2_ref[...] = f2_ref[...].astype(f32)
+        for c in bias_x:
+            c.wait()
+        bo_ref[...] = jnp.sum(bsx[...], axis=0)
+        for c in lift:
+            c.wait()
+
+    vm, hbm = pl.BlockSpec(memory_space=pltpu.VMEM), pl.BlockSpec(memory_space=pl.ANY)
+    sds, dma = jax.ShapeDtypeStruct, pltpu.SemaphoreType.DMA
+    res = pl.pallas_call(
+        kern,
+        out_shape=[
+            sds((T, D), f32), sds((r1, 3 * D), f32), sds((r1, D), f32), sds((r1, FF), f32), sds((r2, D), f32),
+            sds((rows_a, E), f32), sds((1, E), f32), sds((n, 1, rows_a), f32), sds((1, M), f32),
+        ],
+        in_specs=[vm] * (3 + 2 * s) + [hbm] + [vm] * 3 + [hbm, hbm] + [vm] * 6,
+        out_specs=[vm] * 9,
+        scratch_shapes=[
+            pltpu.VMEM((D, T), bf16), pltpu.VMEM((2, T, GW), bf16),
+            pltpu.VMEM((2, 2, T, GW), f32), pltpu.VMEM((U, s - 1, 2, T, GW), bf16),
+            pltpu.VMEM((U, s - 1, 2, T, GW), bf16), pltpu.VMEM((T, 3 * GW), bf16),
+            pltpu.VMEM((U, J, 2, r1, 3 * GW), bf16), pltpu.VMEM((3, D, GW), bf16),
+            pltpu.VMEM((U, A, r1, F), bf16), pltpu.VMEM((r2, D), bf16),
+            dma((3,)), dma((U,)), dma((U, s - 1)), dma((U, s - 1)), dma(()), dma(()),
+        ]
+        + RowSum.scratch(U, r1, 3 * GW, A, B, True)
+        + RowSum.scratch(1, r1, D, A, B, True)
+        + RowSum.scratch(U, r1, F, A, B, False)
+        + [
+            pltpu.VMEM((s, 1, E), f32), pltpu.VMEM((n, 1, E), f32), pltpu.VMEM((n, 1, rows_a), f32),
+            pltpu.VMEM((1, NBIAS), f32), pltpu.VMEM((n, 1, M), f32), pltpu.VMEM((s, 1, M), f32),
+            dma((n - 1,)), dma((n - 1,)), dma((n - 1,)), dma((n - 1,)),
+            dma((4, n - 1)), dma((4, n - 1)), dma((2, s - 1)), dma((2, s - 1)),
+        ],
+        compiler_params=pltpu.CompilerParams(
+            collective_id=4, has_side_effects=True, vmem_limit_bytes=64 * 1024 * 1024 - 65536
+        ),
+        name="attention_and_sums",
+    )(
+        q, *ks, *vs, d_attn, lse, hidden, tokens, scale, d_middle, w_qkv, half_fc1.reshape(A, B, r1, FF),
+        grad_proj.reshape(1, J, 2, r1, D), sum_fc2, sums, bias_fc1, lf, w_ada,
+    )
+    grad_tokens, t_qkv, t_proj, t_fc1, t_fc2, t_ada, ada_sums, d_lifted, bias = res
+    if s != 2:
+        t_qkv, t_proj, t_fc1, t_fc2 = lax.psum((t_qkv, t_proj, t_fc1, t_fc2), "seq")
+    me = lax.axis_index("fsdp")
+    biases = []
+    for width, wide, off in zip(m_bias, blocks, offs):
+        biases.append(lax.dynamic_slice_in_dim(bias[0, off : off + wide], (me * width) % wide, width))
+    return grad_tokens, t_qkv, t_proj, t_fc1, t_fc2, t_ada, ada_sums, d_lifted, biases
+
+
 def layer_norm(values):
     center = values - jnp.mean(values, axis=-1, keepdims=True)
     rscale = lax.rsqrt(jnp.mean(center * center, axis=-1, keepdims=True) + norm_eps)
     return (center * rscale, rscale)
-
-
-def norm_back(upstream, normed, rscale):
-    mean_up = jnp.mean(upstream, axis=-1, keepdims=True)
-    mean_cross = jnp.mean(upstream * normed, axis=-1, keepdims=True)
-    return rscale * (upstream - mean_up - normed * mean_cross)
 
 
 def on_device(
@@ -858,102 +1024,20 @@
     branch = nn(attn, proj_w) + proj_b
     middle = tokens_f + gate_one * branch
 
-    half_d = width // 2
-
-    def exchange(lhs, rhs):
-        return Exchange(tn(lhs, rhs).astype(bf16), n, s)
-
     vectors = jnp.concatenate([shift_two, scale_two, gate_two, gate_one, fc2_b, jnp.zeros((3, width), f32)], axis=0)
     result, d_middle, d_attn, sums, bias_fc1, grad_proj, half_fc1, sum_fc2 = feed_forward(
         middle, branch, attn, cotangent[0], vectors, fc1_b, proj_w, fc1_w, fc2_w, n
     )
-    d_shift_two, d_scale_two, d_gate_two, d_gate_one, bias_fc2, bias_proj = [sums[i : i + 1] for i in range(6)]
-    bias_fc1 = bias_fc1.reshape(-1)
-    fc2 = Exchange.summed(sum_fc2, n, s)
-    sum_fc2 = fc2.x_send()
-    fc2.x_start(sum_fc2)
-    half_f = fc1_w.shape[1] // 2
-    fc1a, fc1b = Exchange.halved(half_fc1[:, :, :half_f], n, s), Exchange.halved(half_fc1[:, :, half_f:], n, s)
-    proj = Exchange(grad_proj, n, s)
-    fc1a.b_start(fc1a.b_send())
-    fc1b.b_start(fc1b.b_send())
-    proj.c_start(proj.c_send())
-    halves = []
-    lo = slice(0, half_d)
-    hi = slice(half_d, width)
-
-    def attention(part):
-        heads = slice(part.start // 128, part.stop // 128)
-        grads = attend_backward(
-            queries[:, part], d_attn[:, part], lse[heads], [k[:, part] for k in ks], [v[:, part] for v in vs]
+    grad_input, total_qkv, total_proj, total_fc1, total_fc2, total_ada, sums_ada, d_lifted, total_bias = (
+        attention_and_sums(
+            queries, ks, vs, d_attn, lse, hidden_one, tokens[0], scale_one, d_middle, qkv_w, half_fc1,
+            grad_proj, sum_fc2, sums, bias_fc1.reshape(1, -1), lf, w_ada, n, s,
         )
-        return grads
-
-    def back(dk):
-        return [seq_shift(dk[k], s - k, s) for k in range(1, s)]
-
-    q1, dk1, dv1 = attention(lo)
-    q1, dk1, dv1, sa, sb = tie(q1, dk1, dv1, proj.b_send(), fc1a.a_send())
-    rk1, rv1 = back(dk1), back(dv1)
-    proj.b_start(sa)
-    fc1a.a_start(sb)
-    d_attn, q1 = tie(d_attn, q1)
-    q2, dk2, dv2 = attention(hi)
-    q2, dk2, dv2, sa, sb = tie(q2, dk2, dv2, fc1b.a_send(), proj.a_send())
-    rk2, rv2 = back(dk2), back(dv2)
-    fc1b.a_start(sa)
-    proj.a_start(sb)
-
-    def joined(q, dk, rk, dv, rv):
-        gk, gv = dk[0], dv[0]
-        for v in rk:
-            gk = gk + v.astype(f32)
-        for v in rv:
-            gv = gv + v.astype(f32)
-        return jnp.concatenate([q, gk.astype(bf16), gv.astype(bf16)], axis=1)
-
-    d1 = joined(q1, dk1, rk1, dv1, rv1)
-    qkv1 = exchange(hidden_one, d1)
-    d2, sa = tie(joined(q2, dk2, rk2, dv2, rv2), qkv1.c_send())
-    qkv1.c_start(sa)
-    qkv2 = exchange(hidden_one, d2)
-    d2, sa, sb = tie(d2, qkv1.b_send(), qkv2.c_send())
-    qkv1.b_start(sa)
-    qkv2.c_start(sb)
-    sums1, sums2 = jnp.sum(d1, axis=0, dtype=f32), jnp.sum(d2, axis=0, dtype=f32)
-    bias_qv = jnp.concatenate([sums1[:half_d], sums2[:half_d], sums1[width:], sums2[width:]])
-    d_qkv = jnp.concatenate([v[:, i * half_d : (i + 1) * half_d] for i in range(3) for v in (d1, d2)], axis=1)
-    d_hidden_one = nt(d_qkv, qkv_w)
-    d_shift_one = jnp.sum(d_hidden_one, axis=0, keepdims=True)
-    d_scale_one = jnp.sum(d_hidden_one * normed_one, axis=0, keepdims=True)
-    grad_input = d_middle + norm_back(d_hidden_one * (1.0 + scale_one), normed_one, rscale_one)
-    d_scale_one, sa, sb, sc = tie(d_scale_one, qkv2.b_send(), proj.x_send(), fc1a.x_send())
-    qkv2.b_start(sa)
-    proj.x_start(sb)
-    fc1a.x_start(sc)
-
-    d_part = jnp.concatenate(
-        [d_shift_one, d_scale_one, d_gate_one, d_shift_two, d_scale_two, d_gate_two], axis=-1
     )
-    bias_part = jnp.concatenate(
-        [bias_qv.reshape(n, -1), bias_proj.reshape(n, -1), bias_fc1.reshape(n, -1), bias_fc2.reshape(n, -1)], axis=1
-    )[:, None, :]
-    total_ada, sums_ada, d_lifted, total_bias = modulation_backward(d_part, bias_part, lf, w_ada, n, s)
     share = b_ada.shape[0]
     total_bada = lax.dynamic_slice_in_dim(sums_ada[0], lax.axis_index("fsdp") * share, share)
     grad_condition = silu_back(d_lifted.reshape(1, width))[0]
-    total_bias, sa, sb = tie(total_bias, qkv1.a_send(), fc1b.x_send())
-    qkv1.a_start(sa)
-    fc1b.x_start(sb)
-    qkv2.a_start(qkv2.a_send())
-    qkv1.x_start(qkv1.x_send())
-    qkv2.x_start(qkv2.x_send())
-    total_fc2 = fc2.result()
-    total_fc1 = jnp.concatenate([fc1a.result(), fc1b.result()], axis=1)
-    total_proj = proj.result()
-    r1, r2 = qkv1.result(), qkv2.result()
-    total_qkv = jnp.concatenate([v[:, i * half_d : (i + 1) * half_d] for i in range(3) for v in (r1, r2)], axis=1)
-    total_bqv, total_bproj, total_bfc1, total_bfc2 = [total_bias[0, edges[i] : edges[i + 1]] for i in range(4)]
+    total_bqv, total_bproj, total_bfc1, total_bfc2 = total_bias
     return (
         result[None],
         grad_input[None],

time: 562 us -> 473 us (0.84); the launches traced: 555 us -> 472 us
  Pallas kernels: 306 us -> 387 us
  waiting for transfers between devices: 107 us -> 37 us
  starting transfers between devices: 40.4 us -> 2.03 us
  local copies, waits for them, and re-layouts: 47.4 us -> 20.3 us
  other arithmetic: 28.8 us -> 8.32 us
  matrix products: 23.3 us -> 16 us
    pallas_call x3 -> x1, Pallas kernels: 54.8 us -> 136 us  [attention_and_sums(): pl.pallas_call(kern, out_shape=[sds((T, D), f32), sds((r1, 3 * D), f32),...]
    ppermute x23 -> x0, waiting for transfers between devices: 57.6 us -> none  [shift(): return lax.ppermute(value, 'fsdp', pairs)]
    ppermute x23 -> x0, starting transfers between devices: 27.9 us -> none  [shift(): return lax.ppermute(value, 'fsdp', pairs)]
    slice x12 -> x2, local copies, waits for them, and re-layouts: 18.1 us -> 2.48 us  [attention_and_sums(): bias[0, off:off + wide]]
    ppermute x12 -> x2, waiting for transfers between devices: 49.8 us -> 37 us  [seq_shift(): return lax.ppermute(value, 'seq', [(i, (i + k) % s) for i in range(s)])]
    ppermute x12 -> x2, starting transfers between devices: 12.5 us -> 2.03 us  [seq_shift(): return lax.ppermute(value, 'seq', [(i, (i + k) % s) for i in range(s)])]
    add x11 -> x0, other arithmetic: 9.66 us -> none  [the longest x5 6.64 us: a_send(): total = total + v.astype(f32)]
    dot_general x3 -> x0, matrix products: 8.13 us -> none  [the longest x2 4.13 us: tn(): lax.dot_general(a, b, (((0,), (0,)), ((), ())), preferred_element_type=f32)]
  transfers between devices with their start and end apart: 35 -> 2, of which waited for: 12 -> 2; matrix products, arithmetic and copies ran while one was open for 10% -> 2% of each run, Pallas kernels for 6% -> 0%
where the time goes in v4:
time: 473 us; the launch traced here: 472 us
  Pallas kernels  387 us (82%)
  waiting for transfers between devices  37 us (8%)
  local copies, waits for them, and re-layouts  20.3 us (4%)
  matrix products  16 us (3%)
  other arithmetic  8.32 us (2%)
    pallas_call x1, Pallas kernels, attention_and_sums(): pl.pallas_call(kern, out_shape=[sds((T, D), f32), sds((r1, 3 * D), f32),...  136 us
    pallas_call x1, Pallas kernels, gather_weights(): pl.pallas_call(kern, out_shape=[jax.ShapeDtypeStruct((A, B, 2) + w.shape,...  128 us
    pallas_call x1, Pallas kernels, feed_forward(): pl.pallas_call(kern, out_shape=[sds((T, D), bf16), sds((T, D), f32), sds(...  85.1 us
    ppermute x2, waiting for transfers between devices, seq_shift(): return lax.ppermute(value, 'seq', [(i, (i + k) % s) for i in range(s)])  37 us
    pallas_call x1, Pallas kernels, modulation_forward(): pl.pallas_call(kern, out_shape=[jax.ShapeDtypeStruct((1, E), f32), jax.Sh...  20.6 us
    pallas_call x1, Pallas kernels, attend_forward(): pl.pallas_call(partial(attend_forward_kernel, n), grid=(D // 128,), in_sp...  17.8 us
    dot_general x4, matrix products, nn(): lax.dot_general(a, b, (((1,), (0,)), ((), ())), preferred_element_type=f32)  16 us
    unnamed x27, local copies, waits for them, and re-layouts  9.63 us
  transfers between devices with their start and end apart: 2, of which 2 were waited for; matrix products, arithmetic and copies ran while one was open for 2% of the time, Pallas kernels for 0%

profile of v4, /device:TPU:0, one launch (start us, length us, event | category | flops | bytes accessed | tf_op | source)
XLA Modules:
  0.0 471.9 jit_solution(4877638842483501573)
XLA Ops:
  0.7 1.4 convert_reduce_fusion.1
  5.4 20.6 %modulation_forward.1 = (f32[1,6144]{1,0:T(1,128)}, f32[16,1,64]{2,1,0:T(1,128)}, f32[16,1,896]{2,1,0:T(1,128)}) custom-call(f32[16,1,64]{2,1,0:T(1,128)} %bitcast.56, bf16[64,6144]{1,0:T(8,128)(2,1)} %refs_18_.1, f32[1,896]{1,0:T(1,128)} %convert_element_type.35.bias_ref), custom_call_target="tpu_custom_call" | custom-call | tf_op jit(solution)/shard_map/modulation_forward/pallas_call | solution.py:194
  28.8 1.4 convert_reduce_fusion
  31.2 127.8 %gather_weights.1 = (bf16[4,2,2,64,3072]{4,3,2,1,0:T(8,128)(2,1)}, bf16[4,2,2,64,1024]{4,3,2,1,0:T(8,128)(2,1)}, bf16[4,2,2,64,4096]{4,3,2,1,0:T(8,128)(2,1)}, bf16[4,2,2,256,1024]{4,3,2,1,0:T(8,128)(2,1)}) custom-call(bf16[64,3072]{1,0:T(8,128)(2,1)} %refs_0_.1, bf16[64,1024]{1,0:T(8,128)(2,1)} %refs_1_.1, bf16[64,4096]{1,0:T(8,128)(2,1)} %refs_2_.1, ...), custom_call_target="tpu_custom_call" | custom-call | tf_op jit(solution)/shard_map/gather_weights/pallas_call | solution.py:131
  159.0 3.8 add_convert_fusion.refs_2_.refs_3_
  162.8 1.1 collective-permute-start.1
  163.9 3.8 fusion.16.refs_0_.refs_1_
  170.3 3.8 add_convert_fusion.1.q_ref.refs_0_
  174.1 15.1 %collective-permute-done.1.refs_3_.refs_4_ = bf16[512,1024]{1,0:T(8,128)(2,1)} collective-permute-done((bf16[512,1024]{1,0:T(8,128)(2,1)}, bf16[512,1024]{1,0:T(8,128)(2,1)}, u32[]{:S(2)}, u32[]{:S(2)}) %collective-permute-start.1) | collective-permute-done | bytes 1048608 | tf_op jit(solution)/shard_map/ppermute | solution.py:266
  189.2 21.9 %collective-permute-done.refs_1_.refs_2_ = bf16[512,1024]{1,0:T(8,128)(2,1)} collective-permute-done((bf16[512,1024]{1,0:T(8,128)(2,1)}, bf16[512,1024]{1,0:T(8,128)(2,1)}, u32[]{:S(2)}, u32[]{:S(2)}) %collective-permute-start) | collective-permute-done | bytes 1048608 | tf_op jit(solution)/shard_map/ppermute | solution.py:266
  211.0 17.8 %attend_forward.1 = (bf16[512,1024]{1,0:T(8,128)(2,1)}, f32[8,2,512]{2,1,0:T(2,128)}) custom-call(bf16[512,1024]{1,0:T(8,128)(2,1)} %add_convert_fusion.1.q_ref.refs_0_, bf16[512,1024]{1,0:T(8,128)(2,1)} %fusion.16.refs_0_.refs_1_, bf16[512,1024]{1,0:T(8,128)(2,1)} %collective-permute-done.refs_1_.refs_2_, ...), custom_call_target="tpu_custom_call" | custom-call | flops 8589934592 | bytes 6291456 | tf_op jit(solution)/shard_map/attend_forward/pallas_call | solution.py:254
  228.8 4.5 convert_add_fusion
  233.3 85.1 %feed_forward.1 = (bf16[512,1024]{1,0:T(8,128)(2,1)}, f32[512,1024]{1,0:T(8,128)}, bf16[512,1024]{1,0:T(8,128)(2,1)}, f32[8,1024]{1,0:T(8,128)}, f32[8,1,512]{2,...) custom-call(f32[512,1024]{1,0:T(8,128)} %get-tuple-element.81.mid_ref, ...), custom_call_target="tpu_custom_call" | custom-call | tf_op jit(solution)/shard_map/feed_forward/pallas_call | solution.py:534
  318.5 136.2 %attention_and_sums.1 = (f32[512,1024]{1,0:T(8,128)}, f32[64,3072]{1,0:T(8,128)}, f32[64,1024]{1,0:T(8,128)}, f32[64,4096]{1,0:T(8,128)}, f32[256,1024]{1,0:T(8,...) custom-call(bf16[512,1024]{1,0:T(8,128)(2,1)} %add_convert_fusion.1.q_ref.refs_0_, ...), custom_call_target="tpu_custom_call" | custom-call | tf_op jit(solution)/shard_map/attention_and_sums/pallas_call | solution.py:931
  454.7 1.3 fusion.25
  456.0 1.2 slice.54
  457.7 1.4 reduce.17
  459.1 1.3 fusion.20
  460.4 1.2 dynamic-slice_reduce_fusion
  462.2 2.3 copy.34
  464.5 1.3 copy.35
  466.7 1.1 copy.36
  469.9 1.0 copy.39
  470.9 1.0 copy.40
  (46 shorter events, 13.7 us)
Async XLA Ops:
  0.6 29.6 %copy-start = (bf16[1,512,1024]{2,1,0:T(8,128)(2,1)S(1)}, bf16[1,512,1024]{2,1,0:T(8,128)(2,1)}, u32[]{:S(2)}) copy-start(bf16[1,512,1024]{2,1,0:T(8,128)(2,1)} %param.13) | copy-start | bytes 3145732
  31.2 139.1 %copy-start.1 = (bf16[512,1024]{1,0:T(8,128)(2,1)}, bf16[512,1024]{1,0:T(8,128)(2,1)S(1)}, u32[]{:S(2)}) copy-start(bf16[512,1024]{1,0:T(8,128)(2,1)S(1)} %fusion.5.refs_7_) | copy-start | bytes 3145732
  162.8 5.8 %copy-start.9 = (f32[16,1,896]{2,1,0:T(1,128)S(1)}, f32[16,1,896]{2,1,0:T(1,128)}, u32[]{:S(2)}) copy-start(f32[16,1,896]{2,1,0:T(1,128)} %get-tuple-element.40) | copy-start | bytes 172036
  162.8 26.3 %collective-permute-start.1 = (bf16[512,1024]{1,0:T(8,128)(2,1)}, bf16[512,1024]{1,0:T(8,128)(2,1)}, u32[]{:S(2)}, u32[]{:S(2)}) collective-permute-start(bf16[512,1024]{1,0:T(8,128)(2,1)} %add_convert_fusion.refs_2_.refs_3_), channel_id=1, source_target_pairs={{0,1},{1,0},{2,3},{3,2},{4,5},{5,4},{6,7},{7,6},{8,9},{9,8},{10,11... | collective-permute-start | bytes 3145736 | tf_op jit(solution)/shard_map/ppermute | solution.py:266
  167.7 43.3 %collective-permute-start = (bf16[512,1024]{1,0:T(8,128)(2,1)}, bf16[512,1024]{1,0:T(8,128)(2,1)}, u32[]{:S(2)}, u32[]{:S(2)}) collective-permute-start(bf16[512,1024]{1,0:T(8,128)(2,1)} %fusion.16.refs_0_.refs_1_), channel_id=1, source_target_pairs={{0,1},{1,0},{2,3},{3,2},{4,5},{5,4},{6,7},{7,6},{8,9},{9,8},{10,11... | collective-permute-start | bytes 3145736 | tf_op jit(solution)/shard_map/ppermute | solution.py:266
  174.1 54.7 %copy-start.3 = (bf16[4,2,2,64,1024]{4,3,2,1,0:T(8,128)(2,1)S(1)}, bf16[4,2,2,64,1024]{4,3,2,1,0:T(8,128)(2,1)}, u32[]{:S(2)}) copy-start(bf16[4,2,2,64,1024]{4,3,2,1,0:T(8,128)(2,1)} %get-tuple-element.43) | copy-start | bytes 6291460
  454.7 9.8 %copy-start.2 = (f32[512,1024]{1,0:T(8,128)S(1)}, f32[512,1024]{1,0:T(8,128)}, u32[]{:S(2)}) copy-start(f32[512,1024]{1,0:T(8,128)} %get-tuple-element.56) | copy-start | bytes 6291460
  464.5 2.2 copy-start.4
  466.7 1.7 copy-start.7
  466.7 2.5 copy-start.8
  466.7 3.2 copy-start.6
  468.3 2.6 copy-start.5

commit v5 on v4

--- a/solution.py
+++ b/solution.py
@@ -31,184 +31,8 @@
     return lax.dot_general(a, b, (((0,), (0,)), ((), ())), preferred_element_type=f32)
 
 
-def gather_weights(shards, chunks, n, s):
-    A, B = grid_of(n)
-    nc, ns = len(chunks), len(shards)
-    NB = (A - 1) + (B - 1)
-    steps = 2 * NB + 1
-
-    def kern(*refs):
-        ins, outs = refs[:ns], refs[ns : 2 * ns]
-        own_sem, send, recv = refs[2 * ns :]
-        me, x = lax.axis_index("fsdp"), lax.axis_index("seq")
-        a, b, c = me // (2 * B), (me // 2) % B, me % 2
-
-        def dev(a, b, c):
-            return {"fsdp": (a * B + b) * 2 + c}
-
-        apeers = [lax.rem(a + k, A) for k in range(1, A)]
-        bpeers = [lax.rem(b + k, B) for k in range(1, B)]
-        peers = [dev(p, b, c) for p in apeers] + [dev(a, p, c) for p in bpeers]
-        peers.append(dev(a, b, 1 - c))
-        if s == 2:
-            peers.append({"seq": 1 - x})
-        bar = pltpu.get_barrier_semaphore()
-        for p in peers:
-            pl.semaphore_signal(bar, inc=1, device_id=p, device_id_type=MESH)
-        pl.semaphore_wait(bar, len(peers))
-        owns = [pltpu.make_async_copy(ins[i], outs[i].at[a, b, c], own_sem.at[i]) for i in range(ns)]
-        for o in owns:
-            o.start()
-
-        def cp(i, k, src, dst, d):
-            r = pltpu.make_async_remote_copy(
-                src_ref=src,
-                dst_ref=dst,
-                send_sem=send.at[i, k],
-                recv_sem=recv.at[i, k],
-                device_id=d,
-                device_id_type=MESH,
-            )
-            r.start()
-            return r
-
-        za, zb, zx, zc = {}, {}, {}, {}
-
-        def part(i):
-            w, lo, sz, sh = chunks[i]
-            if sh and s == 2:
-                return w, pl.ds(pl.multiple_of(lo + x * (sz // 2), 128), sz // 2)
-            return w, pl.ds(lo, sz)
-
-        for i in range(nc):
-            w, cols = part(i)
-            za[i] = [
-                cp(i, k, ins[w].at[:, cols], outs[w].at[a, b, c, :, cols], dev(p, b, c))
-                for k, p in enumerate(apeers)
-            ]
-        for o in owns:
-            o.wait()
-
-        def phase_b(i):
-            w, cols = part(i)
-            for r in za[i]:
-                r.wait_recv()
-            sl = outs[w].at[:, b, c, :, cols]
-            zb[i] = [cp(i, A - 1 + k, sl, sl, dev(a, p, c)) for k, p in enumerate(bpeers)]
-
-        def phase_x(i):
-            w, cols = part(i)
-            for r in zb[i]:
-                r.wait_recv()
-            zx[i] = []
-            if chunks[i][3] and s == 2:
-                for k, p in enumerate(apeers):
-                    sl = outs[w].at[p, :, c, :, cols]
-                    zx[i].append(cp(i, NB + k, sl, sl, {"seq": 1 - x}))
-                for k, p in enumerate(bpeers):
-                    sl = outs[w].at[a, p, c, :, cols]
-                    zx[i].append(cp(i, NB + A - 1 + k, sl, sl, {"seq": 1 - x}))
-
-        def phase_c(i):
-            w, lo, sz, sh = chunks[i]
-            for r in zx[i]:
-                r.wait_recv()
-            sl = outs[w].at[:, :, c, :, pl.ds(lo, sz)]
-            zc[i] = cp(i, 2 * NB, sl, sl, dev(a, b, 1 - c))
-
-        for i in range(nc + 2):
-            if i < nc:
-                phase_b(i)
-            if 0 <= i - 1 < nc:
-                phase_x(i - 1)
-            if 0 <= i - 2 < nc:
-                phase_c(i - 2)
-        for i in range(nc):
-            zc[i].wait_recv()
-            for r in za[i] + zb[i] + zx[i] + [zc[i]]:
-                r.wait_send()
-
-    res = pl.pallas_call(
-        kern,
-        out_shape=[jax.ShapeDtypeStruct((A, B, 2) + w.shape, w.dtype) for w in shards],
-        in_specs=[pl.BlockSpec(memory_space=pltpu.VMEM)] * ns,
-        out_specs=[pl.BlockSpec(memory_space=pl.ANY)] * ns,
-        scratch_shapes=[
-            pltpu.SemaphoreType.DMA((ns,)),
-            pltpu.SemaphoreType.DMA((nc, steps)),
-            pltpu.SemaphoreType.DMA((nc, steps)),
-        ],
-        compiler_params=pltpu.CompilerParams(collective_id=0, has_side_effects=True),
-        name="gather_weights",
-    )(*shards)
-    return [r.reshape((n * w.shape[0], w.shape[1])) for r, w in zip(res, shards)]
-
-
 def fsdp_peers(n, me):
     return [lax.rem(me + k, n) for k in range(1, n)]
-
-
-def modulation_forward(lifted, w_ada, bias, n):
-    rows, E = w_ada.shape
-    m = bias.shape[-1]
-
-    def kern(l_ref, w_ref, bias_ref, mod_ref, lf_ref, bout_ref, part, acc, send, recv):
-        me = lax.axis_index("fsdp")
-        peers = fsdp_peers(n, me)
-        bar = pltpu.get_barrier_semaphore()
-        for p in peers:
-            pl.semaphore_signal(bar, inc=1, device_id={"fsdp": p}, device_id_type=MESH)
-        pl.semaphore_wait(bar, n - 1)
-
-        def cp(i, k, src, dst):
-            r = pltpu.make_async_remote_copy(
-                src_ref=src,
-                dst_ref=dst,
-                send_sem=send.at[i, k],
-                recv_sem=recv.at[i, k],
-                device_id={"fsdp": peers[k]},
-                device_id_type=MESH,
-            )
-            r.start()
-            return r
-
-        lf_ref[me] = l_ref[me]
-        bout_ref[me] = bias_ref[...]
-        first = [cp(0, k, l_ref.at[p], lf_ref.at[me]) for k, p in enumerate(peers)]
-        other = [cp(1, k, bias_ref, bout_ref.at[me]) for k, p in enumerate(peers)]
-        for r in first:
-            r.wait_recv()
-        lf = lf_ref[...].reshape(n, rows).astype(bf16)
-        part[...] = nn(lf, w_ref[...]).reshape(n, 1, E)
-        acc[0] = part[me]
-        last = [cp(2, k, part.at[p], acc.at[k + 1]) for k, p in enumerate(peers)]
-        for r in last:
-            r.wait_recv()
-        mod_ref[...] = jnp.sum(acc[...], axis=0)
-        for r in other:
-            r.wait_recv()
-        for r in first + other + last:
-            r.wait_send()
-
-    vm = pl.BlockSpec(memory_space=pltpu.VMEM)
-    return pl.pallas_call(
-        kern,
-        out_shape=[
-            jax.ShapeDtypeStruct((1, E), f32),
-            jax.ShapeDtypeStruct((n, 1, rows), f32),
-            jax.ShapeDtypeStruct((n, 1, m), f32),
-        ],
-        in_specs=[vm] * 3,
-        out_specs=[vm] * 3,
-        scratch_shapes=[
-            pltpu.VMEM((n, 1, E), f32),
-            pltpu.VMEM((n, 1, E), f32),
-            pltpu.SemaphoreType.DMA((3, n - 1)),
-            pltpu.SemaphoreType.DMA((3, n - 1)),
-        ],
-        compiler_params=pltpu.CompilerParams(collective_id=1, has_side_effects=True),
-        name="modulation_forward",
-    )(lifted, w_ada, bias)
 
 
 def head_mask(ref_shape, h):
@@ -218,52 +42,6 @@
 
 def pick(values, h):
     return jnp.where(head_mask(values.shape, h), values, jnp.zeros_like(values))
-
-
-def attend_forward_kernel(n, q_ref, *refs):
-    k_refs, v_refs, (o_ref, lse_ref) = refs[:n], refs[n : 2 * n], refs[2 * n :]
-    q = q_ref[...] * bf16(HD**-0.5)
-    total = None
-    for h in range(2):
-        qh = pick(q, h)
-        scores = [nt(k[...], qh) for k in k_refs]
-        top = scores[0].max(axis=0, keepdims=True)
-        for sc in scores[1:]:
-            top = jnp.maximum(top, sc.max(axis=0, keepdims=True))
-        mass, out = None, None
-        for sc, v in zip(scores, v_refs):
-            p = jnp.exp(sc - top)
-            part = p.sum(axis=0, keepdims=True)
-            mass = part if mass is None else mass + part
-            o = tn(pick(v[...], h), p.astype(bf16))
-            out = o if out is None else out + o
-        out = out * (1.0 / mass)
-        total = out if total is None else total + out
-        lse_ref[0, h : h + 1, :] = top + jnp.log(mass)
-    o_ref[...] = total.T.astype(bf16)
-
-
-def attend_forward(q, ks, vs):
-    T, D = q.shape
-    n = len(ks)
-
-    def col(rows):
-        return pl.BlockSpec((rows, 128), lambda i: (0, i))
-
-    keys = sum(k.shape[0] for k in ks)
-    return pl.pallas_call(
-        partial(attend_forward_kernel, n),
-        grid=(D // 128,),
-        in_specs=[col(T)] + [col(k.shape[0]) for k in ks] * 2,
-        out_specs=[col(T), pl.BlockSpec((1, 2, T), lambda i: (i, 0, 0))],
-        out_shape=[jax.ShapeDtypeStruct((T, D), bf16), jax.ShapeDtypeStruct((D // 128, 2, T), f32)],
-        cost_estimate=pl.CostEstimate(flops=16 * T * keys * D, bytes_accessed=4 * (T + keys) * D, transcendentals=0),
-        name="attend_forward",
-    )(q, *ks, *vs)
-
-
-def seq_shift(value, k, s):
-    return lax.ppermute(value, "seq", [(i, (i + k) % s) for i in range(s)])
 
 
 def remote(src, dst, send, recv, device):
@@ -324,7 +102,376 @@
     return center * rscale, rscale
 
 
-def feed_forward(middle, branch, attn, g, vectors, b_fc1, proj_w, w1, w2, n):
+def bias_block(width, n):
+    return max(-(-((p * width) % 128 + width) // 128) * 128 for p in range(n))
+
+
+def placed_bias(bias, n):
+    width, wide = bias.shape[0], bias_block(bias.shape[0], n)
+    bias = bias.astype(f32)[None]
+    if wide == width:
+        return bias
+    at = (lax.axis_index("fsdp") * width) % 128
+    return lax.dynamic_update_slice(jnp.zeros((1, wide), f32), bias, (0, at))
+
+
+def forward_attention(lifted, w_ada, biases, tokens, w_qkv, w_proj, w_fc1, w_fc2, n, s):
+    T, D = tokens.shape
+    E = w_ada.shape[1]
+    FF = w_fc1.shape[1]
+    A, B = grid_of(n)
+    rows_a = w_ada.shape[0]
+    r1, r2 = w_qkv.shape[0], w_fc2.shape[0]
+    widths = [v.shape[0] for v in biases]
+    blocks = [bias_block(w, n) for w in widths]
+    offs = [sum(blocks[:i]) for i in range(5)]
+    bases = [n * sum(widths[:i]) for i in range(5)]
+    packed = jnp.concatenate([placed_bias(v, n) for v in biases], axis=1)
+    M = packed.shape[1]
+    share = s == 2
+    NT = 8
+    CQ, CF, RF = 4 * D // NT, FF // NT, r2 // NT
+    RB = min(T, 64)
+    AHEAD, ATTEND = 3, NT + 5
+    NA, NY = A - 1, B - 1
+    NQ = 2 * (NA + NY) + 1
+    NF = 4 * (NA + NY) + 2
+    pairs = D // 128
+
+    def kern(
+        l_ref, wa_ref, bias_ref, tok_ref, wqkv_ref, wproj_ref, wfc1_ref, wfc2_ref,
+        qkv_ref, kvr_ref, h_ref, attn_ref, lse_ref, br_ref, mid_ref, vec_ref, bfc1_ref, lf_ref, w4_ref, f1_ref, f2_ref,
+        normed, wq, part, acc, bout, bvec, mod, msend, mrecv, qsend, qrecv, fsend, frecv, ksend, krecv, osem,
+    ):
+        at = Place(n)
+        a, b, c, me, x = at.a, at.b, at.c, at.me, lax.axis_index("seq")
+        peers = fsdp_peers(n, me)
+        other = {"seq": lax.rem(x + 1, s)}
+        greet([{"fsdp": p} for p in peers] + [{"seq": lax.rem(x + k, s)} for k in range(1, s)])
+
+        def small(i, src, dst):
+            return [
+                remote(src(p), dst(k), msend.at[i, k], mrecv.at[i, k], {"fsdp": p}) for k, p in enumerate(peers)
+            ]
+
+        m_lift = small(0, lambda p: l_ref.at[p], lambda k: lf_ref.at[me])
+        m_bias = small(1, lambda p: bias_ref, lambda k: bout.at[me])
+        m_part = small(2, lambda p: part.at[p], lambda k: acc.at[k + 1])
+        for r in m_lift + m_bias:
+            r.start()
+        owns = [
+            pltpu.make_async_copy(wqkv_ref, wq.at[a, b, c, :, pl.ds(0, 3 * D)], osem.at[0]),
+            pltpu.make_async_copy(wproj_ref, wq.at[a, b, c, :, pl.ds(3 * D, D)], osem.at[1]),
+            pltpu.make_async_copy(wfc1_ref, f1_ref.at[a, b, c], osem.at[2]),
+            pltpu.make_async_copy(wfc2_ref, f2_ref.at[a, b, c], osem.at[3]),
+        ]
+        for o in owns:
+            o.start()
+
+        def block(i):
+            return jnp.where(i < 6, lax.rem(i + 2, 6), i)
+
+        def span(lo, size, step):
+            return pl.ds(pl.multiple_of(lo, step), size)
+
+        class Ticks:
+            def __init__(self, pieces, whole, send, recv):
+                self.pieces, self.whole, self.send, self.recv = pieces, whole, send, recv
+
+            def copy(self, j, i, src, dst, device):
+                return remote(src, dst, self.send.at[j, i], self.recv.at[j, i], device)
+
+            def z(self, j):
+                return [
+                    self.copy(j, i * NA + k, src.at[rows, cols], buf.at[a, b, c, rows, cols], at.at_a(k + 1))
+                    for i, (src, buf, rows, cols, _) in enumerate(self.pieces(j))
+                    for k in range(NA)
+                ]
+
+            def y(self, j):
+                out, ps = [], self.pieces(j)
+                for i, (_, buf, rows, cols, _) in enumerate(ps):
+                    sl = buf.at[:, b, c, rows, cols]
+                    out += [self.copy(j, len(ps) * NA + i * NY + k, sl, sl, at.at_b(k + 1)) for k in range(NY)]
+                return out
+
+            def x(self, j):
+                out, ps = [], self.pieces(j)
+                i = len(ps) * (NA + NY)
+                for _, buf, rows, cols, shared in ps:
+                    if not shared:
+                        continue
+                    for k in range(NA):
+                        sl = buf.at[lax.rem(a + k + 1, A), :, c, rows, cols]
+                        out.append(self.copy(j, i, sl, sl, other))
+                        i += 1
+                    for k in range(NY):
+                        sl = buf.at[a, lax.rem(b + k + 1, B), c, rows, cols]
+                        out.append(self.copy(j, i, sl, sl, other))
+                        i += 1
+                return out
+
+            def c(self, j):
+                ps = self.whole(j)
+                i = self.send.shape[1] - len(ps)
+                return [
+                    self.copy(j, i + k, buf.at[:, :, c, rows, cols], buf.at[:, :, c, rows, cols], at.sibling())
+                    for k, (buf, rows, cols) in enumerate(ps)
+                ]
+
+            def start_z(self, j):
+                for r in self.z(j):
+                    r.start()
+
+            def start_y(self, j):
+                for r in self.z(j):
+                    r.wait_recv()
+                for r in self.y(j):
+                    r.start()
+
+            def start_x(self, j):
+                for r in self.y(j):
+                    r.wait_recv()
+                for r in self.x(j):
+                    r.start()
+
+            def start_c(self, j):
+                for r in self.x(j):
+                    r.wait_recv()
+                for r in self.c(j):
+                    r.start()
+
+            def finish(self, j):
+                for r in self.z(j) + self.y(j) + self.x(j):
+                    r.wait_send()
+                for r in self.c(j):
+                    r.wait()
+
+        all_r1 = pl.ds(0, r1)
+        mine = wq.at[a, b, c]
+
+        def q_pieces(i):
+            lo, size = block(i) * CQ, CQ
+            if share:
+                size = CQ // 2
+                lo = lo + x * size
+            return [(mine, wq, all_r1, span(lo, size, size), share)]
+
+        def q_whole(i):
+            return [(wq, all_r1, span(block(i) * CQ, CQ, CQ))]
+
+        def f_pieces(j):
+            first = (wfc1_ref, f1_ref, all_r1, span(j * CF, CF, CF), False)
+            if not share:
+                return [first, (wfc2_ref, f2_ref, span(j * RF, RF, RF), pl.ds(0, D), False)]
+            h, w = RF // 2, D // 2
+            return [
+                first,
+                (wfc2_ref, f2_ref, span(j * RF, h, h), span(x * w, w, w), True),
+                (wfc2_ref, f2_ref, span(j * RF + h, h, h), pl.ds(0, D), False),
+            ]
+
+        def f_whole(j):
+            return [(f1_ref, all_r1, span(j * CF, CF, CF)), (f2_ref, span(j * RF, RF, RF), pl.ds(0, D))]
+
+        tq, tf = Ticks(q_pieces, q_whole, qsend, qrecv), Ticks(f_pieces, f_whole, fsend, frecv)
+
+        owns[0].wait()
+        owns[1].wait()
+        for i in range(AHEAD):
+            tq.start_z(i)
+        lf_ref[me] = l_ref[me]
+        bout[me] = bias_ref[...]
+        bvec[...] = jnp.zeros_like(bvec)
+
+        def norm(i, _):
+            rows = pl.ds(pl.multiple_of(i * RB, RB), RB)
+            normed[rows, :] = normalize(tok_ref[rows, :].astype(f32))[0]
+            return 0
+
+        for r in m_lift:
+            r.wait_recv()
+        part[...] = nn(lf_ref[...].reshape(n, rows_a).astype(bf16), wa_ref[...]).reshape(n, 1, E)
+        acc[0] = part[me]
+        for r in m_part:
+            r.start()
+        for i in range(AHEAD, AHEAD + 2):
+            tq.start_z(i)
+        tq.start_y(0)
+        lax.fori_loop(0, T // RB, norm, 0)
+        tq.start_y(1)
+        tq.start_x(0)
+        for r in m_bias:
+            r.wait_recv()
+        for i in range(5):
+            for p in range(n):
+                lo = bases[i] + p * widths[i] // 128 * 128
+                value = bout[p, :, offs[i] : offs[i] + blocks[i]]
+                if widths[i] % 128 == 0:
+                    bvec[:, lo : lo + blocks[i]] = value
+                else:
+                    bvec[:, lo : lo + blocks[i]] += value
+        for r in m_part:
+            r.wait_recv()
+        mod[...] = jnp.sum(acc[...], axis=0) + bvec[:, bases[4] :]
+        shift1, scale1, gate1, shift2, scale2, gate2 = [mod[:, i * D : (i + 1) * D] for i in range(6)]
+        vec_ref[...] = jnp.zeros_like(vec_ref)
+        for i, v in enumerate((shift2, scale2, gate2, gate1, bvec[:, bases[3] : bases[3] + D], scale1)):
+            vec_ref[i : i + 1, :] = v
+        bfc1_ref[...] = bvec[:, bases[2] : bases[2] + FF]
+
+        def modulate(i, _):
+            rows = pl.ds(pl.multiple_of(i * RB, RB), RB)
+            h_ref[rows, :] = (normed[rows, :] * (1.0 + scale1) + shift1).astype(bf16)
+            return 0
+
+        lax.fori_loop(0, T // RB, modulate, 0)
+
+        def kv_copy(m, k):
+            return remote(
+                qkv_ref.at[:, span(D + m * CQ, CQ, CQ)],
+                kvr_ref.at[k - 1, :, span(m * CQ, CQ, CQ)],
+                ksend.at[m, k - 1],
+                krecv.at[m, k - 1],
+                {"seq": lax.rem(x + k, s)},
+            )
+
+        def project(m):
+            tq.finish(m)
+
+            @pl.when(m < 6)
+            def _():
+                lo = block(m) * CQ
+                cols = span(lo, CQ, CQ)
+                from_v = (block(m) >= 4).astype(jnp.int32)
+                bias = bvec[:, span(lo - from_v * D, CQ, CQ)]
+                is_key = jnp.logical_and(block(m) >= 2, block(m) < 4)
+                bias = jnp.where(is_key, jnp.zeros_like(bias), bias)
+                out = nn(h_ref[...], wq[:, :, :, :, cols].reshape(D, CQ))
+                qkv_ref[:, cols] = (out + bias).astype(bf16)
+
+            @pl.when(m < 4)
+            def _():
+                for k in range(1, s):
+                    kv_copy(m, k).start()
+
+        def attend(pair):
+            def cols(lo):
+                return span(lo + pair * 128, 128, 128)
+
+            q = qkv_ref[:, cols(0)] * bf16(HD**-0.5)
+            ks = [qkv_ref[:, cols(D)]] + [kvr_ref[k, :, cols(0)] for k in range(s - 1)]
+            vs = [qkv_ref[:, cols(2 * D)]] + [kvr_ref[k, :, cols(D)] for k in range(s - 1)]
+            total = None
+            for h in range(2):
+                qh = pick(q, h)
+                scores = [nt(k, qh) for k in ks]
+                top = scores[0].max(axis=0, keepdims=True)
+                for sc in scores[1:]:
+                    top = jnp.maximum(top, sc.max(axis=0, keepdims=True))
+                mass, out = None, None
+                for sc, v in zip(scores, vs):
+                    p = jnp.exp(sc - top)
+                    got = p.sum(axis=0, keepdims=True)
+                    mass = got if mass is None else mass + got
+                    o = tn(pick(v, h), p.astype(bf16))
+                    out = o if out is None else out + o
+                out = out * (1.0 / mass)
+                total = out if total is None else total + out
+                lse_ref[pair, h : h + 1, :] = top + jnp.log(mass)
+            attn_ref[:, cols(0)] = total.T.astype(bf16)
+
+        def branch(i, _):
+            cols = span(i * 256, 256, 256)
+            weight = wq[:, :, :, :, span(3 * D + i * 256, 256, 256)].reshape(D, 256)
+            got = nn(attn_ref[...], weight) + bvec[:, span(bases[1] + i * 256, 256, 256)]
+            br_ref[:, cols] = got
+            mid_ref[:, cols] = tok_ref[:, cols].astype(f32) + mod[:, span(2 * D + i * 256, 256, 256)] * got
+            return 0
+
+        out4 = pltpu.make_async_copy(wq, w4_ref, osem.at[0])
+
+        def step(i, _):
+            def when(lo, hi, f, shift):
+                @pl.when(jnp.logical_and(i >= lo, i < hi))
+                def _():
+                    f(i - shift)
+
+            when(0, NT - AHEAD, lambda j: tq.start_z(j + AHEAD), 0)
+            when(NT - AHEAD, 2 * NT - AHEAD, lambda j: tf.start_z(j), NT - AHEAD)
+            when(2, NT, tq.start_y, 0)
+            when(NT, 2 * NT, tf.start_y, NT)
+            when(2, NT + 1, tq.start_x, 1)
+            when(NT + 1, 2 * NT + 1, tf.start_x, NT + 1)
+            when(2, NT + 2, tq.start_c, 2)
+            when(NT + 2, 2 * NT + 2, tf.start_c, NT + 2)
+            when(3, NT + 3, project, 3)
+            when(NT + 3, 2 * NT + 3, tf.finish, NT + 3)
+
+            @pl.when(i == NT + 3)
+            def _():
+                out4.start()
+
+            @pl.when(i == ATTEND)
+            def _():
+                for m in range(4):
+                    for k in range(1, s):
+                        kv_copy(m, k).wait()
+
+            per = pairs // 4
+
+            @pl.when(jnp.logical_and(i >= ATTEND, i < ATTEND + 4))
+            def _():
+                def one(o, _):
+                    attend((i - ATTEND) * per + o)
+                    return 0
+
+                lax.fori_loop(0, per, one, 0)
+
+            @pl.when(i == ATTEND + 4)
+            def _():
+                lax.fori_loop(0, D // 256, branch, 0)
+
+            return 0
+
+        owns[2].wait()
+        owns[3].wait()
+        lax.fori_loop(2, 2 * NT + 3, step, 0)
+        out4.wait()
+        for r in m_lift + m_bias + m_part:
+            r.wait_send()
+
+    vm, hbm = pl.BlockSpec(memory_space=pltpu.VMEM), pl.BlockSpec(memory_space=pl.ANY)
+    sds, dma = jax.ShapeDtypeStruct, pltpu.SemaphoreType.DMA
+    res = pl.pallas_call(
+        kern,
+        out_shape=[
+            sds((T, 3 * D), bf16), sds((s - 1, T, 2 * D), bf16), sds((T, D), bf16), sds((T, D), bf16),
+            sds((pairs, 2, T), f32), sds((T, D), f32), sds((T, D), f32), sds((8, D), f32), sds((1, FF), f32),
+            sds((n, 1, rows_a), f32), sds((A, B, 2, r1, 4 * D), bf16), sds((A, B, 2, r1, FF), bf16),
+            sds((A, B, 2, r2, D), bf16),
+        ],
+        in_specs=[vm] * 8,
+        out_specs=[vm] * 10 + [hbm] * 3,
+        scratch_shapes=[
+            pltpu.VMEM((T, D), f32), pltpu.VMEM((A, B, 2, r1, 4 * D), bf16), pltpu.VMEM((n, 1, E), f32),
+            pltpu.VMEM((n, 1, E), f32), pltpu.VMEM((n, 1, M), f32), pltpu.VMEM((1, n * sum(widths)), f32),
+            pltpu.VMEM((1, E), f32), dma((3, n - 1)), dma((3, n - 1)), dma((NT, NQ)), dma((NT, NQ)),
+            dma((NT, NF)), dma((NT, NF)), dma((4, s - 1)), dma((4, s - 1)), dma((4,)),
+        ],
+        compiler_params=pltpu.CompilerParams(
+            collective_id=0, has_side_effects=True, vmem_limit_bytes=64 * 1024 * 1024 - 65536
+        ),
+        name="forward_attention",
+    )(lifted, w_ada, packed, tokens, w_qkv, w_proj, w_fc1, w_fc2)
+    qkv, kvr, hidden, attn, lse, branch, middle, vectors, b_fc1, lf, w4, f1, f2 = res
+    return (
+        qkv, kvr, hidden, attn, lse, branch, middle, vectors, b_fc1, lf,
+        w4.reshape(D, 4 * D), f1.reshape(D, FF), f2.reshape(FF, D),
+    )
+
+
+def feed_forward(middle, branch, attn, g, vectors, b_fc1, w4, w1, w2, n):
     T, D = middle.shape
     FF = w1.shape[1]
     A, B = grid_of(n)
@@ -333,10 +480,10 @@
     RB = min(T, 64)
 
     def kern(
-        mid_ref, br_ref, attn_ref, g_ref, vec_ref, b1_ref, pw_ref, w1_ref, w2_ref,
+        mid_ref, br_ref, attn_ref, g_ref, vec_ref, b1_ref, w4_ref, w1_ref, w2_ref,
         out_ref, dmid_ref, dattn_ref, sums_ref, bfc1_ref, gproj_ref, g1_ref, g2_ref,
         h2, h2t, dm, dh2, mlp, dbr, w1b, w2b, gb, cr, ys, yr, zs, zr, t1, c1, s1,
-        wsem, osem, cs, crs, c1s, c1r, yss, yrs, zss, zrs,
+        pw, psem, wsem, osem, cs, crs, c1s, c1r, yss, yrs, zss, zrs,
     ):
         at = Place(n)
         greet(at.all())
@@ -355,6 +502,8 @@
 
         for w in weights(0, 0):
             w.start()
+        proj_copy = pltpu.make_async_copy(w4_ref.at[:, pl.ds(3 * D, D)], pw, psem)
+        proj_copy.start()
 
         def head(i, _):
             rows = pl.ds(pl.multiple_of(i * RB, RB), RB)
@@ -499,7 +648,8 @@
             return 0
 
         lax.fori_loop(0, T // RB, back, 0)
-        dattn_ref[...] = nt(dbr[...], pw_ref[...]).astype(bf16)
+        proj_copy.wait()
+        dattn_ref[...] = nt(dbr[...], pw[...]).astype(bf16)
 
         def proj(i, _):
             cols = pl.ds(pl.multiple_of(i * 256, 256), 256)
@@ -537,7 +687,7 @@
             sds((T, D), bf16), sds((T, D), f32), sds((T, D), bf16), sds((8, D), f32), sds((J, 1, W), f32),
             sds((D, D), bf16), sds((J, r1, FF), bf16), sds((r2, D), bf16),
         ],
-        in_specs=[vm] * 7 + [hbm] * 2,
+        in_specs=[vm] * 6 + [hbm] * 3,
         out_specs=[vm] * 6 + [hbm, vm],
         scratch_shapes=[
             pltpu.VMEM((T, D), bf16), pltpu.VMEM((D, T), bf16), pltpu.VMEM((T, D), bf16),
@@ -547,14 +697,14 @@
             pltpu.VMEM((A, B - 1, r2, D), bf16), pltpu.VMEM((A, B - 1, r2, D), bf16),
             pltpu.VMEM((A - 1, r2, D), bf16), pltpu.VMEM((A - 1, r2, D), bf16),
             pltpu.VMEM((2, J, 2, r1, W), bf16), pltpu.VMEM((J, J, r1, W), bf16), pltpu.VMEM((2, J, r1, W), bf16),
-            dma((2, 2)), dma((2,)), dma((J,)), dma((J,)), dma((J,)), dma((J,)),
+            pltpu.VMEM((D, D), bf16), dma(()), dma((2, 2)), dma((2,)), dma((J,)), dma((J,)), dma((J,)), dma((J,)),
             dma((A, B - 1)), dma((A, B - 1)), dma((A - 1,)), dma((A - 1,)),
         ],
         compiler_params=pltpu.CompilerParams(
             collective_id=3, has_side_effects=True, vmem_limit_bytes=64 * 1024 * 1024 - 65536
         ),
         name="feed_forward",
-    )(middle, branch, attn, g, vectors, b_fc1.reshape(J, 1, W), proj_w, w1, w2)
+    )(middle, branch, attn, g, vectors, b_fc1.reshape(J, 1, W), w4, w1, w2)
 
 
 class RowSum:
@@ -637,9 +787,9 @@
 
 
 def attention_and_sums(
-    q, ks, vs, d_attn, lse, hidden, tokens, scale, d_middle, w_qkv, half_fc1, grad_proj, sum_fc2, sums, bias_fc1, lf, w_ada, n, s
+    qkv, kvr, d_attn, lse, hidden, tokens, vectors, d_middle, w_qkv, half_fc1, grad_proj, sum_fc2, sums, bias_fc1, lf, w_ada, n, s
 ):
-    T, D = q.shape
+    T, D = tokens.shape
     FF = half_fc1.shape[-1]
     A, B = grid_of(n)
     J, r1, r2 = A * B, D // n, FF // n
@@ -664,8 +814,7 @@
         def take(count):
             return [next(it) for _ in range(count)]
 
-        (q_ref,) = take(1)
-        k_refs, v_refs = take(s), take(s)
+        qkv_ref, kvr_ref = take(2)
         e_ref, lse_ref, h_ref, tok_ref, sc_ref, dmid_ref, w_ref, f1_ref, gp_ref, f2_ref, sum_ref, bf_ref, lf_ref, wa_ref = take(14)
         gt_ref, oq_ref, op_ref, o1_ref, o2_ref, gw_ref, gb_ref, dl_ref, bo_ref = take(9)
         h1t, dqg, kvl, kvs, kvr, dg, gq, wq, f1o, x2 = take(10)
@@ -735,17 +884,19 @@
             slot = lax.rem(u, 2)
             for o in range(2):
                 pair = u * 2 + o
-                cols = pl.ds(pl.multiple_of(pair * 128, 128), 128)
+                cols, k_cols, v_cols = [pl.ds(pl.multiple_of(lo + pair * 128, 128), 128) for lo in (0, D, 2 * D)]
                 here = slice(o * 128, o * 128 + 128)
-                qv, e = q_ref[:, cols] * bf16(HD**-0.5), e_ref[:, cols]
+                qv, e = qkv_ref[:, cols] * bf16(HD**-0.5), e_ref[:, cols]
+                ks = [qkv_ref[:, k_cols]] + [kvr_ref[k, :, cols] for k in range(s - 1)]
+                vs = [qkv_ref[:, v_cols]] + [kvr_ref[k, :, k_cols] for k in range(s - 1)]
                 dqt, dks, dvs = None, [None] * s, [None] * s
                 for h in range(2):
                     qh, eh = pick(qv, h), pick(e, h)
                     total = lse_ref[pair, h : h + 1, :]
                     probs, dprobs, cross = [], [], None
                     for j in range(s):
-                        p = jnp.exp(nt(k_refs[j][:, cols], qh) - total)
-                        dp = nt(v_refs[j][:, cols], eh)
+                        p = jnp.exp(nt(ks[j], qh) - total)
+                        dp = nt(vs[j], eh)
                         part = (p * dp).sum(axis=0, keepdims=True)
                         cross = part if cross is None else cross + part
                         dv = nn(p.astype(bf16), eh)
@@ -756,7 +907,7 @@
                         ds = (probs[j] * (dprobs[j] - cross)).astype(bf16)
                         dk = nn(ds, qh)
                         dks[j] = dk if dks[j] is None else dks[j] + dk
-                        t = tn(pick(k_refs[j][:, cols], h), ds)
+                        t = tn(pick(ks[j], h), ds)
                         dqt = t if dqt is None else dqt + t
                 dqg[slot, :, here] = (dqt * (HD**-0.5)).T.astype(bf16)
                 kvl[slot, 0, :, here] = dks[0]
@@ -825,7 +976,7 @@
             sq.send_z(u)
 
         sums = [jnp.zeros((1, D), f32), jnp.zeros((1, D), f32)]
-        scale1 = sc_ref[...]
+        scale1 = sc_ref[5:6, :]
 
         def back(i, carry):
             rows = pl.ds(pl.multiple_of(i * RB, RB), RB)
@@ -934,7 +1085,7 @@
             sds((T, D), f32), sds((r1, 3 * D), f32), sds((r1, D), f32), sds((r1, FF), f32), sds((r2, D), f32),
             sds((rows_a, E), f32), sds((1, E), f32), sds((n, 1, rows_a), f32), sds((1, M), f32),
         ],
-        in_specs=[vm] * (3 + 2 * s) + [hbm] + [vm] * 3 + [hbm, hbm] + [vm] * 6,
+        in_specs=[vm] * 4 + [hbm] + [vm] * 3 + [hbm, hbm] + [vm] * 6,
         out_specs=[vm] * 9,
         scratch_shapes=[
             pltpu.VMEM((D, T), bf16), pltpu.VMEM((2, T, GW), bf16),
@@ -958,7 +1109,7 @@
         ),
         name="attention_and_sums",
     )(
-        q, *ks, *vs, d_attn, lse, hidden, tokens, scale, d_middle, w_qkv, half_fc1.reshape(A, B, r1, FF),
+        qkv, kvr, d_attn, lse, hidden, tokens, vectors, d_middle, w_qkv, half_fc1.reshape(A, B, r1, FF),
         grad_proj.reshape(1, J, 2, r1, D), sum_fc2, sums, bias_fc1, lf, w_ada,
     )
     grad_tokens, t_qkv, t_proj, t_fc1, t_fc2, t_ada, ada_sums, d_lifted, bias = res
@@ -969,12 +1120,6 @@
     for width, wide, off in zip(m_bias, blocks, offs):
         biases.append(lax.dynamic_slice_in_dim(bias[0, off : off + wide], (me * width) % wide, width))
     return grad_tokens, t_qkv, t_proj, t_fc1, t_fc2, t_ada, ada_sums, d_lifted, biases
-
-
-def layer_norm(values):
-    center = values - jnp.mean(values, axis=-1, keepdims=True)
-    rscale = lax.rsqrt(jnp.mean(center * center, axis=-1, keepdims=True) + norm_eps)
-    return (center * rscale, rscale)
 
 
 def on_device(
@@ -994,43 +1139,18 @@
 ):
     n, s = lax.axis_size("fsdp"), lax.axis_size("seq")
     width = tokens.shape[-1]
-    T = tokens.shape[1]
-    tokens_f = tokens[0].astype(f32)
-    grad_out = cotangent[0].astype(f32)
 
     lifted, silu_back = jax.vjp(jax.nn.silu, condition.astype(f32))
     lifted_q = lifted.astype(bf16).astype(f32).reshape(n, 1, width // n)
-    packed = [b_qv, b_proj, b_fc1, b_fc2, b_ada]
-    edges = [sum(v.shape[0] for v in packed[:i]) for i in range(6)]
-    modulation, lf, biases = modulation_forward(lifted_q, w_ada, jnp.concatenate(packed).astype(f32)[None], n)
-    qv_b, proj_b, fc1_b, fc2_b, ada_b = [biases[:, 0, edges[i] : edges[i + 1]].reshape(1, -1) for i in range(5)]
-    modulation = modulation + ada_b
-    shift_one, scale_one, gate_one, shift_two, scale_two, gate_two = jnp.split(modulation, 6, axis=-1)
-
-    h, q4 = w_fc1.shape[1], w_fc2.shape[1]
-    chunks = [(0, width, width, True), (0, 2 * width, width, True), (0, 0, width, True), (1, 0, width, True)]
-    chunks += [(3, i * (q4 // 4), q4 // 4, i != 2) for i in range(4)]
-    chunks += [(2, i * (h // 8), h // 8, i % 2 == 0) for i in range(8)]
-    qkv_w, proj_w, fc1_w, fc2_w = gather_weights([w_qkv, w_proj, w_fc1, w_fc2], chunks, n, s)
-
-    normed_one, rscale_one = layer_norm(tokens_f)
-    hidden_one = (normed_one * (1.0 + scale_one) + shift_one).astype(bf16)
-    keys = nn(hidden_one, qkv_w[:, width : 2 * width]).astype(bf16)
-    values = (nn(hidden_one, qkv_w[:, 2 * width :]) + qv_b[:, width:]).astype(bf16)
-    ks = [keys] + [seq_shift(keys, k, s) for k in range(1, s)]
-    vs = [values] + [seq_shift(values, k, s) for k in range(1, s)]
-    queries = (nn(hidden_one, qkv_w[:, :width]) + qv_b[:, :width]).astype(bf16)
-    attn, lse = attend_forward(queries, ks, vs)
-    branch = nn(attn, proj_w) + proj_b
-    middle = tokens_f + gate_one * branch
-
-    vectors = jnp.concatenate([shift_two, scale_two, gate_two, gate_one, fc2_b, jnp.zeros((3, width), f32)], axis=0)
+    qkv, kvr, hidden_one, attn, lse, branch, middle, vectors, fc1_b, lf, w4, fc1_w, fc2_w = forward_attention(
+        lifted_q, w_ada, [b_qv, b_proj, b_fc1, b_fc2, b_ada], tokens[0], w_qkv, w_proj, w_fc1, w_fc2, n, s
+    )
     result, d_middle, d_attn, sums, bias_fc1, grad_proj, half_fc1, sum_fc2 = feed_forward(
-        middle, branch, attn, cotangent[0], vectors, fc1_b, proj_w, fc1_w, fc2_w, n
+        middle, branch, attn, cotangent[0], vectors, fc1_b, w4, fc1_w, fc2_w, n
     )
     grad_input, total_qkv, total_proj, total_fc1, total_fc2, total_ada, sums_ada, d_lifted, total_bias = (
         attention_and_sums(
-            queries, ks, vs, d_attn, lse, hidden_one, tokens[0], scale_one, d_middle, qkv_w, half_fc1,
+            qkv, kvr, d_attn, lse, hidden_one, tokens[0], vectors, d_middle, w4, half_fc1,
             grad_proj, sum_fc2, sums, bias_fc1.reshape(1, -1), lf, w_ada, n, s,
         )
     )

time: 473 us -> 439 us (0.928)
  waiting for transfers between devices: 37 us -> 0 us
  Pallas kernels: 387 us -> 411 us
  matrix products: 16 us -> 0 us
    ppermute x2 -> x0, waiting for transfers between devices: 37 us -> none  [seq_shift(): return lax.ppermute(value, 'seq', [(i, (i + k) % s) for i in range(s)])]
    pallas_call x3 -> x1, Pallas kernels: 166 us -> 195 us  [forward_attention(): pl.pallas_call(kern, out_shape=[sds((T, 3 * D), bf16), sds((s - 1, T, 2 *...]
    dot_general x4 -> x0, matrix products: 16 us -> none  [nn(): lax.dot_general(a, b, (((1,), (0,)), ((), ())), preferred_element_type=f32)]
    pallas_call x1, Pallas kernels: 85.1 us -> 80 us  [feed_forward(): pl.pallas_call(kern, out_shape=[sds((T, D), bf16), sds((T, D), f32), sds(...]
    unnamed x27 -> x22, local copies, waits for them, and re-layouts: 9.63 us -> 11.2 us
  transfers between devices with their start and end apart: 2 -> 0, of which waited for: 2 -> 0; matrix products, arithmetic and copies ran while one was open for 2% -> 0% of each run, Pallas kernels for 0% -> 0%
where the time goes in v5:
time: 439 us; the launch traced here: 437 us
  Pallas kernels  411 us (94%)
  local copies, waits for them, and re-layouts  17.6 us (4%)
  other arithmetic  7.79 us (2%)
    pallas_call x1, Pallas kernels, forward_attention(): pl.pallas_call(kern, out_shape=[sds((T, 3 * D), bf16), sds((s - 1, T, 2 *...  195 us
    pallas_call x1, Pallas kernels, attention_and_sums(): pl.pallas_call(kern, out_shape=[sds((T, D), f32), sds((r1, 3 * D), f32),...  137 us
    pallas_call x1, Pallas kernels, feed_forward(): pl.pallas_call(kern, out_shape=[sds((T, D), bf16), sds((T, D), f32), sds(...  80 us
    unnamed x22, local copies, waits for them, and re-layouts  11.2 us

profile of v5, /device:TPU:0, one launch (start us, length us, event | category | flops | bytes accessed | tf_op | source)
XLA Modules:
  0.0 437.4 jit_solution(15820166584698145058)
XLA Ops:
  0.7 0.7 bitcast_convert_fusion.1
  1.4 1.2 constant_dynamic-update-slice_fusion.4
  3.1 0.7 broadcast_in_dim.50
  4.3 0.7 bitcast_convert_fusion
  5.6 0.7 broadcast_in_dim.52
  6.8 1.3 convert_reduce_fusion
  8.1 0.7 reshape.69.l_ref
  8.8 194.5 %forward_attention.1 = (bf16[512,3072]{1,0:T(8,128)(2,1)}, bf16[1,512,2048]{2,1,0:T(8,128)(2,1)}, bf16[512,1024]{1,0:T(8,128)(2,1)}, bf16[512,1024]{1,0:T(8,128)...) custom-call(f32[16,1,64]{2,1,0:T(1,128)} %reshape.69.l_ref, ...), custom_call_target="tpu_custom_call" | custom-call | tf_op jit(solution)/shard_map/forward_attention/pallas_call | solution.py:446
  203.3 80.0 %feed_forward.1 = (bf16[512,1024]{1,0:T(8,128)(2,1)}, f32[512,1024]{1,0:T(8,128)}, bf16[512,1024]{1,0:T(8,128)(2,1)}, f32[8,1024]{1,0:T(8,128)}, f32[8,1,512]{2,...) custom-call(f32[512,1024]{1,0:T(8,128)} %get-tuple-element.43.mid_ref, ...), custom_call_target="tpu_custom_call" | custom-call | tf_op jit(solution)/shard_map/feed_forward/pallas_call | solution.py:684
  283.3 136.7 %attention_and_sums.1 = (f32[512,1024]{1,0:T(8,128)}, f32[64,3072]{1,0:T(8,128)}, f32[64,1024]{1,0:T(8,128)}, f32[64,4096]{1,0:T(8,128)}, f32[256,1024]{1,0:T(8,...) custom-call(bf16[512,3072]{1,0:T(8,128)(2,1)} %get-tuple-element.52.refs_0_, ...), custom_call_target="tpu_custom_call" | custom-call | tf_op jit(solution)/shard_map/attention_and_sums/pallas_call | solution.py:1082
  420.1 1.3 fusion.4
  421.4 0.6 fusion.2
  422.5 1.4 reduce.9
  424.0 1.3 fusion.1
  425.3 1.2 dynamic-slice_reduce_fusion
  426.5 1.2 slice.14
  427.7 2.3 copy.39
  430.0 1.3 copy.40
  431.3 0.8 copy-done.1
  432.2 1.1 copy.41
  433.8 0.9 copy.42
  434.7 0.7 copy.43
  435.4 1.0 copy.44
  436.4 1.0 copy.45
  (21 shorter events, 3.4 us)
Async XLA Ops:
  420.1 9.9 %copy-start = (f32[512,1024]{1,0:T(8,128)S(1)}, f32[512,1024]{1,0:T(8,128)}, u32[]{:S(2)}) copy-start(f32[512,1024]{1,0:T(8,128)} %get-tuple-element.64) | copy-start | bytes 6291460
  430.0 2.2 copy-start.1
  432.2 1.7 copy-start.4
  432.2 2.5 copy-start.5
  432.2 3.2 copy-start.3
  433.8 2.6 copy-start.2

commit v6 on v5

--- a/solution.py
+++ b/solution.py
@@ -129,13 +129,13 @@
     packed = jnp.concatenate([placed_bias(v, n) for v in biases], axis=1)
     M = packed.shape[1]
     share = s == 2
-    NT = 8
-    CQ, CF, RF = 4 * D // NT, FF // NT, r2 // NT
+    NT, NL = 8, 16
+    CQ, CF, RF = 4 * D // NT, FF // NL, r2 // NL
     RB = min(T, 64)
-    AHEAD, ATTEND = 3, NT + 5
+    AHEAD, MODULATE, LAG, ATTEND = 2, 4, 6, NT + 7
     NA, NY = A - 1, B - 1
-    NQ = 2 * (NA + NY) + 1
-    NF = 4 * (NA + NY) + 2
+    NQ = NA + NY + 1
+    NF = 3 * (NA + NY) + 2
     pairs = D // 128
 
     def kern(
@@ -241,6 +241,10 @@
                 for r in self.c(j):
                     r.start()
 
+            def relay(self, j):
+                self.start_x(j)
+                self.start_c(j)
+
             def finish(self, j):
                 for r in self.z(j) + self.y(j) + self.x(j):
                     r.wait_send()
@@ -251,24 +255,17 @@
         mine = wq.at[a, b, c]
 
         def q_pieces(i):
-            lo, size = block(i) * CQ, CQ
-            if share:
-                size = CQ // 2
-                lo = lo + x * size
-            return [(mine, wq, all_r1, span(lo, size, size), share)]
+            return [(mine, wq, all_r1, span(block(i) * CQ, CQ, CQ), False)]
 
         def q_whole(i):
             return [(wq, all_r1, span(block(i) * CQ, CQ, CQ))]
 
         def f_pieces(j):
-            first = (wfc1_ref, f1_ref, all_r1, span(j * CF, CF, CF), False)
-            if not share:
-                return [first, (wfc2_ref, f2_ref, span(j * RF, RF, RF), pl.ds(0, D), False)]
-            h, w = RF // 2, D // 2
+            w = D // 2 if share else D
+            part = span(x * w, w, w) if share else pl.ds(0, D)
             return [
-                first,
-                (wfc2_ref, f2_ref, span(j * RF, h, h), span(x * w, w, w), True),
-                (wfc2_ref, f2_ref, span(j * RF + h, h, h), pl.ds(0, D), False),
+                (wfc1_ref, f1_ref, all_r1, span(j * CF, CF, CF), False),
+                (wfc2_ref, f2_ref, span(j * RF, RF, RF), part, share),
             ]
 
         def f_whole(j):
@@ -295,37 +292,32 @@
         acc[0] = part[me]
         for r in m_part:
             r.start()
-        for i in range(AHEAD, AHEAD + 2):
-            tq.start_z(i)
-        tq.start_y(0)
-        lax.fori_loop(0, T // RB, norm, 0)
-        tq.start_y(1)
-        tq.start_x(0)
-        for r in m_bias:
-            r.wait_recv()
-        for i in range(5):
-            for p in range(n):
-                lo = bases[i] + p * widths[i] // 128 * 128
-                value = bout[p, :, offs[i] : offs[i] + blocks[i]]
-                if widths[i] % 128 == 0:
-                    bvec[:, lo : lo + blocks[i]] = value
-                else:
-                    bvec[:, lo : lo + blocks[i]] += value
-        for r in m_part:
-            r.wait_recv()
-        mod[...] = jnp.sum(acc[...], axis=0) + bvec[:, bases[4] :]
-        shift1, scale1, gate1, shift2, scale2, gate2 = [mod[:, i * D : (i + 1) * D] for i in range(6)]
-        vec_ref[...] = jnp.zeros_like(vec_ref)
-        for i, v in enumerate((shift2, scale2, gate2, gate1, bvec[:, bases[3] : bases[3] + D], scale1)):
-            vec_ref[i : i + 1, :] = v
-        bfc1_ref[...] = bvec[:, bases[2] : bases[2] + FF]
-
-        def modulate(i, _):
-            rows = pl.ds(pl.multiple_of(i * RB, RB), RB)
-            h_ref[rows, :] = (normed[rows, :] * (1.0 + scale1) + shift1).astype(bf16)
-            return 0
-
-        lax.fori_loop(0, T // RB, modulate, 0)
+
+        def modulation():
+            for r in m_bias + m_part:
+                r.wait_recv()
+            for i in range(5):
+                for p in range(n):
+                    lo = bases[i] + p * widths[i] // 128 * 128
+                    value = bout[p, :, offs[i] : offs[i] + blocks[i]]
+                    if widths[i] % 128 == 0:
+                        bvec[:, lo : lo + blocks[i]] = value
+                    else:
+                        bvec[:, lo : lo + blocks[i]] += value
+            mod[...] = jnp.sum(acc[...], axis=0) + bvec[:, bases[4] :]
+            shift1, scale1, gate1, shift2, scale2, gate2 = [mod[:, i * D : (i + 1) * D] for i in range(6)]
+            vec_ref[...] = jnp.zeros_like(vec_ref)
+            for i, v in enumerate((shift2, scale2, gate2, gate1, bvec[:, bases[3] : bases[3] + D], scale1)):
+                vec_ref[i : i + 1, :] = v
+            bfc1_ref[...] = bvec[:, bases[2] : bases[2] + FF]
+
+            def modulate(i, _):
+                rows = pl.ds(pl.multiple_of(i * RB, RB), RB)
+                h_ref[rows, :] = (normed[rows, :] * (1.0 + scale1) + shift1).astype(bf16)
+                return 0
+
+            lax.fori_loop(0, T // RB, modulate, 0)
+
 
         def kv_copy(m, k):
             return remote(
@@ -398,17 +390,22 @@
                     f(i - shift)
 
             when(0, NT - AHEAD, lambda j: tq.start_z(j + AHEAD), 0)
-            when(NT - AHEAD, 2 * NT - AHEAD, lambda j: tf.start_z(j), NT - AHEAD)
-            when(2, NT, tq.start_y, 0)
-            when(NT, 2 * NT, tf.start_y, NT)
-            when(2, NT + 1, tq.start_x, 1)
-            when(NT + 1, 2 * NT + 1, tf.start_x, NT + 1)
-            when(2, NT + 2, tq.start_c, 2)
-            when(NT + 2, 2 * NT + 2, tf.start_c, NT + 2)
-            when(3, NT + 3, project, 3)
-            when(NT + 3, 2 * NT + 3, tf.finish, NT + 3)
-
-            @pl.when(i == NT + 3)
+            when(NT - AHEAD, NT + NL - AHEAD, tf.start_z, NT - AHEAD)
+            when(0, NT, tq.start_y, 0)
+            when(NT, NT + NL, tf.start_y, NT)
+            when(1, NT + 1, tq.relay, 1)
+            when(NT + 1, NT + NL + 1, tf.start_x, NT + 1)
+            when(NT + LAG, NT + NL + LAG, tf.start_c, NT + LAG)
+            when(NT + LAG + 1, NT + NL + LAG + 1, tf.finish, NT + LAG + 1)
+
+            @pl.when(i == 0)
+            def _():
+                lax.fori_loop(0, T // RB, norm, 0)
+
+            pl.when(i == MODULATE)(modulation)
+            when(MODULATE, MODULATE + NT, project, MODULATE)
+
+            @pl.when(i == MODULATE + NT)
             def _():
                 out4.start()
 
@@ -418,17 +415,9 @@
                     for k in range(1, s):
                         kv_copy(m, k).wait()
 
-            per = pairs // 4
-
-            @pl.when(jnp.logical_and(i >= ATTEND, i < ATTEND + 4))
-            def _():
-                def one(o, _):
-                    attend((i - ATTEND) * per + o)
-                    return 0
-
-                lax.fori_loop(0, per, one, 0)
-
-            @pl.when(i == ATTEND + 4)
+            when(ATTEND, ATTEND + pairs, attend, ATTEND)
+
+            @pl.when(i == ATTEND + pairs)
             def _():
                 lax.fori_loop(0, D // 256, branch, 0)
 
@@ -436,7 +425,7 @@
 
         owns[2].wait()
         owns[3].wait()
-        lax.fori_loop(2, 2 * NT + 3, step, 0)
+        lax.fori_loop(0, NT + NL + LAG + 1, step, 0)
         out4.wait()
         for r in m_lift + m_bias + m_part:
             r.wait_send()
@@ -457,7 +446,7 @@
             pltpu.VMEM((T, D), f32), pltpu.VMEM((A, B, 2, r1, 4 * D), bf16), pltpu.VMEM((n, 1, E), f32),
             pltpu.VMEM((n, 1, E), f32), pltpu.VMEM((n, 1, M), f32), pltpu.VMEM((1, n * sum(widths)), f32),
             pltpu.VMEM((1, E), f32), dma((3, n - 1)), dma((3, n - 1)), dma((NT, NQ)), dma((NT, NQ)),
-            dma((NT, NF)), dma((NT, NF)), dma((4, s - 1)), dma((4, s - 1)), dma((4,)),
+            dma((NL, NF)), dma((NL, NF)), dma((4, s - 1)), dma((4, s - 1)), dma((4,)),
         ],
         compiler_params=pltpu.CompilerParams(
             collective_id=0, has_side_effects=True, vmem_limit_bytes=64 * 1024 * 1024 - 65536

time: 439 us -> 407 us (0.927)
  Pallas kernels: 411 us -> 380 us
    pallas_call x1, Pallas kernels: 195 us -> 163 us  [forward_attention(): pl.pallas_call(kern, out_shape=[sds((T, 3 * D), bf16), sds((s - 1, T, 2 *...]
where the time goes in v6:
time: 407 us; the launch traced here: 406 us
  Pallas kernels  380 us (93%)
  local copies, waits for them, and re-layouts  17.6 us (4%)
  other arithmetic  7.79 us (2%)
    pallas_call x1, Pallas kernels, forward_attention(): pl.pallas_call(kern, out_shape=[sds((T, 3 * D), bf16), sds((s - 1, T, 2 *...  163 us
    pallas_call x1, Pallas kernels, attention_and_sums(): pl.pallas_call(kern, out_shape=[sds((T, D), f32), sds((r1, 3 * D), f32),...  136 us
    pallas_call x1, Pallas kernels, feed_forward(): pl.pallas_call(kern, out_shape=[sds((T, D), bf16), sds((T, D), f32), sds(...  80.7 us
    unnamed x22, local copies, waits for them, and re-layouts  11.2 us

profile of v6, /device:TPU:0, one launch (start us, length us, event | category | flops | bytes accessed | tf_op | source)
XLA Modules:
  0.0 406.2 jit_solution(14840359158150250754)
XLA Ops:
  0.7 0.7 bitcast_convert_fusion.1
  1.4 1.2 constant_dynamic-update-slice_fusion.4
  3.1 0.7 broadcast_in_dim.50
  4.3 0.7 bitcast_convert_fusion
  5.6 0.7 broadcast_in_dim.52
  6.8 1.3 convert_reduce_fusion
  8.1 0.7 reshape.69.l_ref
  8.8 163.5 %forward_attention.1 = (bf16[512,3072]{1,0:T(8,128)(2,1)}, bf16[1,512,2048]{2,1,0:T(8,128)(2,1)}, bf16[512,1024]{1,0:T(8,128)(2,1)}, bf16[512,1024]{1,0:T(8,128)...) custom-call(f32[16,1,64]{2,1,0:T(1,128)} %reshape.69.l_ref, ...), custom_call_target="tpu_custom_call" | custom-call | tf_op jit(solution)/shard_map/forward_attention/pallas_call | solution.py:435
  172.3 80.7 %feed_forward.1 = (bf16[512,1024]{1,0:T(8,128)(2,1)}, f32[512,1024]{1,0:T(8,128)}, bf16[512,1024]{1,0:T(8,128)(2,1)}, f32[8,1024]{1,0:T(8,128)}, f32[8,1,512]{2,...) custom-call(f32[512,1024]{1,0:T(8,128)} %get-tuple-element.43.mid_ref, ...), custom_call_target="tpu_custom_call" | custom-call | tf_op jit(solution)/shard_map/feed_forward/pallas_call | solution.py:673
  253.0 135.9 %attention_and_sums.1 = (f32[512,1024]{1,0:T(8,128)}, f32[64,3072]{1,0:T(8,128)}, f32[64,1024]{1,0:T(8,128)}, f32[64,4096]{1,0:T(8,128)}, f32[256,1024]{1,0:T(8,...) custom-call(bf16[512,3072]{1,0:T(8,128)(2,1)} %get-tuple-element.52.refs_0_, ...), custom_call_target="tpu_custom_call" | custom-call | tf_op jit(solution)/shard_map/attention_and_sums/pallas_call | solution.py:1071
  389.0 1.3 fusion.4
  390.3 0.6 fusion.2
  391.4 1.4 reduce.9
  392.8 1.3 fusion.1
  394.2 1.2 dynamic-slice_reduce_fusion
  395.4 1.2 slice.14
  396.6 2.3 copy.39
  398.9 1.3 copy.40
  400.2 0.8 copy-done.1
  401.0 1.1 copy.41
  402.7 0.9 copy.42
  403.6 0.7 copy.43
  404.3 1.0 copy.44
  405.3 1.0 copy.45
  (21 shorter events, 3.4 us)
Async XLA Ops:
  389.0 9.9 %copy-start = (f32[512,1024]{1,0:T(8,128)S(1)}, f32[512,1024]{1,0:T(8,128)}, u32[]{:S(2)}) copy-start(f32[512,1024]{1,0:T(8,128)} %get-tuple-element.64) | copy-start | bytes 6291460
  398.9 2.2 copy-start.1
  401.0 1.7 copy-start.4
  401.0 2.5 copy-start.5
  401.0 3.2 copy-start.3
  402.7 2.6 copy-start.2

commit v7 on v6

--- a/solution.py
+++ b/solution.py
@@ -460,22 +460,25 @@
     )
 
 
-def feed_forward(middle, branch, attn, g, vectors, b_fc1, w4, w1, w2, n):
+def feed_forward(middle, branch, attn, g, vectors, b_fc1, w4, w1, w2, n, s):
     T, D = middle.shape
     FF = w1.shape[1]
     A, B = grid_of(n)
     J, r1, r2 = A * B, D // n, FF // n
     W = 2 * r2
     RB = min(T, 64)
+    H = W // 2 if s == 2 else W
 
     def kern(
         mid_ref, br_ref, attn_ref, g_ref, vec_ref, b1_ref, w4_ref, w1_ref, w2_ref,
         out_ref, dmid_ref, dattn_ref, sums_ref, bfc1_ref, gproj_ref, g1_ref, g2_ref,
-        h2, h2t, dm, dh2, mlp, dbr, w1b, w2b, gb, cr, ys, yr, zs, zr, t1, c1, s1,
+        h2, h2t, dm, dh2, mlp, dbr, w1b, w2b, gb, cr, ys, yr, zs, zr, t1, c1, s1, x1, o1, x1s, x1r,
         pw, psem, wsem, osem, cs, crs, c1s, c1r, yss, yrs, zss, zrs,
     ):
         at = Place(n)
-        greet(at.all())
+        x = lax.axis_index("seq")
+        other = {"seq": lax.rem(x + 1, s)}
+        greet(at.all() + ([other] if s == 2 else []))
         shift2, scale2, gate2, gate1, bias2 = [vec_ref[i : i + 1, :] for i in range(5)]
 
         def tile(t):
@@ -520,23 +523,50 @@
         def z_copy(k):
             return remote(zs.at[k], zr.at[k], zss.at[k], zrs.at[k], at.at_a(k + 1))
 
-        def s1_copy(t, slot):
-            lo = pl.multiple_of(tile(t) * W, W)
-            return pltpu.make_async_copy(s1.at[slot], g1_ref.at[:, :, pl.ds(lo, W)], osem.at[slot])
+        def out1_copy(t, slot):
+            lo = pl.multiple_of(tile(t) * H, H)
+            src = o1 if s == 2 else s1
+            return pltpu.make_async_copy(src.at[slot], g1_ref.at[:, :, pl.ds(lo, H)], osem.at[slot])
+
+        def half(k):
+            return pl.ds(pl.multiple_of(k * H, H), H)
+
+        def x1_copy(t, slot):
+            return remote(s1.at[slot, :, :, half(1 - x)], x1.at[t], x1s.at[t], x1r.at[t], other)
+
+        def when_not(first, f):
+            if not isinstance(first, bool):
+                pl.when(jnp.logical_not(first))(f)
+            elif not first:
+                f()
 
         def chip_sum1(t, slot, first):
             c1_copy(t, slot).wait()
-
-            @pl.when(jnp.logical_not(first))
-            def _():
-                s1_copy(t, slot).wait()
+            if s != 2:
+                when_not(first, lambda: out1_copy(t, slot).wait())
 
             def part(i, _):
                 s1[slot, i] = add32(t1[slot, i, at.c], c1[t, i]).astype(bf16)
                 return 0
 
             lax.fori_loop(0, J, part, 0)
-            s1_copy(t, slot).start()
+            if s == 2:
+                x1_copy(t, slot).start()
+            else:
+                out1_copy(t, slot).start()
+
+        def seq_sum1(t, slot, first):
+            if s != 2:
+                return
+            x1_copy(t, slot).wait()
+            when_not(first, lambda: out1_copy(t, slot).wait())
+
+            def part(i, _):
+                o1[slot, i] = add32(s1[slot, i, :, half(x)], x1[t, i]).astype(bf16)
+                return 0
+
+            lax.fori_loop(0, J, part, 0)
+            out1_copy(t, slot).start()
 
         R2 = min(r2, 64)
 
@@ -597,12 +627,21 @@
                 dh2[...] += nt(dpre, w1b[slot])
                 if m > 0:
                     chip_sum1(t - 1, 1 - slot, jnp.logical_and(k == 0, m < 3))
+                    if m > 1:
+                        seq_sum1(t - 2, slot, jnp.logical_and(k == 0, m < 4))
+                    else:
+
+                        @pl.when(k > 0)
+                        def _():
+                            seq_sum1(t - 2, slot, k * B < 3)
+
                     send_y(k, m - 1)
                 else:
 
                     @pl.when(k > 0)
                     def _():
                         chip_sum1(t - 1, 1 - slot, k * B < 3)
+                        seq_sum1(t - 2, slot, k * B < 4)
 
                 if m == B - 1:
 
@@ -613,7 +652,8 @@
             return 0
 
         lax.fori_loop(0, A, pair, 0)
-        chip_sum1(J - 1, (B - 1) % 2, jnp.bool_(J < 3))
+        chip_sum1(J - 1, 1, J < 3)
+        seq_sum1(J - 2, 0, J < 4)
 
         def back(i, _):
             rows = pl.ds(pl.multiple_of(i * RB, RB), RB)
@@ -647,6 +687,7 @@
 
         lax.fori_loop(0, D // 256, proj, 0)
 
+        seq_sum1(J - 1, 1, J < 3)
         last = J - 1
         own_sum(last, A - 1)
         for k in range(A - 1):
@@ -664,8 +705,8 @@
             return 0
 
         lax.fori_loop(0, r2 // R2, part, 0)
-        s1_copy(J - 2, 0).wait()
-        s1_copy(J - 1, 1).wait()
+        out1_copy(J - 2, 0).wait()
+        out1_copy(J - 1, 1).wait()
 
     vm, hbm = pl.BlockSpec(memory_space=pltpu.VMEM), pl.BlockSpec(memory_space=pl.ANY)
     sds = jax.ShapeDtypeStruct
@@ -674,7 +715,7 @@
         kern,
         out_shape=[
             sds((T, D), bf16), sds((T, D), f32), sds((T, D), bf16), sds((8, D), f32), sds((J, 1, W), f32),
-            sds((D, D), bf16), sds((J, r1, FF), bf16), sds((r2, D), bf16),
+            sds((D, D), bf16), sds((J, r1, J * H), bf16), sds((r2, D), bf16),
         ],
         in_specs=[vm] * 6 + [hbm] * 3,
         out_specs=[vm] * 6 + [hbm, vm],
@@ -686,6 +727,7 @@
             pltpu.VMEM((A, B - 1, r2, D), bf16), pltpu.VMEM((A, B - 1, r2, D), bf16),
             pltpu.VMEM((A - 1, r2, D), bf16), pltpu.VMEM((A - 1, r2, D), bf16),
             pltpu.VMEM((2, J, 2, r1, W), bf16), pltpu.VMEM((J, J, r1, W), bf16), pltpu.VMEM((2, J, r1, W), bf16),
+            pltpu.VMEM((J, J, r1, H) if s == 2 else (8, 128), bf16), pltpu.VMEM((2, J, r1, H), bf16), dma((J,)), dma((J,)),
             pltpu.VMEM((D, D), bf16), dma(()), dma((2, 2)), dma((2,)), dma((J,)), dma((J,)), dma((J,)), dma((J,)),
             dma((A, B - 1)), dma((A, B - 1)), dma((A - 1,)), dma((A - 1,)),
         ],
@@ -779,12 +821,13 @@
     qkv, kvr, d_attn, lse, hidden, tokens, vectors, d_middle, w_qkv, half_fc1, grad_proj, sum_fc2, sums, bias_fc1, lf, w_ada, n, s
 ):
     T, D = tokens.shape
-    FF = half_fc1.shape[-1]
+    FH = half_fc1.shape[-1]
+    FF = 2 * FH if s == 2 else FH
     A, B = grid_of(n)
     J, r1, r2 = A * B, D // n, FF // n
-    GW = 256
+    GW, LAGZ = 256, 3
     U = D // GW
-    F = FF // U
+    F = FH // U
     E = 6 * D
     RB = min(T, 64)
     rows_a = D // n
@@ -834,10 +877,49 @@
         own_f = [
             pltpu.make_async_copy(f1_ref.at[:, at.b, :, pl.ds(u * F, F)], f1o.at[u], fsem.at[u]) for u in range(U)
         ]
+        spans = [pl.ds(2 * D, 4 * D), pl.ds(0, 2 * D)]
+
+        def mod_x(i):
+            sl = dx.at[x, :, spans[i]]
+            return [remote(sl, sl, xsend.at[i, k - 1], xrecv.at[i, k - 1], seq_dev(k)) for k in range(1, s)]
+
+        def mod_all(i):
+            dm[me, :, spans[i]] = jnp.sum(dx[:, :, spans[i]], axis=0).astype(bf16).astype(f32)
+            sl = dm.at[me, :, spans[i]]
+            out = [remote(sl, sl, asend.at[i, k], arecv.at[i, k], {"fsdp": p}) for k, p in enumerate(peers)]
+            for c in out:
+                c.start()
+            return out
+
+        def bias_span(p, i):
+            lo = starts[i] + ((p * m_bias[i]) // blocks[i]) * blocks[i]
+            return pl.ds(pl.multiple_of(lo, 128), blocks[i])
+
+        def bias_out(lo, hi):
+            out = []
+            for i in range(lo, hi):
+                at_i = pl.ds(offs[i], blocks[i])
+                bx[me, :, at_i] = bsum[:, bias_span(me, i)]
+                for k, p in enumerate(peers):
+                    dst = bx.at[me, :, at_i]
+                    out.append(remote(bsum.at[:, bias_span(p, i)], dst, bsend.at[i, k], brecv.at[i, k], {"fsdp": p}))
+            for c in out:
+                c.start()
+            return out
+
+        for i, row in enumerate((3, 0, 1, 2)):
+            dx[x, :, (i + 2) * D : (i + 3) * D] = sum_ref[row : row + 1, :]
+        early_x = mod_x(0)
+        for c in early_x:
+            c.start()
+        bsum[:, starts[1] : starts[1] + D] = sum_ref[5:6, :]
+        bsum[:, starts[2] : starts[2] + FF] = bf_ref[...]
+        bsum[:, starts[3] : starts[3] + D] = sum_ref[4:5, :]
         sp.c_copy(0).start()
         for u in range(U):
             for m in range(B - 1):
                 sf.y_copy(u, m).start()
+        early_bias = bias_out(1, 4)
         if s == 2:
             x2_copy = remote(f2_ref, x2, x2s, x2r, other)
             x2_copy.start()
@@ -861,18 +943,21 @@
         dh1[...] = jnp.zeros_like(dh1)
         for o in own_f:
             o.wait()
+        for c in early_x:
+            c.wait()
+        early_all = mod_all(0)
 
         def w_copy(u, i):
             lo = pl.multiple_of(i * D + u * GW, GW)
-            return pltpu.make_async_copy(w_ref.at[:, pl.ds(lo, GW)], wq.at[i], wsem.at[i])
+            return pltpu.make_async_copy(w_ref.at[:, pl.ds(lo, GW)], wq.at[:, pl.ds(i * GW, GW)], wsem.at[i])
 
         def kv_copy(u, k):
             return remote(kvs.at[u, k - 1], kvr.at[u, k - 1], kss.at[u, k - 1], krs.at[u, k - 1], seq_dev(s - k))
 
         def attend(u):
             slot = lax.rem(u, 2)
-            for o in range(2):
-                pair = u * 2 + o
+            for o in range(GW // 128):
+                pair = u * (GW // 128) + o
                 cols, k_cols, v_cols = [pl.ds(pl.multiple_of(lo + pair * 128, 128), 128) for lo in (0, D, 2 * D)]
                 here = slice(o * 128, o * 128 + 128)
                 qv, e = qkv_ref[:, cols] * bf16(HD**-0.5), e_ref[:, cols]
@@ -926,10 +1011,7 @@
             bsum[:, there] = jnp.sum(dg[:, 2 * GW :].astype(f32), axis=0, keepdims=True)
             for i in range(3):
                 w_copy(u, i).wait()
-            total = nt(dg[:, :GW], wq[0])
-            for i in range(1, 3):
-                total = total + nt(dg[:, i * GW : (i + 1) * GW], wq[i])
-            dh1[...] += total
+            dh1[...] += nt(dg[...], wq[...])
 
         def step(i, _):
             @pl.when(i < U)
@@ -957,12 +1039,17 @@
             def _():
                 sq.send_y(i - 2)
 
+            @pl.when(i == LAGZ - 1)
+            def _():
+                sp.send_z(0)
+
+            @pl.when(i >= LAGZ)
+            def _():
+                sq.send_z(i - LAGZ)
+
             return 0
 
         lax.fori_loop(0, U + 2, step, 0)
-        sp.send_z(0)
-        for u in range(U - 2):
-            sq.send_z(u)
 
         sums = [jnp.zeros((1, D), f32), jnp.zeros((1, D), f32)]
         scale1 = sc_ref[5:6, :]
@@ -983,55 +1070,34 @@
             )
 
         shift1_sum, scale1_sum = lax.fori_loop(0, T // RB, back, tuple(sums))
-        parts = [shift1_sum, scale1_sum, sum_ref[3:4, :], sum_ref[0:1, :], sum_ref[1:2, :], sum_ref[2:3, :]]
-        for i, v in enumerate(parts):
-            dx[x, :, i * D : (i + 1) * D] = v
-        mod_x = [remote(dx.at[x], dx.at[x], xsend.at[0, k - 1], xrecv.at[0, k - 1], seq_dev(k)) for k in range(1, s)]
-        for c in mod_x:
+        dx[x, :, :D] = shift1_sum
+        dx[x, :, D : 2 * D] = scale1_sum
+        late_x = mod_x(1)
+        for c in late_x:
             c.start()
-        bsum[:, starts[1] : starts[1] + D] = sum_ref[5:6, :]
-        bsum[:, starts[2] : starts[2] + FF] = bf_ref[...]
-        bsum[:, starts[3] : starts[3] + D] = sum_ref[4:5, :]
-
-        def block(p, i):
-            lo = starts[i] + ((p * m_bias[i]) // blocks[i]) * blocks[i]
-            return bsum.at[:, pl.ds(pl.multiple_of(lo, 128), blocks[i])]
-
-        def bias_copy(k, p, i):
-            dst = bx.at[me, :, pl.ds(offs[i], blocks[i])]
-            return remote(block(p, i), dst, bsend.at[i, k], brecv.at[i, k], {"fsdp": p})
-
-        bias_out = [bias_copy(k, p, i) for k, p in enumerate(peers) for i in range(4)]
-        for c in bias_out:
-            c.start()
-        for i in range(4):
-            lo = starts[i] + ((me * m_bias[i]) // blocks[i]) * blocks[i]
-            bx[me, :, offs[i] : offs[i] + blocks[i]] = bsum[:, pl.ds(pl.multiple_of(lo, 128), blocks[i])]
-
+        late_bias = bias_out(0, 1)
+        for c in late_x:
+            c.wait()
+        late_all = mod_all(1)
+
+        for u in range(U + 2 - LAGZ, U):
+            sq.send_z(u)
         for u in range(U):
             if s == 2:
                 sf.send_x(u)
             else:
                 o1_ref[:, u * F : (u + 1) * F] = sf.send_x(u)
-        sq.send_z(U - 2)
-        for c in mod_x:
-            c.wait()
-        dm[me] = jnp.sum(dx[...], axis=0).astype(bf16).astype(f32)
-        mod_all = [remote(dm.at[me], dm.at[me], asend.at[k], arecv.at[k], {"fsdp": p}) for k, p in enumerate(peers)]
-        for c in mod_all:
-            c.start()
-        sq.send_z(U - 1)
-        for c in bias_out:
+        for c in early_bias + late_bias:
             c.wait()
         bsx[x] = jnp.sum(bx[...], axis=0)
-        bias_x = [remote(bsx.at[x], bsx.at[x], xsend.at[1, k - 1], xrecv.at[1, k - 1], seq_dev(k)) for k in range(1, s)]
+        bias_x = [remote(bsx.at[x], bsx.at[x], xsend.at[2, k - 1], xrecv.at[2, k - 1], seq_dev(k)) for k in range(1, s)]
         for c in bias_x:
             c.start()
         if s == 2:
             sp.send_x(0)
         else:
             op_ref[...] = sp.send_x(0)
-        for c in mod_all:
+        for c in early_all + late_all:
             c.wait()
         dmod = dm[...].reshape(n, E).astype(bf16)
         lp[...] = nt(dmod, wa_ref[...]).reshape(n, 1, rows_a)
@@ -1054,7 +1120,12 @@
             x2_copy.wait()
             o2_ref[...] = add32(f2_ref[...], x2[...])
             for u in range(U):
-                o1_ref[:, u * F : (u + 1) * F] = sf.finish(u)
+                sf.x_copy(u).wait()
+                for q in range(F // r2):
+                    lo = 2 * (u * F + q * r2)
+                    for k, got in ((x, sf.xs), (1 - x, sf.xr)):
+                        cols = pl.ds(pl.multiple_of(lo + k * r2, 128), r2)
+                        o1_ref[:, cols] = got[u, :, q * r2 : (q + 1) * r2].astype(f32)
             op_ref[...] = sp.finish(0)
             for u in range(U):
                 put_q(u, sq.finish(u))
@@ -1080,7 +1151,7 @@
             pltpu.VMEM((D, T), bf16), pltpu.VMEM((2, T, GW), bf16),
             pltpu.VMEM((2, 2, T, GW), f32), pltpu.VMEM((U, s - 1, 2, T, GW), bf16),
             pltpu.VMEM((U, s - 1, 2, T, GW), bf16), pltpu.VMEM((T, 3 * GW), bf16),
-            pltpu.VMEM((U, J, 2, r1, 3 * GW), bf16), pltpu.VMEM((3, D, GW), bf16),
+            pltpu.VMEM((U, J, 2, r1, 3 * GW), bf16), pltpu.VMEM((D, 3 * GW), bf16),
             pltpu.VMEM((U, A, r1, F), bf16), pltpu.VMEM((r2, D), bf16),
             dma((3,)), dma((U,)), dma((U, s - 1)), dma((U, s - 1)), dma(()), dma(()),
         ]
@@ -1090,15 +1161,15 @@
         + [
             pltpu.VMEM((s, 1, E), f32), pltpu.VMEM((n, 1, E), f32), pltpu.VMEM((n, 1, rows_a), f32),
             pltpu.VMEM((1, NBIAS), f32), pltpu.VMEM((n, 1, M), f32), pltpu.VMEM((s, 1, M), f32),
-            dma((n - 1,)), dma((n - 1,)), dma((n - 1,)), dma((n - 1,)),
-            dma((4, n - 1)), dma((4, n - 1)), dma((2, s - 1)), dma((2, s - 1)),
+            dma((2, n - 1)), dma((2, n - 1)), dma((n - 1,)), dma((n - 1,)),
+            dma((4, n - 1)), dma((4, n - 1)), dma((3, s - 1)), dma((3, s - 1)),
         ],
         compiler_params=pltpu.CompilerParams(
             collective_id=4, has_side_effects=True, vmem_limit_bytes=64 * 1024 * 1024 - 65536
         ),
         name="attention_and_sums",
     )(
-        qkv, kvr, d_attn, lse, hidden, tokens, vectors, d_middle, w_qkv, half_fc1.reshape(A, B, r1, FF),
+        qkv, kvr, d_attn, lse, hidden, tokens, vectors, d_middle, w_qkv, half_fc1.reshape(A, B, r1, FH),
         grad_proj.reshape(1, J, 2, r1, D), sum_fc2, sums, bias_fc1, lf, w_ada,
     )
     grad_tokens, t_qkv, t_proj, t_fc1, t_fc2, t_ada, ada_sums, d_lifted, bias = res
@@ -1135,7 +1206,7 @@
         lifted_q, w_ada, [b_qv, b_proj, b_fc1, b_fc2, b_ada], tokens[0], w_qkv, w_proj, w_fc1, w_fc2, n, s
     )
     result, d_middle, d_attn, sums, bias_fc1, grad_proj, half_fc1, sum_fc2 = feed_forward(
-        middle, branch, attn, cotangent[0], vectors, fc1_b, w4, fc1_w, fc2_w, n
+        middle, branch, attn, cotangent[0], vectors, fc1_b, w4, fc1_w, fc2_w, n, s
     )
     grad_input, total_qkv, total_proj, total_fc1, total_fc2, total_ada, sums_ada, d_lifted, total_bias = (
         attention_and_sums(

time: 407 us -> 393 us (0.966)
  Pallas kernels: 380 us -> 366 us
    pallas_call x1, Pallas kernels: 136 us -> 122 us  [attention_and_sums(): pl.pallas_call(kern, out_shape=[sds((T, D), f32), sds((r1, 3 * D), f32),...]
where the time goes in v7:
time: 393 us; the launch traced here: 392 us
  Pallas kernels  366 us (93%)
  local copies, waits for them, and re-layouts  17.6 us (4%)
  other arithmetic  7.79 us (2%)
    pallas_call x1, Pallas kernels, forward_attention(): pl.pallas_call(kern, out_shape=[sds((T, 3 * D), bf16), sds((s - 1, T, 2 *...  164 us
    pallas_call x1, Pallas kernels, attention_and_sums(): pl.pallas_call(kern, out_shape=[sds((T, D), f32), sds((r1, 3 * D), f32),...  122 us
    pallas_call x1, Pallas kernels, feed_forward(): pl.pallas_call(kern, out_shape=[sds((T, D), bf16), sds((T, D), f32), sds(...  79.8 us
    unnamed x22, local copies, waits for them, and re-layouts  11.2 us

profile of v7, /device:TPU:0, one launch (start us, length us, event | category | flops | bytes accessed | tf_op | source)
XLA Modules:
  0.0 392.0 jit_solution(12583676938383501762)
XLA Ops:
  0.7 0.7 bitcast_convert_fusion.1
  1.4 1.2 constant_dynamic-update-slice_fusion.4
  3.1 0.7 broadcast_in_dim.50
  4.3 0.7 bitcast_convert_fusion
  5.6 0.7 broadcast_in_dim.52
  6.8 1.3 convert_reduce_fusion
  8.1 0.7 reshape.69.l_ref
  8.8 163.6 %forward_attention.1 = (bf16[512,3072]{1,0:T(8,128)(2,1)}, bf16[1,512,2048]{2,1,0:T(8,128)(2,1)}, bf16[512,1024]{1,0:T(8,128)(2,1)}, bf16[512,1024]{1,0:T(8,128)...) custom-call(f32[16,1,64]{2,1,0:T(1,128)} %reshape.69.l_ref, ...), custom_call_target="tpu_custom_call" | custom-call | tf_op jit(solution)/shard_map/forward_attention/pallas_call | solution.py:435
  172.4 79.8 %feed_forward.1 = (bf16[512,1024]{1,0:T(8,128)(2,1)}, f32[512,1024]{1,0:T(8,128)}, bf16[512,1024]{1,0:T(8,128)(2,1)}, f32[8,1024]{1,0:T(8,128)}, f32[8,1,512]{2,...) custom-call(f32[512,1024]{1,0:T(8,128)} %get-tuple-element.43.mid_ref, ...), custom_call_target="tpu_custom_call" | custom-call | tf_op jit(solution)/shard_map/feed_forward/pallas_call | solution.py:714
  252.2 122.5 %attention_and_sums.1 = (f32[512,1024]{1,0:T(8,128)}, f32[64,3072]{1,0:T(8,128)}, f32[64,1024]{1,0:T(8,128)}, f32[64,4096]{1,0:T(8,128)}, f32[256,1024]{1,0:T(8,...) custom-call(bf16[512,3072]{1,0:T(8,128)(2,1)} %get-tuple-element.52.refs_0_, ...), custom_call_target="tpu_custom_call" | custom-call | tf_op jit(solution)/shard_map/attention_and_sums/pallas_call | solution.py:1142
  374.7 1.3 fusion.4
  376.1 0.6 fusion.2
  377.2 1.4 reduce.9
  378.6 1.3 fusion.1
  379.9 1.3 dynamic-slice_reduce_fusion
  381.2 1.2 slice.14
  382.4 2.3 copy.39
  384.7 1.3 copy.40
  386.0 0.8 copy-done.1
  386.8 1.1 copy.41
  388.5 0.9 copy.42
  389.4 0.7 copy.43
  390.1 1.0 copy.44
  391.0 1.0 copy.45
  (21 shorter events, 3.4 us)
Async XLA Ops:
  374.7 9.9 %copy-start = (f32[512,1024]{1,0:T(8,128)S(1)}, f32[512,1024]{1,0:T(8,128)}, u32[]{:S(2)}) copy-start(f32[512,1024]{1,0:T(8,128)} %get-tuple-element.64) | copy-start | bytes 6291460
  384.7 2.2 copy-start.1
  386.8 1.7 copy-start.4
  386.8 2.5 copy-start.5
  386.8 3.2 copy-start.3
  388.5 2.6 copy-start.2

commit v8 on v7

--- a/solution.py
+++ b/solution.py
@@ -112,6 +112,9 @@
     if wide == width:
         return bias
     at = (lax.axis_index("fsdp") * width) % 128
+    if wide == 128:
+        mine = lax.broadcasted_iota(jnp.int32, (1, wide), 1) // width == at // width
+        return jnp.where(mine, jnp.concatenate([bias] * (wide // width), axis=1), 0.0)
     return lax.dynamic_update_slice(jnp.zeros((1, wide), f32), bias, (0, at))
 
 
@@ -472,7 +475,7 @@
     def kern(
         mid_ref, br_ref, attn_ref, g_ref, vec_ref, b1_ref, w4_ref, w1_ref, w2_ref,
         out_ref, dmid_ref, dattn_ref, sums_ref, bfc1_ref, gproj_ref, g1_ref, g2_ref,
-        h2, h2t, dm, dh2, mlp, dbr, w1b, w2b, gb, cr, ys, yr, zs, zr, t1, c1, s1, x1, o1, x1s, x1r,
+        h2, h2t, dm, dh2, mlp, dbr, w1b, w2b, gb, cr, ys, yr, zs, zr, t1, c1, s1, keep, x1, o1, x1s, x1r,
         pw, psem, wsem, osem, cs, crs, c1s, c1r, yss, yrs, zss, zrs,
     ):
         at = Place(n)
@@ -532,7 +535,7 @@
             return pl.ds(pl.multiple_of(k * H, H), H)
 
         def x1_copy(t, slot):
-            return remote(s1.at[slot, :, :, half(1 - x)], x1.at[t], x1s.at[t], x1r.at[t], other)
+            return remote(s1.at[slot], x1.at[t], x1s.at[t], x1r.at[t], other)
 
         def when_not(first, f):
             if not isinstance(first, bool):
@@ -546,7 +549,12 @@
                 when_not(first, lambda: out1_copy(t, slot).wait())
 
             def part(i, _):
-                s1[slot, i] = add32(t1[slot, i, at.c], c1[t, i]).astype(bf16)
+                if s == 2:
+                    keep[slot, i] = add32(t1[slot, i, at.c, :, half(x)], c1[t, i, :, half(x)])
+                    send = half(1 - x)
+                    s1[slot, i] = add32(t1[slot, i, at.c, :, send], c1[t, i, :, send]).astype(bf16)
+                else:
+                    s1[slot, i] = add32(t1[slot, i, at.c], c1[t, i]).astype(bf16)
                 return 0
 
             lax.fori_loop(0, J, part, 0)
@@ -562,7 +570,7 @@
             when_not(first, lambda: out1_copy(t, slot).wait())
 
             def part(i, _):
-                o1[slot, i] = add32(s1[slot, i, :, half(x)], x1[t, i]).astype(bf16)
+                o1[slot, i] = add32(keep[slot, i], x1[t, i]).astype(bf16)
                 return 0
 
             lax.fori_loop(0, J, part, 0)
@@ -726,7 +734,8 @@
             pltpu.VMEM((J, 2, r2, D), bf16), pltpu.VMEM((J, r2, D), bf16),
             pltpu.VMEM((A, B - 1, r2, D), bf16), pltpu.VMEM((A, B - 1, r2, D), bf16),
             pltpu.VMEM((A - 1, r2, D), bf16), pltpu.VMEM((A - 1, r2, D), bf16),
-            pltpu.VMEM((2, J, 2, r1, W), bf16), pltpu.VMEM((J, J, r1, W), bf16), pltpu.VMEM((2, J, r1, W), bf16),
+            pltpu.VMEM((2, J, 2, r1, W), bf16), pltpu.VMEM((J, J, r1, W), bf16), pltpu.VMEM((2, J, r1, H), bf16),
+            pltpu.VMEM((2, J, r1, H) if s == 2 else (8, 128), f32),
             pltpu.VMEM((J, J, r1, H) if s == 2 else (8, 128), bf16), pltpu.VMEM((2, J, r1, H), bf16), dma((J,)), dma((J,)),
             pltpu.VMEM((D, D), bf16), dma(()), dma((2, 2)), dma((2,)), dma((J,)), dma((J,)), dma((J,)), dma((J,)),
             dma((A, B - 1)), dma((A, B - 1)), dma((A - 1,)), dma((A - 1,)),
@@ -740,11 +749,11 @@
 
 class RowSum:
     @staticmethod
-    def scratch(U, r, W, A, B, cores):
+    def scratch(U, r, W, A, B, cores, last=bf16):
         dma = pltpu.SemaphoreType.DMA
         shapes = [
             pltpu.VMEM((U, B - 1, A, r, W), bf16), pltpu.VMEM((U, A - 1, r, W), bf16),
-            pltpu.VMEM((U, A - 1, r, W), bf16), pltpu.VMEM((U, r, W), bf16), pltpu.VMEM((U, r, W), bf16),
+            pltpu.VMEM((U, A - 1, r, W), bf16), pltpu.VMEM((U, r, W), last), pltpu.VMEM((U, r, W), last),
             dma((U, B - 1)), dma((U, B - 1)), dma((U, A - 1)), dma((U, A - 1)), dma((U,)), dma((U,)),
         ]
         if cores:
@@ -808,7 +817,7 @@
         total = add32(self.own(u, self.at.a), *[self.zr[u, k] for k in range(self.at.A - 1)])
         if self.s != 2:
             return total
-        self.xs[u] = total.astype(bf16)
+        self.xs[u] = total.astype(self.xs.dtype)
         self.x_copy(u).start()
         return None
 
@@ -1125,7 +1134,7 @@
                     lo = 2 * (u * F + q * r2)
                     for k, got in ((x, sf.xs), (1 - x, sf.xr)):
                         cols = pl.ds(pl.multiple_of(lo + k * r2, 128), r2)
-                        o1_ref[:, cols] = got[u, :, q * r2 : (q + 1) * r2].astype(f32)
+                        o1_ref[:, cols] = got[u, :, q * r2 : (q + 1) * r2]
             op_ref[...] = sp.finish(0)
             for u in range(U):
                 put_q(u, sq.finish(u))
@@ -1157,7 +1166,7 @@
         ]
         + RowSum.scratch(U, r1, 3 * GW, A, B, True)
         + RowSum.scratch(1, r1, D, A, B, True)
-        + RowSum.scratch(U, r1, F, A, B, False)
+        + RowSum.scratch(U, r1, F, A, B, False, f32)
         + [
             pltpu.VMEM((s, 1, E), f32), pltpu.VMEM((n, 1, E), f32), pltpu.VMEM((n, 1, rows_a), f32),
             pltpu.VMEM((1, NBIAS), f32), pltpu.VMEM((n, 1, M), f32), pltpu.VMEM((s, 1, M), f32),

time: 393 us -> 391 us (level)
  no operation moved by 1% of the time
where the time goes in v8:
time: 391 us; the launch traced here: 390 us
  Pallas kernels  366 us (94%)
  local copies, waits for them, and re-layouts  15.9 us (4%)
  other arithmetic  7.59 us (2%)
    pallas_call x1, Pallas kernels, forward_attention(): pl.pallas_call(kern, out_shape=[sds((T, 3 * D), bf16), sds((s - 1, T, 2 *...  164 us
    pallas_call x1, Pallas kernels, attention_and_sums(): pl.pallas_call(kern, out_shape=[sds((T, D), f32), sds((r1, 3 * D), f32),...  123 us
    pallas_call x1, Pallas kernels, feed_forward(): pl.pallas_call(kern, out_shape=[sds((T, D), bf16), sds((T, D), f32), sds(...  79.6 us
    unnamed x22, local copies, waits for them, and re-layouts  10.2 us

profile of v8, /device:TPU:0, one launch (start us, length us, event | category | flops | bytes accessed | tf_op | source)
XLA Modules:
  0.0 390.1 jit_solution(2538153116417056505)
XLA Ops:
  0.7 0.7 broadcast_in_dim.41
  1.3 0.7 broadcast_in_dim.42
  2.0 0.7 constant_dynamic-update-slice_fusion.4
  2.7 0.8 constant_dynamic-update-slice_fusion.3
  3.5 0.8 constant_dynamic-update-slice_fusion.1
  4.3 0.6 copy-done.6
  4.9 1.3 convert_reduce_fusion
  6.2 0.7 reshape.205.l_ref
  6.9 163.6 %forward_attention.1 = (bf16[512,3072]{1,0:T(8,128)(2,1)}, bf16[1,512,2048]{2,1,0:T(8,128)(2,1)}, bf16[512,1024]{1,0:T(8,128)(2,1)}, bf16[512,1024]{1,0:T(8,128)...) custom-call(f32[16,1,64]{2,1,0:T(1,128)} %reshape.205.l_ref, ...), custom_call_target="tpu_custom_call" | custom-call | tf_op jit(solution)/shard_map/forward_attention/pallas_call | solution.py:438
  170.5 79.6 %feed_forward.1 = (bf16[512,1024]{1,0:T(8,128)(2,1)}, f32[512,1024]{1,0:T(8,128)}, bf16[512,1024]{1,0:T(8,128)(2,1)}, f32[8,1024]{1,0:T(8,128)}, f32[8,1,512]{2,...) custom-call(f32[512,1024]{1,0:T(8,128)} %get-tuple-element.43.mid_ref, ...), custom_call_target="tpu_custom_call" | custom-call | tf_op jit(solution)/shard_map/feed_forward/pallas_call | solution.py:722
  250.1 122.6 %attention_and_sums.1 = (f32[512,1024]{1,0:T(8,128)}, f32[64,3072]{1,0:T(8,128)}, f32[64,1024]{1,0:T(8,128)}, f32[64,4096]{1,0:T(8,128)}, f32[256,1024]{1,0:T(8,...) custom-call(bf16[512,3072]{1,0:T(8,128)(2,1)} %get-tuple-element.52.refs_0_, ...), custom_call_target="tpu_custom_call" | custom-call | tf_op jit(solution)/shard_map/attention_and_sums/pallas_call | solution.py:1151
  372.8 1.4 slice.14
  374.2 1.2 fusion.4
  375.9 1.3 dynamic-slice_reduce_fusion
  377.7 1.4 reduce.9
  379.1 1.3 fusion.1
  380.5 2.3 copy.37
  382.7 1.3 copy.38
  384.0 0.8 copy-done.1
  384.9 1.1 copy.39
  386.5 0.9 copy.40
  387.4 0.7 copy.41
  388.1 1.0 copy.42
  389.1 1.0 copy.43
  (17 shorter events, 1.7 us)
Async XLA Ops:
  4.3 0.6 copy-start.6
  372.8 9.9 %copy-start = (f32[512,1024]{1,0:T(8,128)S(1)}, f32[512,1024]{1,0:T(8,128)}, u32[]{:S(2)}) copy-start(f32[512,1024]{1,0:T(8,128)} %get-tuple-element.64) | copy-start | bytes 6291460
  382.7 2.2 copy-start.1
  384.9 1.7 copy-start.4
  384.9 2.5 copy-start.5
  384.9 3.2 copy-start.3
  386.5 2.6 copy-start.2

commit v9 on v8

--- a/solution.py
+++ b/solution.py
@@ -1089,13 +1089,13 @@
             c.wait()
         late_all = mod_all(1)
 
-        for u in range(U + 2 - LAGZ, U):
-            sq.send_z(u)
         for u in range(U):
             if s == 2:
                 sf.send_x(u)
             else:
                 o1_ref[:, u * F : (u + 1) * F] = sf.send_x(u)
+        for u in range(U + 2 - LAGZ, U):
+            sq.send_z(u)
         for c in early_bias + late_bias:
             c.wait()
         bsx[x] = jnp.sum(bx[...], axis=0)

time: 391 us -> 391 us (level)
  no operation moved by 1% of the time
where the time goes in v9:
time: 391 us; the launch traced here: 390 us
  Pallas kernels  366 us (94%)
  local copies, waits for them, and re-layouts  15.9 us (4%)
  other arithmetic  7.59 us (2%)
    pallas_call x1, Pallas kernels, forward_attention(): pl.pallas_call(kern, out_shape=[sds((T, 3 * D), bf16), sds((s - 1, T, 2 *...  164 us
    pallas_call x1, Pallas kernels, attention_and_sums(): pl.pallas_call(kern, out_shape=[sds((T, D), f32), sds((r1, 3 * D), f32),...  123 us
    pallas_call x1, Pallas kernels, feed_forward(): pl.pallas_call(kern, out_shape=[sds((T, D), bf16), sds((T, D), f32), sds(...  79.6 us
    unnamed x22, local copies, waits for them, and re-layouts  10.2 us

profile of v9, /device:TPU:0, one launch (start us, length us, event | category | flops | bytes accessed | tf_op | source)
XLA Modules:
  0.0 390.1 jit_solution(8441428824216713382)
XLA Ops:
  0.7 0.7 broadcast_in_dim.41
  1.3 0.7 broadcast_in_dim.42
  2.0 0.7 constant_dynamic-update-slice_fusion.4
  2.7 0.8 constant_dynamic-update-slice_fusion.3
  3.5 0.8 constant_dynamic-update-slice_fusion.1
  4.3 0.6 copy-done.6
  4.9 1.3 convert_reduce_fusion
  6.2 0.7 reshape.205.l_ref
  6.9 163.6 %forward_attention.1 = (bf16[512,3072]{1,0:T(8,128)(2,1)}, bf16[1,512,2048]{2,1,0:T(8,128)(2,1)}, bf16[512,1024]{1,0:T(8,128)(2,1)}, bf16[512,1024]{1,0:T(8,128)...) custom-call(f32[16,1,64]{2,1,0:T(1,128)} %reshape.205.l_ref, ...), custom_call_target="tpu_custom_call" | custom-call | tf_op jit(solution)/shard_map/forward_attention/pallas_call | solution.py:438
  170.5 79.6 %feed_forward.1 = (bf16[512,1024]{1,0:T(8,128)(2,1)}, f32[512,1024]{1,0:T(8,128)}, bf16[512,1024]{1,0:T(8,128)(2,1)}, f32[8,1024]{1,0:T(8,128)}, f32[8,1,512]{2,...) custom-call(f32[512,1024]{1,0:T(8,128)} %get-tuple-element.43.mid_ref, ...), custom_call_target="tpu_custom_call" | custom-call | tf_op jit(solution)/shard_map/feed_forward/pallas_call | solution.py:722
  250.1 122.6 %attention_and_sums.1 = (f32[512,1024]{1,0:T(8,128)}, f32[64,3072]{1,0:T(8,128)}, f32[64,1024]{1,0:T(8,128)}, f32[64,4096]{1,0:T(8,128)}, f32[256,1024]{1,0:T(8,...) custom-call(bf16[512,3072]{1,0:T(8,128)(2,1)} %get-tuple-element.52.refs_0_, ...), custom_call_target="tpu_custom_call" | custom-call | tf_op jit(solution)/shard_map/attention_and_sums/pallas_call | solution.py:1151
  372.8 1.4 slice.14
  374.2 1.2 fusion.4
  375.9 1.3 dynamic-slice_reduce_fusion
  377.7 1.4 reduce.9
  379.1 1.3 fusion.1
  380.5 2.3 copy.37
  382.7 1.3 copy.38
  384.0 0.8 copy-done.1
  384.9 1.1 copy.39
  386.5 0.9 copy.40
  387.4 0.7 copy.41
  388.1 1.0 copy.42
  389.1 1.0 copy.43
  (17 shorter events, 1.7 us)
Async XLA Ops:
  4.3 0.6 copy-start.6
  372.8 9.9 %copy-start = (f32[512,1024]{1,0:T(8,128)S(1)}, f32[512,1024]{1,0:T(8,128)}, u32[]{:S(2)}) copy-start(f32[512,1024]{1,0:T(8,128)} %get-tuple-element.64) | copy-start | bytes 6291460
  382.7 2.2 copy-start.1
  384.9 1.7 copy-start.4
  384.9 2.5 copy-start.5
  384.9 3.2 copy-start.3
  386.5 2.6 copy-start.2
